TPU v7x, 32 devices: a whole 2x2x4 slice. The times are simulated.
32 devices in a mesh: grp: 1, seq: 16 (over z, y, x), head: 1, srv: 2 (over core).
Axes of the slice: x: 2, y: 2, z: 4, core: 2. Of those that a mesh axis runs over, the one named last changes fastest.
Arguments:
- tokens: bfloat16 [4096, 4096], P(('grp', 'seq', 'srv'), 'head'), may hold values from -6 to 6
- norm_gain: float32 [4096], replicated, may hold values from 0.5 to 12, as said below
- wq: bfloat16 [4096, 4096], P(('seq', 'srv'), 'head'), may hold values from -0.09375 to 0.09375
- wk: bfloat16 [4096, 1024], P(('seq', 'srv'), 'head'), may hold values from -0.09375 to 0.09375
- wv: bfloat16 [4096, 1024], P(('seq', 'srv'), 'head'), may hold values from -0.09375 to 0.09375
- wo: bfloat16 [4096, 4096], P('head', ('seq', 'srv')), may hold values from -0.09375 to 0.09375
- doc_ids: int32 [4096], P(('grp', 'seq', 'srv')), may hold values from 0 to 7, never falling along the last dimension, each value on 1 to 3072 neighbouring positions
Outputs:
- mixed: bfloat16 [4096, 4096], P(('grp', 'seq', 'srv'), 'head')
Inputs may be any that keep to these rules, and one draw needn't show every extreme that they name: `norm_gain`: the gain is positive.
All inputs are finite; a program needn't handle non-finite values.
Results may differ from a plain program's by a relative error of at most 0.015.
The roundings to bfloat16 on the way count: a program that leaves them out, or rounds other values in their place, can miss the bound.
Values may be sent and summed in bfloat16 or wider, within the bound.
No kernel may reach another device: no remote copies, remote signals or barrier semaphores. Data moves between devices by JAX's collectives and lax.ppermute only.
A program may use at most 128 MiB of HBM per device.

v0:
```python
import math

import jax
import jax.numpy as jnp
from jax import lax
from jax.sharding import PartitionSpec as P

QUERY_HEADS = 32
KV_HEAD_COUNT = 8
HEAD_WIDTH = 128


def rope(field, positions):
    half = field.shape[-1] // 2
    freqs = 500000.0 ** (-(jnp.arange(half, dtype=jnp.float32) * 2.0 / field.shape[-1]))
    angles = positions.astype(jnp.float32)[:, None] * freqs[None, :]
    cosine = jnp.cos(angles)[:, None, :]
    sine = jnp.sin(angles)[:, None, :]
    first = field[..., :half]
    second = field[..., half:]
    return jnp.concatenate(
        [first * cosine - second * sine, second * cosine + first * sine], axis=-1
    )


def local(tokens, norm_gain, wq, wk, wv, wo, doc_ids):
    tok_rows = tokens.shape[0]
    head_size = HEAD_WIDTH
    kv_local = wk.shape[1] // head_size
    query_group = QUERY_HEADS // KV_HEAD_COUNT
    source = tokens.astype(jnp.float32)
    whole = lax.all_gather(tokens, "head", axis=1, tiled=True).astype(jnp.float32)
    mean_sq = jnp.mean(whole * whole, axis=1, keepdims=True)
    normed_input = (whole * lax.rsqrt(mean_sq + 1e-05) * norm_gain[None, :]).astype(jnp.bfloat16)
    query_acc = jnp.dot(
        normed_input,
        lax.all_gather(wq, ("seq", "srv"), axis=0, tiled=True),
        preferred_element_type=jnp.float32,
    )
    key_acc = jnp.dot(
        normed_input,
        lax.all_gather(wk, ("seq", "srv"), axis=0, tiled=True),
        preferred_element_type=jnp.float32,
    )
    value_acc = jnp.dot(
        normed_input,
        lax.all_gather(wv, ("seq", "srv"), axis=0, tiled=True),
        preferred_element_type=jnp.float32,
    )
    first_pos = lax.axis_index(("seq", "srv")) * tok_rows
    positions = first_pos + jnp.arange(tok_rows, dtype=jnp.int32)
    query_matrix = rope(query_acc.reshape(tok_rows, kv_local * query_group, head_size), positions)
    query_matrix = query_matrix.astype(jnp.bfloat16).reshape(
        tok_rows, kv_local, query_group, head_size
    )
    key_matrix = rope(key_acc.reshape(tok_rows, kv_local, head_size), positions).astype(
        jnp.bfloat16
    )
    key_matrix = key_matrix.reshape(tok_rows, kv_local * head_size)
    value_matrix = value_acc.astype(jnp.bfloat16)
    scale = 1.0 / head_size**0.5

    def attend_block(carry, key_rows, value_rows, doc_rows, key_pos):
        run_top, run_total, run_acc = carry
        key_heads = key_rows.reshape(key_rows.shape[0], kv_local, head_size)
        value_heads = value_rows.reshape(value_rows.shape[0], kv_local, head_size)
        scores = (
            jnp.einsum(
                "qcgd,kcd->qcgk", query_matrix, key_heads, preferred_element_type=jnp.float32
            )
            * scale
        )
        allowed = (
            (key_pos[None, :] <= positions[:, None])
            & (key_pos[None, :] >= 0)
            & (doc_rows[None, :] == doc_ids[:, None])
        )
        allowed = allowed[:, None, None, :]
        masked = jnp.where(allowed, scores, -1e30)
        new_top = jnp.maximum(run_top, jnp.max(masked, axis=3))
        expd = jnp.where(allowed, jnp.exp(masked - new_top[..., None]), 0.0)
        factor = jnp.exp(run_top - new_top)
        new_total = run_total * factor + jnp.sum(expd, axis=3)
        weights = expd.astype(jnp.bfloat16)
        update = jnp.einsum(
            "qcgk,kcd->qcgd", weights, value_heads, preferred_element_type=jnp.float32
        )
        return (new_top, new_total, run_acc * factor[..., None] + update)

    start_state = (
        jnp.full((tok_rows, kv_local, query_group), -1e30, jnp.float32),
        jnp.zeros((tok_rows, kv_local, query_group), jnp.float32),
        jnp.zeros((tok_rows, kv_local, query_group, head_size), jnp.float32),
    )
    key_piece = lax.all_gather(key_matrix, ("seq", "srv"), axis=0, tiled=True)
    value_piece = lax.all_gather(value_matrix, ("seq", "srv"), axis=0, tiled=True)
    doc_piece = lax.all_gather(doc_ids, ("seq", "srv"), axis=0, tiled=True)
    count = key_piece.shape[0]
    width = math.gcd(count, 512)

    def step(inner, index):
        offset = index * width
        key_rows = lax.dynamic_slice_in_dim(key_piece, offset, width, 0)
        value_rows = lax.dynamic_slice_in_dim(value_piece, offset, width, 0)
        doc_rows = lax.dynamic_slice_in_dim(doc_piece, offset, width, 0)
        key_pos = offset + jnp.arange(width, dtype=jnp.int32)
        return (attend_block(inner, key_rows, value_rows, doc_rows, key_pos), None)

    def run_all(inner):
        result, unused = lax.scan(step, inner, jnp.arange(count // width, dtype=jnp.int32))
        return result

    beyond = jnp.int32(0) > first_pos + tok_rows - 1
    before = doc_piece[count - 1] < doc_ids[0]
    final_top, final_total, final_acc = lax.cond(
        beyond | before, lambda inner: inner, run_all, start_state
    )
    attended = (final_acc / final_total[..., None]).astype(jnp.bfloat16)
    attended = attended.reshape(tok_rows, kv_local * query_group * head_size)
    terms = jnp.dot(
        attended,
        lax.all_gather(wo, ("seq", "srv"), axis=1, tiled=True),
        preferred_element_type=jnp.float32,
    )
    summed = lax.psum_scatter(
        terms.astype(jnp.bfloat16), "head", scatter_dimension=1, tiled=True
    ).astype(jnp.float32)
    return (source + summed).astype(jnp.bfloat16)


def solution(mesh):
    in_specs = (
        P(("grp", "seq", "srv"), "head"),
        P(),
        P(("seq", "srv"), "head"),
        P(("seq", "srv"), "head"),
        P(("seq", "srv"), "head"),
        P("head", ("seq", "srv")),
        P(("grp", "seq", "srv")),
    )
    out_specs = P(("grp", "seq", "srv"), "head")
    return jax.shard_map(local, mesh=mesh, in_specs=in_specs, out_specs=out_specs, check_vma=False)
```

profile of v0, /device:TPU:0, one launch (start us, length us, event | category | flops | bytes accessed | tf_op | source)
XLA Modules:
  0.0 751.4 jit_solution(5832325511100395149)
XLA Ops:
  6.5 0.7 all-gather.8.cloned.1.call-update
  7.3 0.7 all-gather.14.cloned.1.call-update
  8.1 0.7 all-gather.12.cloned.1.call-update
  9.5 80.5 %all-gather.8.cloned.1.call-done = bf16[4096,1024]{1,0:T(8,128)(2,1)} async-done(((bf16[128,1024]{1,0:T(8,128)(2,1)}), bf16[4096,1024]{1,0:T(8,128)(2,1)}) %all-gather.8.cloned.1.call-update) | async-done | bytes 8388624 | tf_op jit(solution)/shard_map/all_gather | solution.py:42
  90.0 4.7 convolution_bitcast_fusion.1
  95.2 0.9 copy.20
  96.2 72.4 %all-gather.14.cloned.1.call-done = bf16[4096,1024]{1,0:T(8,128)(2,1)} async-done(((bf16[128,1024]{1,0:T(8,128)(2,1)}), bf16[4096,1024]{1,0:T(8,128)(2,1)}) %all-gather.14.cloned.1.call-update) | async-done | bytes 8388624 | tf_op jit(solution)/shard_map/all_gather | solution.py:47
  168.6 5.4 convolution_convert_fusion.1
  174.6 39.8 %all-gather = s32[32,1,128]{2,1,0:T(1,128)S(1)} all-gather(s32[1,1,128]{2,1,0:T(1,128)S(1)} %bitcast.78), channel_id=1, replica_groups=mesh['grp'=1,'seq'=16,'head'=1,'srv'=2] {'seq','srv'}, dimensions={0}, use_global_device_ids=true | all-gather | bytes 16896 | tf_op jit(solution)/shard_map/all_gather | solution.py:97
  215.5 148.8 %all-gather.12.cloned.1.call-done = bf16[4096,4096]{1,0:T(8,128)(2,1)} async-done(((bf16[128,4096]{1,0:T(8,128)(2,1)}), bf16[4096,4096]{1,0:T(8,128)(2,1)}) %all-gather.12.cloned.1.call-update) | async-done | bytes 33554448 | tf_op jit(solution)/shard_map/all_gather | solution.py:37
  364.3 13.2 %convolution_bitcast_fusion = f32[16,8,32,128]{3,1,2,0:T(8,128)S(1)} fusion(bf16[4096,4096]{1,0:T(8,128)(2,1)} %all-gather.12.cloned.1.call-done, bf16[128,4096]{1,0:T(8,128)(2,1)S(1)} %copy-done, f32[4096]{0:T(1024)S(1)} %copy-done.2, f32[128]{0:T(128)S(1)} %add_rsqrt_fusion), kind=kOutput, calls=%fused_computation.34 | convolution fusion | flops 4297064448 | bytes 36717056 | tf_op jit(solution)/shard_map/dot_general | solution.py:35
  377.9 0.8 subtract_convert_fusion
  380.1 76.9 %all-gather.10.cloned.1.call-done = bf16[4096,1024]{0,1:T(8,128)(2,1)} async-done(((bf16[128,1024]{0,1:T(8,128)(2,1)}), bf16[4096,1024]{0,1:T(8,128)(2,1)}) %all-gather.10.cloned.1.call-update) | async-done | bytes 8388624 | tf_op jit(solution)/shard_map/all_gather | solution.py:95
  457.0 78.0 %all-gather.16.cloned.1.call-done = bf16[4096,1024]{1,0:T(8,128)(2,1)} async-done(((bf16[128,1024]{1,0:T(8,128)(2,1)}), bf16[4096,1024]{1,0:T(8,128)(2,1)}) %all-gather.16.cloned.1.call-update) | async-done | bytes 8388624 | tf_op jit(solution)/shard_map/all_gather | solution.py:96
  535.0 174.9 %conditional.1 = (f32[128,8,4]{0,2,1:T(4,128)S(1)}, f32[128,8,4,128]{0,3,2,1:T(8,128)}) conditional(s32[]{:T(128)} %convert_element_type.44, (s32[]{:T(128)}, s32[128]{0:T(128)S(1)}, s32[4096]{0:T(1024)S(1)}, s32[128]{0:T(128)S(1)}, bf16[4096,1024]{0,1:T(8,128)(2,1)}, /*index=5*/bf16[128,8,4,128]{3,0,2,1:T(8,128)(2,1)S(1)}, ...), branch_computations={%region_1.6_spmd, %region_6.7_spmd} | conditional | flops 1102861952 | bytes 39335320 | solution.py:115
  535.0 174.9 %while.14 = (s32[]{:T(128)}, f32[128,8,4]{0,2,1:T(4,128)S(1)}, f32[128,8,4]{0,2,1:T(4,128)S(1)}, f32[128,8,4,128]{0,3,2,1:T(8,128)}, s32[8]{0:T(128)S(1)}, /*ind...) while((s32[]{:T(128)}, f32[128,8,4]{0,2,1:T(4,128)S(1)}, ...), condition=%wide.region_5.5_spmd.clone, body=%wide.region_2.4_spmd.clone.sunk | while | flops 1102861824 | bytes 39334116 | solution.py:110
  535.0 0.6 dynamic_slice.25
  536.6 1.3 constant_dynamic-slice_fusion.4
  537.9 4.7 fusion.40
  542.7 4.7 fusion.41
  547.4 1.3 constant_dynamic-slice_fusion.5
  549.2 7.0 bitcast_add_fusion.2
  556.2 0.6 dynamic_slice.25
  557.8 1.3 constant_dynamic-slice_fusion.4
  559.2 4.7 fusion.40
  563.9 4.5 fusion.41
  568.4 1.3 constant_dynamic-slice_fusion.5
  570.3 7.8 %bitcast_add_fusion.2 = f32[128,8,4,128]{0,3,2,1:T(8,128)} fusion(f32[128,8,4,128]{0,3,2,1:T(8,128)} %get-tuple-element.272, bf16[512,8,128,1]{0,2,3,1:T(8,128)(2,1)S(1)} %bitcast.69, f32[8,512,128,4]{2,1,3,0:T(8,128)} %get-tuple-element.251, f32[128,8,4]{0,2,1:T(4,128)S(1)} %select_maximum_fusion.2, pred[128,512]{0,1:T(8,128)(4,1)S(1)} %compare_and_fusion.2, ...), kind=kOutput, calls=%fused_computation.7.clone.1 | convolution fusion | flops 548929536 | bytes 13729793 | tf_op jit(solution)/shard_map/cond/branch_0_fun/while/body/eval_jaxpr/qcgk,kcd->qcgd/dot_general | solution.py:85
  578.1 0.6 dynamic_slice.25
  579.7 1.3 constant_dynamic-slice_fusion.4
  581.0 4.7 fusion.40
  585.7 4.6 fusion.41
  590.4 1.3 constant_dynamic-slice_fusion.5
  592.2 8.0 %bitcast_add_fusion.2 = f32[128,8,4,128]{0,3,2,1:T(8,128)} fusion(f32[128,8,4,128]{0,3,2,1:T(8,128)} %get-tuple-element.272, bf16[512,8,128,1]{0,2,3,1:T(8,128)(2,1)S(1)} %bitcast.69, f32[8,512,128,4]{2,1,3,0:T(8,128)} %get-tuple-element.251, f32[128,8,4]{0,2,1:T(4,128)S(1)} %select_maximum_fusion.2, pred[128,512]{0,1:T(8,128)(4,1)S(1)} %compare_and_fusion.2, ...), kind=kOutput, calls=%fused_computation.7.clone.1 | convolution fusion | flops 548929536 | bytes 13729793 | tf_op jit(solution)/shard_map/cond/branch_0_fun/while/body/eval_jaxpr/qcgk,kcd->qcgd/dot_general | solution.py:85
  600.3 0.6 dynamic_slice.25
  601.9 1.3 constant_dynamic-slice_fusion.4
  603.2 4.7 fusion.40
  607.9 4.7 fusion.41
  612.6 1.3 constant_dynamic-slice_fusion.5
  614.5 7.6 %bitcast_add_fusion.2 = f32[128,8,4,128]{0,3,2,1:T(8,128)} fusion(f32[128,8,4,128]{0,3,2,1:T(8,128)} %get-tuple-element.272, bf16[512,8,128,1]{0,2,3,1:T(8,128)(2,1)S(1)} %bitcast.69, f32[8,512,128,4]{2,1,3,0:T(8,128)} %get-tuple-element.251, f32[128,8,4]{0,2,1:T(4,128)S(1)} %select_maximum_fusion.2, pred[128,512]{0,1:T(8,128)(4,1)S(1)} %compare_and_fusion.2, ...), kind=kOutput, calls=%fused_computation.7.clone.1 | convolution fusion | flops 548929536 | bytes 13729793 | tf_op jit(solution)/shard_map/cond/branch_0_fun/while/body/eval_jaxpr/qcgk,kcd->qcgd/dot_general | solution.py:85
  622.1 0.6 dynamic_slice.25
  623.7 1.3 constant_dynamic-slice_fusion.4
  625.0 4.7 fusion.40
  629.7 4.9 fusion.41
  634.7 1.3 constant_dynamic-slice_fusion.5
  636.6 7.6 %bitcast_add_fusion.2 = f32[128,8,4,128]{0,3,2,1:T(8,128)} fusion(f32[128,8,4,128]{0,3,2,1:T(8,128)} %get-tuple-element.272, bf16[512,8,128,1]{0,2,3,1:T(8,128)(2,1)S(1)} %bitcast.69, f32[8,512,128,4]{2,1,3,0:T(8,128)} %get-tuple-element.251, f32[128,8,4]{0,2,1:T(4,128)S(1)} %select_maximum_fusion.2, pred[128,512]{0,1:T(8,128)(4,1)S(1)} %compare_and_fusion.2, ...), kind=kOutput, calls=%fused_computation.7.clone.1 | convolution fusion | flops 548929536 | bytes 13729793 | tf_op jit(solution)/shard_map/cond/branch_0_fun/while/body/eval_jaxpr/qcgk,kcd->qcgd/dot_general | solution.py:85
  645.8 1.3 constant_dynamic-slice_fusion.4
  647.1 4.7 fusion.40
  651.8 4.9 fusion.41
  656.8 1.3 constant_dynamic-slice_fusion.5
  658.7 7.6 %bitcast_add_fusion.2 = f32[128,8,4,128]{0,3,2,1:T(8,128)} fusion(f32[128,8,4,128]{0,3,2,1:T(8,128)} %get-tuple-element.272, bf16[512,8,128,1]{0,2,3,1:T(8,128)(2,1)S(1)} %bitcast.69, f32[8,512,128,4]{2,1,3,0:T(8,128)} %get-tuple-element.251, f32[128,8,4]{0,2,1:T(4,128)S(1)} %select_maximum_fusion.2, pred[128,512]{0,1:T(8,128)(4,1)S(1)} %compare_and_fusion.2, ...), kind=kOutput, calls=%fused_computation.7.clone.1 | convolution fusion | flops 548929536 | bytes 13729793 | tf_op jit(solution)/shard_map/cond/branch_0_fun/while/body/eval_jaxpr/qcgk,kcd->qcgd/dot_general | solution.py:85
  667.9 1.3 constant_dynamic-slice_fusion.4
  669.2 4.7 fusion.40
  674.0 4.5 fusion.41
  678.5 1.3 constant_dynamic-slice_fusion.5
  680.4 7.8 %bitcast_add_fusion.2 = f32[128,8,4,128]{0,3,2,1:T(8,128)} fusion(f32[128,8,4,128]{0,3,2,1:T(8,128)} %get-tuple-element.272, bf16[512,8,128,1]{0,2,3,1:T(8,128)(2,1)S(1)} %bitcast.69, f32[8,512,128,4]{2,1,3,0:T(8,128)} %get-tuple-element.251, f32[128,8,4]{0,2,1:T(4,128)S(1)} %select_maximum_fusion.2, pred[128,512]{0,1:T(8,128)(4,1)S(1)} %compare_and_fusion.2, ...), kind=kOutput, calls=%fused_computation.7.clone.1 | convolution fusion | flops 548929536 | bytes 13729793 | tf_op jit(solution)/shard_map/cond/branch_0_fun/while/body/eval_jaxpr/qcgk,kcd->qcgd/dot_general | solution.py:85
  689.8 1.3 constant_dynamic-slice_fusion.4
  691.1 4.7 fusion.40
  695.8 4.6 fusion.41
  700.4 1.3 constant_dynamic-slice_fusion.5
  702.3 7.6 %bitcast_add_fusion.2 = f32[128,8,4,128]{0,3,2,1:T(8,128)} fusion(f32[128,8,4,128]{0,3,2,1:T(8,128)} %get-tuple-element.272, bf16[512,8,128,1]{0,2,3,1:T(8,128)(2,1)S(1)} %bitcast.69, f32[8,512,128,4]{2,1,3,0:T(8,128)} %get-tuple-element.251, f32[128,8,4]{0,2,1:T(4,128)S(1)} %select_maximum_fusion.2, pred[128,512]{0,1:T(8,128)(4,1)S(1)} %compare_and_fusion.2, ...), kind=kOutput, calls=%fused_computation.7.clone.1 | convolution fusion | flops 548929536 | bytes 13729793 | tf_op jit(solution)/shard_map/cond/branch_0_fun/while/body/eval_jaxpr/qcgk,kcd->qcgd/dot_general | solution.py:85
  709.9 2.0 divide_convert_fusion
  711.9 18.6 %all-gather.18.cloned.1.call-done = bf16[4096,4096]{1,0:T(8,128)(2,1)} async-done(((bf16[4096,128]{1,0:T(8,128)(2,1)}), bf16[4096,4096]{1,0:T(8,128)(2,1)}) %all-gather.18.cloned.1.call-update) | async-done | bytes 33554448 | tf_op jit(solution)/shard_map/all_gather | solution.py:122
  730.5 14.1 %fusion.14 = bf16[128,4096]{1,0:T(8,128)(2,1)} fusion(bf16[128,4096]{0,1:T(8,128)(2,1)S(1)} %bitcast.71, bf16[4096,4096]{1,0:T(8,128)(2,1)} %all-gather.18.cloned.1.call-done, bf16[128,4096]{1,0:T(8,128)(2,1)S(1)} %copy-done.1), kind=kOutput, calls=%fused_computation.25 | convolution fusion | flops 4297588736 | bytes 36700160 | tf_op jit(solution)/shard_map/dot_general | solution.py:120
  (103 shorter events, 13.6 us)
Async XLA Ops:
  6.5 2.3 copy-start
  6.5 83.5 %copy-start.2 = (f32[4096]{0:T(1024)S(1)}, f32[4096]{0:T(1024)}, u32[]{:S(2)}) copy-start(f32[4096]{0:T(1024)} %param.12) | copy-start | bytes 49156
  6.5 83.5 %all-gather.8.cloned.1.call-start = ((), (), s32[]{:S(2)}) async-start(), calls=%async_computation | async-start | bytes 8650752 | tf_op jit(solution)/shard_map/all_gather | solution.py:42
  7.3 161.3 %all-gather.14.cloned.1.call-start = ((), (), s32[]{:S(2)}) async-start(), calls=%async_computation.3 | async-start | bytes 8650752 | tf_op jit(solution)/shard_map/all_gather | solution.py:47
  8.0 356.3 %all-gather.12.cloned.1.call-start = ((), (), s32[]{:S(2)}) async-start(), calls=%async_computation.2 | async-start | bytes 34603008 | tf_op jit(solution)/shard_map/all_gather | solution.py:37
  8.7 448.3 %all-gather.10.cloned.1.call-start = ((), (), s32[]{:S(2)}) async-start(), calls=%async_computation.1 | async-start | bytes 8650752 | tf_op jit(solution)/shard_map/all_gather | solution.py:95
  96.1 78.4 %copy-start.3 = (s32[128]{0:T(128)S(1)}, s32[128]{0:T(128)}, u32[]{:S(2)}) copy-start(s32[128]{0:T(128)} %param.17) | copy-start | bytes 1540
  96.2 438.8 %all-gather.16.cloned.1.call-start = ((), (), s32[]{:S(2)}) async-start(), calls=%async_computation.4 | async-start | bytes 8650752 | tf_op jit(solution)/shard_map/all_gather | solution.py:96
  174.0 556.5 %all-gather.18.cloned.1.call-start = ((), (), s32[]{:S(2)}) async-start(), calls=%async_computation.5 | async-start | bytes 34603008 | tf_op jit(solution)/shard_map/all_gather | solution.py:122
  709.9 20.6 %copy-start.1 = (bf16[128,4096]{1,0:T(8,128)(2,1)S(1)}, bf16[128,4096]{1,0:T(8,128)(2,1)}, u32[]{:S(2)}) copy-start(bf16[128,4096]{1,0:T(8,128)(2,1)} %param.11) | copy-start | bytes 3145732
Sparse Core Ops, SparseCore 0:
  10.2 79.7 all-gather.7
  92.9 75.6 all-gather.13
  171.4 192.8 all-gather.11
  367.0 89.9 all-gather.9
  459.7 75.2 all-gather.15
  536.3 194.1 all-gather.17
where the time goes:
time: 752 us; the launch traced here: 751 us
  waiting for transfers between devices  478 us (64%)
  matrix products  136 us (18%)
  other arithmetic  44.4 us (6%)
  blocking collectives  39.8 us (5%)
  local copies, waits for them, and re-layouts  33.5 us (4%)
  between operations  14.2 us (2%)
    all_gather x1, waiting for transfers between devices, local(): lax.all_gather(wq, ('seq', 'srv'), axis=0, tiled=True)  149 us
    all_gather x1, waiting for transfers between devices, local(): lax.all_gather(wk, ('seq', 'srv'), axis=0, tiled=True)  80.5 us
    all_gather x1, waiting for transfers between devices, local(): lax.all_gather(value_matrix, ('seq', 'srv'), axis=0, tiled=True)  78 us
    all_gather x1, waiting for transfers between devices, local(): key_piece = lax.all_gather(key_matrix, ('seq', 'srv'), axis=0, tiled=True)  76.9 us
    all_gather x1, waiting for transfers between devices, local(): lax.all_gather(wv, ('seq', 'srv'), axis=0, tiled=True)  72.4 us
    dot_general x8, matrix products, attend_block(): jnp.einsum('qcgk,kcd->qcgd', weights, value_heads, preferred_element_type...  61.1 us
    all_gather x1, blocking collectives, local(): doc_piece = lax.all_gather(doc_ids, ('seq', 'srv'), axis=0, tiled=True)  39.8 us
    dot_general x8, matrix products, attend_block(): jnp.einsum('qcgd,kcd->qcgk', query_matrix, key_heads, preferred_element_t...  37.7 us
  transfers between devices with their start and end apart: 6, of which 6 were waited for; matrix products, arithmetic and copies ran while one was open for 27% of the time, Pallas kernels for 0%

commit v1 on v0

--- a/solution.py
+++ b/solution.py
@@ -1,13 +1,442 @@
+import functools
 import math
 
 import jax
 import jax.numpy as jnp
+import numpy as np
 from jax import lax
+from jax.experimental import pallas as pl
+from jax.experimental.pallas import tpu as pltpu
+from jax.sharding import Mesh
 from jax.sharding import PartitionSpec as P
 
 QUERY_HEADS = 32
 KV_HEAD_COUNT = 8
 HEAD_WIDTH = 128
+DOCS = 8
+
+
+AXES = ("zh", "zl", "y", "x", "c")
+QUAD = ("zl", "x", "c")
+SWAP = [(0, 1), (1, 0)]
+EXTRA = 16
+QT = 256
+KT = 512
+NEG = -1e30
+
+ANY = pl.BlockSpec(memory_space=pl.ANY)
+VMEM = pl.BlockSpec(memory_space=pltpu.VMEM)
+SMEM = pl.BlockSpec(memory_space=pltpu.SMEM)
+
+
+def swap(value, axis):
+    return lax.ppermute(value, axis, SWAP)
+
+
+def after(value, *others):
+    return lax.optimization_barrier((value, *others))[0]
+
+
+def quad_gather(block, by_z_first):
+    by_x = swap(block, "x")
+    by_z = swap(block, "zl")
+    far = swap(by_z, "x") if by_z_first else swap(by_x, "zl")
+    got = {(0, 0): block, (0, 1): by_x, (1, 0): by_z, (1, 1): far}
+    out = {}
+    for (dzl, dx), piece in got.items():
+        out[dzl, dx, 0] = piece
+        out[dzl, dx, 1] = swap(piece, "c")
+    return out
+
+
+OFFSETS = [(dzl, dx, dc) for dzl in range(2) for dx in range(2) for dc in range(2)]
+
+
+def start_copies(copies, sems, first=0):
+    started = []
+    for i, (src, dst) in enumerate(copies):
+        copy = pltpu.make_async_copy(src, dst, sems.at[first + i])
+        copy.start()
+        started.append(copy)
+    return started
+
+
+def wait_all(copies):
+    for copy in copies:
+        copy.wait()
+
+
+def aligned(value, step):
+    return pl.multiple_of(value, step)
+
+
+def project_kernel(where, *refs):
+    tok_refs = dict(zip(OFFSETS, refs[:8]))
+    wq_own, wq_y, wq_z0, wq_z1, wq_zy0, wq_zy1, wkv_near, wkv_far, cos_ref, sin_ref = refs[8:18]
+    q_out, kv_out, xs, wq, wkv, sems = refs[18:]
+    zh, zl, y, x, c = (where[i] for i in range(5))
+
+    def rows_of(dzh, dy, zlp):
+        return aligned((4 * (zh ^ dzh) + 2 * zlp + (y ^ dy)) * 512, 512)
+
+    def token_copies(dzl):
+        copies = []
+        for dx in range(2):
+            for dc in range(2):
+                slot = 4 * (zl ^ dzl) + 2 * (x ^ dx) + (c ^ dc)
+                dst = xs.at[pl.ds(aligned(slot * 128, 128), 128), :]
+                copies.append((tok_refs[dzl, dx, dc], dst))
+        return copies
+
+    kv_copies = []
+    for slot, (dzh, dy) in enumerate(((0, 0), (0, 1), (1, 0), (1, 1))):
+        for j in range(8):
+            src = wkv_far.at[j, pl.ds(0, 128), :]
+            if slot < 3:
+                src = wkv_near.at[j, pl.ds(slot * (128 + EXTRA), 128), :]
+            row = aligned(rows_of(dzh, dy, j // 4) + (j % 4) * 128, 128)
+            kv_copies.append((src, wkv.at[pl.ds(row, 128), :]))
+    q_copies = []
+    for zlp in range(2):
+        for dzh, dy, src in (
+            (0, 0, wq_own.at[pl.ds(zlp * 512, 512), :]),
+            (0, 1, wq_y.at[pl.ds(zlp * 512, 512), :]),
+            (1, 0, (wq_z0, wq_z1)[zlp]),
+            (1, 1, (wq_zy0, wq_zy1)[zlp]),
+        ):
+            q_copies.append((src, wq.at[pl.ds(rows_of(dzh, dy, zlp), 512), :]))
+    near = start_copies(token_copies(0), sems)
+    near += start_copies(kv_copies, sems, 4)
+    then = start_copies(q_copies, sems, 36)
+    far = start_copies(token_copies(1), sems, 44)
+
+    def turn(part, rows):
+        return part * cos_ref[rows, :] + pltpu.roll(part, 64, axis=1) * sin_ref[rows, :]
+
+    def rows_at(dzl):
+        return pl.ds(aligned((zl ^ dzl) * 512, 512), 512)
+
+    def kv_part(rows):
+        acc = jnp.dot(xs[rows, :], wkv[...], preferred_element_type=jnp.float32)
+        kv_out[rows, :128] = turn(acc[:, :128], rows).astype(jnp.bfloat16)
+        kv_out[rows, 128:] = acc[:, 128:].astype(jnp.bfloat16)
+
+    def q_part(rows):
+        for n in range(2):
+            acc = jnp.dot(
+                xs[rows, :], wq[:, 256 * n : 256 * n + 256], preferred_element_type=jnp.float32
+            )
+            for k in range(2):
+                columns = slice(256 * n + 128 * k, 256 * n + 128 * k + 128)
+                part = acc[:, 128 * k : 128 * k + 128]
+                q_out[rows, columns] = turn(part, rows).astype(jnp.bfloat16)
+
+    wait_all(near)
+    kv_part(rows_at(0))
+    wait_all(then)
+    q_part(rows_at(0))
+    wait_all(far)
+    kv_part(rows_at(1))
+    q_part(rows_at(1))
+
+
+FACTOR = math.log2(math.e) / math.sqrt(HEAD_WIDTH)
+
+
+def first_position(zh, y, tile):
+    return (2 * zh + tile // 2) * 1024 + y * 512 + (tile % 2) * QT
+
+
+def copy_keys(kv_refs, y, ks, vs, sems):
+    copies = []
+    for dy, ref in enumerate(kv_refs):
+        for zlp in range(2):
+            row = aligned((2 * zlp + (y ^ dy)) * 512, 512)
+            for half, dst in ((0, ks), (1, vs)):
+                src = ref.at[pl.ds(zlp * 512, 512), pl.ds(half * 128, 128)]
+                copies.append((src, dst.at[pl.ds(row, 512), :]))
+    wait_all(start_copies(copies, sems))
+
+
+def attend_step(queries, keys, values, state, mask):
+    top, total, acc = state
+    scores = lax.dot_general(
+        queries, keys, (((1,), (1,)), ((), ())), preferred_element_type=jnp.float32
+    )
+    if mask is not None:
+        scores = jnp.where(mask[None], scores.reshape(4, QT, KT), NEG).reshape(4 * QT, KT)
+    cuts = [slice(128 * i, 128 * i + 128) for i in range(KT // 128)]
+    best = functools.reduce(jnp.maximum, [scores[:, cut] for cut in cuts])
+    old = top[...]
+    new = jnp.maximum(old, jnp.max(best, axis=1, keepdims=True))
+    top[...] = new
+    shrink = jnp.exp2((old - new) * FACTOR)
+    parts = [jnp.exp2((scores[:, cut] - new) * FACTOR) for cut in cuts]
+    total[...] = total[...] * shrink + functools.reduce(jnp.add, parts)
+    weights = jnp.concatenate([part.astype(jnp.bfloat16) for part in parts], axis=1)
+    acc[...] = acc[...] * shrink + jnp.dot(weights, values, preferred_element_type=jnp.float32)
+
+
+def stacked(q_ref):
+    return jnp.concatenate([q_ref[:, 128 * h : 128 * h + 128] for h in range(4)], axis=0)
+
+
+def near_kernel(where, tile_lo, tile_hi, q_ref, start_ref, kv_own, kv_y, *refs):
+    top, total, acc, ks, vs, sems = refs
+    zh, y = where[0], where[2]
+    tile = pl.program_id(0)
+
+    @pl.when(tile == 0)
+    def _():
+        copy_keys((kv_own, kv_y), y, ks, vs, sems)
+
+    state = (top.at[0], total.at[0], acc.at[0])
+    state[0][...] = jnp.full((4 * QT, 128), NEG, jnp.float32)
+    state[1][...] = jnp.zeros((4 * QT, 128), jnp.float32)
+    state[2][...] = jnp.zeros((4 * QT, 128), jnp.float32)
+    first = first_position(zh, y, tile)
+    base = zh * (2048 // KT)
+
+    @pl.loop(jnp.maximum(tile_lo[tile] // KT, base), (first + QT + KT - 1) // KT)
+    def _(block):
+        keys = pl.ds(aligned((block - base) * KT, KT), KT)
+        edge = (block * KT + KT - 1 > first) | (block * KT < tile_hi[tile])
+
+        @pl.when(edge)
+        def _():
+            key_pos = block * KT + lax.broadcasted_iota(jnp.int32, (QT, KT), 1)
+            query_pos = first + lax.broadcasted_iota(jnp.int32, (QT, KT), 0)
+            mask = (key_pos <= query_pos) & (key_pos >= start_ref[:, :1])
+            attend_step(stacked(q_ref), ks[keys, :], vs[keys, :], state, mask)
+
+        @pl.when(jnp.logical_not(edge))
+        def _():
+            attend_step(stacked(q_ref), ks[keys, :], vs[keys, :], state, None)
+
+
+def far_kernel(half, where, tile_lo, tile_hi, q_ref, start_ref, kv_z, kv_zy, *refs):
+    top_in, total_in, acc_in, out_ref, ks, vs, top, total, acc, sems = refs
+    zh, y = where[0], where[2]
+    tile = 2 * half + pl.program_id(0)
+
+    @pl.when((pl.program_id(0) == 0) & (zh == 1))
+    def _():
+        copy_keys((kv_z, kv_zy), y, ks, vs, sems)
+
+    top[...] = top_in[0]
+    total[...] = total_in[0]
+    acc[...] = acc_in[0]
+
+    @pl.loop(tile_lo[tile] // KT, zh * (2048 // KT))
+    def _(block):
+        keys = pl.ds(aligned(block * KT, KT), KT)
+        edge = block * KT < tile_hi[tile]
+
+        @pl.when(edge)
+        def _():
+            key_pos = block * KT + lax.broadcasted_iota(jnp.int32, (QT, KT), 1)
+            mask = key_pos >= start_ref[:, :1]
+            attend_step(stacked(q_ref), ks[keys, :], vs[keys, :], (top, total, acc), mask)
+
+        @pl.when(jnp.logical_not(edge))
+        def _():
+            attend_step(stacked(q_ref), ks[keys, :], vs[keys, :], (top, total, acc), None)
+
+    result = acc[...] / jnp.sum(total[...], axis=1, keepdims=True)
+    for h in range(4):
+        out_ref[:, 128 * h : 128 * h + 128] = result[QT * h : QT * h + QT].astype(jnp.bfloat16)
+
+
+def output_kernel(with_first, where, *refs):
+    att_refs = refs[:8]
+    wo_refs = refs[8:16]
+    rest = refs[16:]
+    out_ref, xs, wo, sems = rest[-4:]
+    zh, zl, y, x, c = (where[i] for i in range(5))
+    copies = []
+    for (dzl, dx, dc), ref in zip(OFFSETS, att_refs):
+        slot = 4 * (zl ^ dzl) + 2 * (x ^ dx) + (c ^ dc)
+        copies.append((ref, xs.at[:, pl.ds(aligned(slot * 512, 512), 512)]))
+    for i, ref in enumerate(wo_refs):
+        column = aligned((2 * (zh ^ (i // 2 % 2)) + (y ^ (i % 2))) * 128, 128)
+        copies.append((ref, wo.at[2048 * (i // 4) : 2048 * (i // 4) + 2048, pl.ds(column, 128)]))
+    started = start_copies(copies, sems)
+    base = 0
+    if with_first:
+        base = 512
+        out_ref[:512, :] = rest[0][...]
+    wait_all(started)
+    for n in range(2):
+        columns = slice(256 * n, 256 * n + 256)
+        acc = jnp.dot(xs[...], wo[:, columns], preferred_element_type=jnp.float32)
+        out_ref[base : base + 512, columns] = acc.astype(jnp.bfloat16)
+
+
+def finish_kernel(tok_ref, sent_ref, out_ref):
+    for block in range(32):
+        zhp, zlp, yp, xp, cp = ((block >> s) & 1 for s in (4, 3, 2, 1, 0))
+        source, part = 4 * zlp + 2 * xp + cp, 2 * zhp + yp
+        columns = slice(128 * block, 128 * block + 128)
+        sent = sent_ref[source, :, 128 * part : 128 * part + 128].astype(jnp.float32)
+        out_ref[:, columns] = (tok_ref[:, columns].astype(jnp.float32) + sent).astype(jnp.bfloat16)
+
+
+def call(kernel, out_shape, in_specs, scratch, cost, **more):
+    flops, moved = cost
+    more.setdefault("out_specs", jax.tree.map(lambda _: VMEM, out_shape))
+    return pl.pallas_call(
+        kernel,
+        out_shape=out_shape,
+        in_specs=in_specs,
+        scratch_shapes=scratch,
+        compiler_params=pltpu.CompilerParams(vmem_limit_bytes=48 * 1024 * 1024),
+        cost_estimate=pl.CostEstimate(flops=flops, bytes_accessed=moved, transcendentals=0),
+        **more,
+    )
+
+
+def split_body(tokens, norm_gain, wq, wk, wv, wo, doc_ids):
+    bf16, f32 = jnp.bfloat16, jnp.float32
+    zh, zl, y, x, c = place = [lax.axis_index(axis) for axis in AXES]
+    where = jnp.stack(place).astype(jnp.int32)
+
+    below = jnp.sum(
+        doc_ids[:, None] < lax.broadcasted_iota(jnp.int32, (1, 256), 1), axis=0, dtype=jnp.int32
+    ).astype(bf16)
+    wkv = jnp.concatenate([wk.reshape(128, 8, 128), wv.reshape(128, 8, 128)], axis=2)
+    wkv = jnp.concatenate([wkv, jnp.broadcast_to(below, (EXTRA, 8, 256))], axis=0)
+    wkv = jnp.transpose(wkv, (1, 0, 2))
+    wkv_z = swap(wkv, "zh")
+    wkv_y = swap(wkv, "y")
+
+    wqs = jnp.transpose(wq.reshape(128, 8, 512), (1, 0, 2))
+    wqs = lax.all_to_all(wqs, QUAD, 0, 0, tiled=True).reshape(1024, 512)
+    wq_z0 = swap(wqs[:512], "zh")
+    wq_z1 = swap(wqs[512:], "zh")
+    wq_y = swap(wqs, "y")
+    wq_zy0 = swap(wq_z0, "y")
+    wq_zy1 = swap(wq_z1, "y")
+
+    near = jnp.concatenate([wkv, wkv_y, wkv_z], axis=1)
+    near = lax.all_to_all(near, QUAD, 0, 0, tiled=True)
+    far = swap(near[:, 2 * (128 + EXTRA) :], "y")
+
+    source = tokens.astype(f32)
+    mean_sq = jnp.mean(source * source, axis=1, keepdims=True)
+    normed = (source * lax.rsqrt(mean_sq + 1e-05) * norm_gain[None, :]).astype(bf16)
+    tok = quad_gather(after(normed, wqs), True)
+
+    token = jnp.arange(1024, dtype=jnp.int32)
+    positions = (2 * zh + token // 512) * 1024 + y * 512 + token % 512
+    freqs = 500000.0 ** (-(jnp.arange(64, dtype=f32) * 2.0 / HEAD_WIDTH))
+    angles = positions.astype(f32)[:, None] * freqs[None, :]
+    cosine, sine = jnp.cos(angles), jnp.sin(angles)
+    cosine = jnp.concatenate([cosine, cosine], axis=1)
+    sine = jnp.concatenate([-sine, sine], axis=1)
+
+    counts = [near[:, 128 + i * (128 + EXTRA), :DOCS] for i in range(3)] + [far[:, 128, :DOCS]]
+    starts = jnp.sum(jnp.concatenate(counts, axis=0).astype(f32), axis=0).astype(jnp.int32)
+    query_start = jnp.max(
+        jnp.where(positions[:, None] >= starts[None, :], starts[None, :], 0), axis=1
+    )
+    tile_lo = query_start[::QT]
+    tile_hi = query_start[QT - 1 :: QT]
+    start_col = jnp.broadcast_to(query_start[:, None], (1024, 128))
+
+    queries, keys_values = call(
+        project_kernel,
+        (
+            jax.ShapeDtypeStruct((1024, 512), bf16),
+            jax.ShapeDtypeStruct((1024, 256), bf16),
+        ),
+        [SMEM] + [ANY] * 16 + [VMEM, VMEM],
+        [
+            pltpu.VMEM((1024, 4096), bf16),
+            pltpu.VMEM((4096, 512), bf16),
+            pltpu.VMEM((4096, 256), bf16),
+            pltpu.SemaphoreType.DMA((48,)),
+        ],
+        (2 * 1024 * 4096 * 768, 17 << 20),
+    )(
+        where, *[tok[at] for at in OFFSETS],
+        wqs, wq_y, wq_z0, wq_z1, wq_zy0, wq_zy1, near, far, cosine, sine,
+    )
+
+    kv_y = swap(keys_values, "y")
+    kv_z = swap(keys_values, "zh")
+    kv_zy = swap(kv_z, "y")
+
+    def tile_spec(shape, first):
+        return pl.BlockSpec(shape, lambda i: (i + first,) + (0,) * (len(shape) - 1))
+
+    def state_specs(first):
+        return [tile_spec((1, 4 * QT, 128), first)] * 3
+
+    state = call(
+        near_kernel,
+        [jax.ShapeDtypeStruct((4, 4 * QT, 128), f32)] * 3,
+        [SMEM, SMEM, SMEM, tile_spec((QT, 512), 0), tile_spec((QT, 128), 0), ANY, ANY],
+        [
+            pltpu.VMEM((2048, 128), bf16),
+            pltpu.VMEM((2048, 128), bf16),
+            pltpu.SemaphoreType.DMA((8,)),
+        ],
+        (4 * 1024 * 2048 * 512, 8 << 20),
+        grid=(4,),
+        out_specs=state_specs(0),
+    )(where, tile_lo, tile_hi, queries, start_col, keys_values, kv_y)
+
+    def far_call(half):
+        return call(
+            functools.partial(far_kernel, half),
+            jax.ShapeDtypeStruct((512, 512), bf16),
+            [SMEM, SMEM, SMEM, tile_spec((QT, 512), 2 * half), tile_spec((QT, 128), 2 * half)]
+            + [ANY, ANY] + state_specs(2 * half),
+            [
+                pltpu.VMEM((2048, 128), bf16),
+                pltpu.VMEM((2048, 128), bf16),
+                pltpu.VMEM((4 * QT, 128), f32),
+                pltpu.VMEM((4 * QT, 128), f32),
+                pltpu.VMEM((4 * QT, 128), f32),
+                pltpu.SemaphoreType.DMA((8,)),
+            ],
+            (4 * 512 * 2048 * 512, 8 << 20),
+            grid=(2,),
+            out_specs=pl.BlockSpec((QT, 512), lambda i: (i, 0)),
+        )(where, tile_lo, tile_hi, queries, start_col, kv_z, kv_zy, *state)
+
+    attended = [far_call(0), far_call(1)]
+
+    wos = []
+    for part in range(2):
+        piece = wo[2048 * part : 2048 * part + 2048]
+        by_z = swap(piece, "zh")
+        wos += [piece, swap(piece, "y"), by_z, swap(by_z, "y")]
+
+    def output(half, first):
+        att = quad_gather(attended[half], half == 1)
+        rows = 1024 if first else 512
+        return call(
+            functools.partial(output_kernel, bool(first)),
+            jax.ShapeDtypeStruct((rows, 512), bf16),
+            [SMEM] + [ANY] * 16 + [VMEM] * len(first),
+            [
+                pltpu.VMEM((512, 4096), bf16),
+                pltpu.VMEM((4096, 512), bf16),
+                pltpu.SemaphoreType.DMA((16,)),
+            ],
+            (2 * 512 * 4096 * 512, 9 << 20),
+        )(where, *[att[at] for at in OFFSETS], *wos, *first)
+
+    sent = output(1, [output(0, [])])
+    home = lax.all_to_all(sent.reshape(8, 128, 512), QUAD, 0, 0, tiled=True)
+    return call(
+        finish_kernel,
+        jax.ShapeDtypeStruct((128, 4096), bf16),
+        [VMEM, VMEM],
+        [],
+        (128 * 4096, 3 << 20),
+    )(tokens, home)
 
 
 def rope(field, positions):
@@ -107,14 +536,12 @@
         return (attend_block(inner, key_rows, value_rows, doc_rows, key_pos), None)
 
     def run_all(inner):
-        result, unused = lax.scan(step, inner, jnp.arange(count // width, dtype=jnp.int32))
+        result, _ = lax.scan(step, inner, jnp.arange(count // width, dtype=jnp.int32))
         return result
 
     beyond = jnp.int32(0) > first_pos + tok_rows - 1
     before = doc_piece[count - 1] < doc_ids[0]
-    final_top, final_total, final_acc = lax.cond(
-        beyond | before, lambda inner: inner, run_all, start_state
-    )
+    _, final_total, final_acc = lax.cond(beyond | before, lambda inner: inner, run_all, start_state)
     attended = (final_acc / final_total[..., None]).astype(jnp.bfloat16)
     attended = attended.reshape(tok_rows, kv_local * query_group * head_size)
     terms = jnp.dot(
@@ -129,6 +556,13 @@
 
 
 def solution(mesh):
+    sizes = dict(mesh.shape)
+    if sizes["grp"] == 1 and sizes["head"] == 1 and sizes["seq"] == 16 and sizes["srv"] == 2:
+        fine = Mesh(np.asarray(mesh.devices).reshape(2, 2, 2, 2, 2), AXES)
+        in_specs = (P(AXES), P(), P(AXES), P(AXES), P(AXES), P(None, AXES), P(AXES))
+        return jax.shard_map(
+            split_body, mesh=fine, in_specs=in_specs, out_specs=P(AXES), check_vma=False
+        )
     in_specs = (
         P(("grp", "seq", "srv"), "head"),
         P(),

time: 752 us -> 362 us (0.48)
  the two profiles are of different devices: /device:TPU:0 before, /device:TPU:16 now
where the time goes in v1:
time: 362 us; the launch traced here: 361 us
  waiting for transfers between devices  223 us (62%)
  Pallas kernels  56.1 us (15%)
  starting transfers between devices  47.6 us (13%)
  blocking collectives  18.3 us (5%)
  local copies, waits for them, and re-layouts  11 us (3%)
  other arithmetic  4.74 us (1%)
    ppermute x38, waiting for transfers between devices, swap(): return lax.ppermute(value, axis, SWAP)  223 us
    ppermute x38, starting transfers between devices, swap(): return lax.ppermute(value, axis, SWAP)  36.7 us
    all_to_all x1, blocking collectives, split_body(): home = lax.all_to_all(sent.reshape(8, 128, 512), QUAD, 0, 0, tiled=True)  18.3 us
    pallas_call x2, Pallas kernels, far_call(): call(functools.partial(far_kernel, half), jax.ShapeDtypeStruct((512, 512)...  17.7 us
    pallas_call x1, Pallas kernels, split_body(): call(project_kernel, (jax.ShapeDtypeStruct((1024, 512), bf16), jax.ShapeD...  13.9 us
    pallas_call x2, Pallas kernels, output(): call(functools.partial(output_kernel, bool(first)), jax.ShapeDtypeStruct(...  12.8 us
    pallas_call x1, Pallas kernels, split_body(): call(near_kernel, [jax.ShapeDtypeStruct((4, 4 * QT, 128), f32)] * 3, [SME...  10.4 us
  transfers between devices with their start and end apart: 40, of which 16 were waited for; matrix products, arithmetic and copies ran while one was open for 3% of the time, Pallas kernels for 9%

profile of v1, /device:TPU:16, one launch (start us, length us, event | category | flops | bytes accessed | tf_op | source)
XLA Modules:
  0.0 360.8 jit_solution(6547482378787055489)
XLA Ops:
  0.0 2.3 copy.38
  2.3 3.9 %all-to-all-start.1 = ((bf16[8,128,512]{2,1,0:T(8,128)(2,1)}), bf16[8,128,512]{2,1,0:T(8,128)(2,1)S(1)}, u32[]{:S(2)}, u32[]{:S(2)}) async-start(bf16[8,128,512]{2,1,0:T(8,128)(2,1)} %bitcast.23), calls=%async_computation.1 | async-start | bytes 2097152 | tf_op jit(solution)/shard_map/all_to_all | solution.py:313
  7.2 1.6 collective-permute-start
  8.8 0.3 collective-permute-start.1
  9.4 13.6 %collective-permute-done = bf16[8,144,256]{2,1,0:T(8,128)(2,1)S(1)} collective-permute-done((bf16[8,144,256]{2,1,0:T(8,128)(2,1)S(1)}, bf16[8,144,256]{2,1,0:T(8,128)(2,1)S(1)}, u32[]{:S(2)}, u32[]{:S(2)}) %collective-permute-start) | collective-permute-done | bytes 589856 | tf_op jit(solution)/shard_map/ppermute | solution.py:33
  23.0 11.8 %collective-permute-done.1 = bf16[8,144,256]{2,1,0:T(8,128)(2,1)S(1)} collective-permute-done((bf16[8,144,256]{2,1,0:T(8,128)(2,1)S(1)}, bf16[8,144,256]{2,1,0:T(8,128)(2,1)S(1)}, u32[]{:S(2)}, u32[]{:S(2)}) %collective-permute-start.1) | collective-permute-done | bytes 589856 | tf_op jit(solution)/shard_map/ppermute | solution.py:33
  34.8 1.3 pad_maximum_fusion
  36.1 7.0 %all-to-all-start = ((bf16[8,432,256]{2,1,0:T(8,128)(2,1)}), bf16[8,432,256]{2,1,0:T(8,128)(2,1)}, u32[]{:S(2)}, u32[]{:S(2)}) async-start(bf16[8,432,256]{2,1,0:T(8,128)(2,1)} %pad_maximum_fusion), calls=%async_computation | async-start | bytes 3538944 | tf_op jit(solution)/shard_map/all_to_all | solution.py:321
  43.5 2.2 collective-permute-start.6
  45.7 1.5 collective-permute-start.4
  47.2 0.7 collective-permute-start.11
  47.9 49.0 %collective-permute-done.6.refs_4_ = bf16[128,4096]{1,0:T(8,128)(2,1)} collective-permute-done((bf16[128,4096]{1,0:T(8,128)(2,1)S(1)}, bf16[128,4096]{1,0:T(8,128)(2,1)}, u32[]{:S(2)}, u32[]{:S(2)}) %collective-permute-start.6) | collective-permute-done | bytes 1048608 | tf_op jit(solution)/shard_map/ppermute | solution.py:33
  97.0 1.6 collective-permute-start.8
  98.6 2.8 collective-permute-start.12
  101.4 0.5 collective-permute-start.13
  101.9 20.9 %collective-permute-done.12.refs_11_ = bf16[512,512]{1,0:T(8,128)(2,1)S(1)} collective-permute-done((bf16[512,512]{1,0:T(8,128)(2,1)S(1)}, bf16[512,512]{1,0:T(8,128)(2,1)S(1)}, u32[]{:S(2)}, u32[]{:S(2)}) %collective-permute-start.12) | collective-permute-done | bytes 524320 | tf_op jit(solution)/shard_map/ppermute | solution.py:33
  122.7 0.5 collective-permute-start.14
  123.2 1.5 collective-permute-start.10
  124.8 0.5 collective-permute-start.5
  125.3 0.4 copy-done.18
  125.9 1.1 slice.55
  127.0 10.5 %collective-permute-done.14.refs_13_ = bf16[512,512]{1,0:T(8,128)(2,1)S(1)} collective-permute-done((bf16[512,512]{1,0:T(8,128)(2,1)S(1)}, bf16[512,512]{1,0:T(8,128)(2,1)S(1)}, u32[]{:S(2)}, u32[]{:S(2)}) %collective-permute-start.14) | collective-permute-done | bytes 524320 | tf_op jit(solution)/shard_map/ppermute | solution.py:33
  137.5 0.5 collective-permute-start.2
  138.0 1.9 fusion.3
  140.4 19.7 %collective-permute-done.10.refs_9_ = bf16[1024,512]{1,0:T(8,128)(2,1)} collective-permute-done((bf16[1024,512]{1,0:T(8,128)(2,1)}, bf16[1024,512]{1,0:T(8,128)(2,1)}, u32[]{:S(2)}, u32[]{:S(2)}) %collective-permute-start.10) | collective-permute-done | bytes 1048608 | tf_op jit(solution)/shard_map/ppermute | solution.py:33
  160.1 11.6 %collective-permute-done.2.refs_15_ = bf16[8,144,256]{2,1,0:T(8,128)(2,1)S(1)} collective-permute-done((bf16[8,144,256]{2,1,0:T(8,128)(2,1)S(1)}, bf16[8,144,256]{2,1,0:T(8,128)(2,1)S(1)}, u32[]{:S(2)}, u32[]{:S(2)}) %collective-permute-start.2) | collective-permute-done | bytes 589856 | tf_op jit(solution)/shard_map/ppermute | solution.py:33
  171.7 1.3 copy-done.6
  173.0 1.0 copy-done.8
  174.0 13.9 %shard_map.73 = (bf16[1024,512]{1,0:T(8,128)(2,1)S(1)}, bf16[1024,256]{1,0:T(8,128)(2,1)}) custom-call(s32[5]{0:T(128)S(1)} %stack.23.where, bf16[128,4096]{1,0:T(8,128)(2,1)} %copy-done.13, bf16[128,4096]{1,0:T(8,128)(2,1)} %copy-done.18, bf16[128,4096]{1,0:T(8,128)(2,1)} %collective-permute-done.4.refs_2_, ...), custom_call_target="tpu_custom_call" | custom-call | flops 6442450944 | bytes 17825792 | tf_op jit(solution)/shard_map/pallas_call | solution.py:346
  187.9 3.4 collective-permute-start.15
  191.3 0.9 fusion.17
  192.2 2.9 collective-permute-start.29
  195.1 0.5 collective-permute-start.17
  195.6 1.5 collective-permute-start.25
  197.1 37.8 %collective-permute-done.15.kv_z = bf16[1024,256]{1,0:T(8,128)(2,1)} collective-permute-done((bf16[1024,256]{1,0:T(8,128)(2,1)}, bf16[1024,256]{1,0:T(8,128)(2,1)}, u32[]{:S(2)}, u32[]{:S(2)}) %collective-permute-start.15) | collective-permute-done | bytes 524320 | tf_op jit(solution)/shard_map/ppermute | solution.py:33
  235.0 0.5 collective-permute-start.16
  235.5 0.8 fusion.16
  236.5 0.7 slice.56
  237.8 8.3 %collective-permute-done.26.refs_10_ = bf16[2048,128]{1,0:T(8,128)(2,1)S(1)} collective-permute-done((bf16[2048,128]{1,0:T(8,128)(2,1)S(1)}, bf16[2048,128]{1,0:T(8,128)(2,1)S(1)}, u32[]{:S(2)}, u32[]{:S(2)}) %collective-permute-start.26) | collective-permute-done | bytes 524320 | tf_op jit(solution)/shard_map/ppermute | solution.py:33
  246.1 0.5 collective-permute-start.28
  246.6 10.7 %collective-permute-done.29.refs_14_ = bf16[2048,128]{1,0:T(8,128)(2,1)} collective-permute-done((bf16[2048,128]{1,0:T(8,128)(2,1)}, bf16[2048,128]{1,0:T(8,128)(2,1)}, u32[]{:S(2)}, u32[]{:S(2)}) %collective-permute-start.29) | collective-permute-done | bytes 524320 | tf_op jit(solution)/shard_map/ppermute | solution.py:33
  257.3 0.5 collective-permute-start.27
  257.9 1.5 collective-permute-start.30
  259.6 10.4 %shard_map.74 = (f32[4,1024,128]{2,1,0:T(8,128)S(1)}, f32[4,1024,128]{2,1,0:T(8,128)}, f32[4,1024,128]{2,1,0:T(8,128)}) custom-call(s32[5]{0:T(128)S(1)} %stack.23.where, s32[4]{0:T(128)S(1)} %slice.44.tile_lo, s32[4]{0:T(128)S(1)} %slice.45.tile_hi, bf16[1024,512]{1,0:T(8,128)(2,1)S(1)} %get-tuple-element.12.q_ref, ...), custom_call_target="tpu_custom_call" | custom-call | flops 4294967296 | bytes 8388608 | tf_op jit(solution)/shard_map/pallas_call | solution.py:375
  270.0 10.5 %shard_map.76.refs_0_ = bf16[512,512]{1,0:T(8,128)(2,1)S(1)} custom-call(s32[5]{0:T(128)S(1)} %stack.23.where, s32[4]{0:T(128)S(1)} %slice.44.tile_lo, s32[4]{0:T(128)S(1)} %slice.45.tile_hi, bf16[1024,512]{1,0:T(8,128)(2,1)S(1)} %get-tuple-element.12.q_ref, s32[1024,128]{1,0:T(8,128)S(1)} %broadcast_in_dim.12.start_ref, ...), custom_call_target="tpu_custom_call" | custom-call | flops 2147483648 | bytes 8388608 | tf_op jit(solution)/shard_map/pallas_call | solution.py:390
  280.6 0.7 collective-permute-start.32
  281.3 7.2 %shard_map.75.refs_0_ = bf16[512,512]{1,0:T(8,128)(2,1)S(1)} custom-call(s32[5]{0:T(128)S(1)} %stack.23.where, s32[4]{0:T(128)S(1)} %slice.44.tile_lo, s32[4]{0:T(128)S(1)} %slice.45.tile_hi, bf16[1024,512]{1,0:T(8,128)(2,1)S(1)} %get-tuple-element.12.q_ref, s32[1024,128]{1,0:T(8,128)S(1)} %broadcast_in_dim.12.start_ref, ...), custom_call_target="tpu_custom_call" | custom-call | flops 2147483648 | bytes 8388608 | tf_op jit(solution)/shard_map/pallas_call | solution.py:390
  288.5 3.4 collective-permute-start.34
  292.1 1.9 collective-permute-done.32.refs_2_
  293.9 3.2 collective-permute-start.36
  297.1 0.8 collective-permute-start.19
  297.9 6.7 %collective-permute-done.34.refs_4_ = bf16[512,512]{1,0:T(8,128)(2,1)S(1)} collective-permute-done((bf16[512,512]{1,0:T(8,128)(2,1)S(1)}, bf16[512,512]{1,0:T(8,128)(2,1)S(1)}, u32[]{:S(2)}, u32[]{:S(2)}) %collective-permute-start.34) | collective-permute-done | bytes 524320 | tf_op jit(solution)/shard_map/ppermute | solution.py:33
  304.6 0.5 collective-permute-start.35
  305.2 10.7 %collective-permute-done.21.refs_4_ = bf16[512,512]{1,0:T(8,128)(2,1)S(1)} collective-permute-done((bf16[512,512]{1,0:T(8,128)(2,1)S(1)}, bf16[512,512]{1,0:T(8,128)(2,1)S(1)}, u32[]{:S(2)}, u32[]{:S(2)}) %collective-permute-start.21) | collective-permute-done | bytes 524320 | tf_op jit(solution)/shard_map/ppermute | solution.py:33
  315.9 1.2 collective-permute-start.23
  317.1 8.5 %collective-permute-done.36.refs_6_ = bf16[512,512]{1,0:T(8,128)(2,1)S(1)} collective-permute-done((bf16[512,512]{1,0:T(8,128)(2,1)S(1)}, bf16[512,512]{1,0:T(8,128)(2,1)S(1)}, u32[]{:S(2)}, u32[]{:S(2)}) %collective-permute-start.36) | collective-permute-done | bytes 524320 | tf_op jit(solution)/shard_map/ppermute | solution.py:33
  325.6 0.5 collective-permute-start.18
  326.2 0.4 collective-permute-start.20
  326.8 0.7 collective-permute-done.37.refs_7_
  327.5 5.7 %shard_map.77.refs_16_ = bf16[512,512]{1,0:T(8,128)(2,1)S(1)} custom-call(s32[5]{0:T(128)S(1)} %stack.23.where, bf16[512,512]{1,0:T(8,128)(2,1)S(1)} %shard_map.76.refs_0_, bf16[512,512]{1,0:T(8,128)(2,1)S(1)} %collective-permute-done.31.refs_1_, bf16[512,512]{1,0:T(8,128)(2,1)S(1)} %collective-permute-done.32.refs_2_, ...), custom_call_target="tpu_custom_call" | custom-call | flops 2147483648 | bytes 9437184 | tf_op jit(solution)/shard_map/pallas_call | solution.py:419
  333.3 0.8 copy-done.3
  334.1 7.1 %shard_map.78 = bf16[1024,512]{1,0:T(8,128)(2,1)} custom-call(s32[5]{0:T(128)S(1)} %stack.23.where, bf16[512,512]{1,0:T(8,128)(2,1)S(1)} %shard_map.75.refs_0_, bf16[512,512]{1,0:T(8,128)(2,1)S(1)} %collective-permute-done.18.refs_1_, bf16[512,512]{1,0:T(8,128)(2,1)S(1)} %collective-permute-done.19.refs_2_, ...), custom_call_target="tpu_custom_call" | custom-call | flops 2147483648 | bytes 9437184 | tf_op jit(solution)/shard_map/pallas_call | solution.py:419
  341.2 18.3 %all_to_all.15.sent_ref = bf16[8,128,512]{2,1,0:T(8,128)(2,1)S(1)} all-to-all(bf16[8,128,512]{2,1,0:T(8,128)(2,1)} %bitcast.24), channel_id=1, replica_groups=mesh['zh'=2,'zl'=2,'y'=2,'x'=2,'c'=2] {'zl','x','c'}, dimensions={0} | all-to-all | bytes 2097152 | tf_op jit(solution)/shard_map/all_to_all | solution.py:432
  359.5 1.3 shard_map.79
  (98 shorter events, 3.7 us)
Async XLA Ops:
  0.0 6.3 %copy-start.15 = (bf16[128,1024]{1,0:T(8,128)(2,1)S(1)}, bf16[128,1024]{1,0:T(8,128)(2,1)}, u32[]{:S(2)}) copy-start(bf16[128,1024]{1,0:T(8,128)(2,1)} %param.10) | copy-start | bytes 786436
  2.3 4.3 %copy-start.16 = (bf16[128,1024]{1,0:T(8,128)(2,1)S(1)}, bf16[128,1024]{1,0:T(8,128)(2,1)}, u32[]{:S(2)}) copy-start(bf16[128,1024]{1,0:T(8,128)(2,1)} %param.11) | copy-start | bytes 786436
  2.3 4.7 %copy-start.19 = (s32[128]{0:T(128)S(1)}, s32[128]{0:T(128)}, u32[]{:S(2)}) copy-start(s32[128]{0:T(128)} %param.13) | copy-start | bytes 1540
  2.3 33.8 %all-to-all-start.1 = ((bf16[8,128,512]{2,1,0:T(8,128)(2,1)}), bf16[8,128,512]{2,1,0:T(8,128)(2,1)S(1)}, u32[]{:S(2)}, u32[]{:S(2)}) async-start(bf16[8,128,512]{2,1,0:T(8,128)(2,1)} %bitcast.23), calls=%async_computation.1 | async-start | bytes 2097152 | tf_op jit(solution)/shard_map/all_to_all | solution.py:313
  6.3 2.9 copy-start
  7.2 15.8 %collective-permute-start = (bf16[8,144,256]{2,1,0:T(8,128)(2,1)S(1)}, bf16[8,144,256]{2,1,0:T(8,128)(2,1)S(1)}, u32[]{:S(2)}, u32[]{:S(2)}) collective-permute-start(bf16[8,144,256]{2,1,0:T(8,128)(2,1)S(1)} %maximum_bitcast_fusion), channel_id=1, source_target_pairs={{0,4},{4,0},{1,5},{5,1},{2,6},{6,2},{3,7},{7,3},{8,12},{12,8},{9,1... | collective-permute-start | bytes 1769480 | tf_op jit(solution)/shard_map/ppermute | solution.py:33
  8.8 26.0 %collective-permute-start.1 = (bf16[8,144,256]{2,1,0:T(8,128)(2,1)S(1)}, bf16[8,144,256]{2,1,0:T(8,128)(2,1)S(1)}, u32[]{:S(2)}, u32[]{:S(2)}) collective-permute-start(bf16[8,144,256]{2,1,0:T(8,128)(2,1)S(1)} %maximum_bitcast_fusion), channel_id=1, source_target_pairs={{0,16},{16,0},{1,17},{17,1},{2,18},{18,2},{3,19},{19,3},{4,20},{20... | collective-permute-start | bytes 1769480 | tf_op jit(solution)/shard_map/ppermute | solution.py:33
  36.1 7.0 %copy-start.17 = (f32[4096]{0:T(1024)S(1)}, f32[4096]{0:T(1024)}, u32[]{:S(2)}) copy-start(f32[4096]{0:T(1024)} %param.8) | copy-start | bytes 49156
  36.1 11.0 %copy-start.9 = (bf16[8,128,512]{2,1,0:T(8,128)(2,1)}, bf16[8,128,512]{2,1,0:T(8,128)(2,1)S(1)}, u32[]{:S(2)}) copy-start(bf16[8,128,512]{2,1,0:T(8,128)(2,1)S(1)} %all-to-all-done.1) | copy-start | bytes 3145732
  36.1 89.7 %all-to-all-start = ((bf16[8,432,256]{2,1,0:T(8,128)(2,1)}), bf16[8,432,256]{2,1,0:T(8,128)(2,1)}, u32[]{:S(2)}, u32[]{:S(2)}) async-start(bf16[8,432,256]{2,1,0:T(8,128)(2,1)} %pad_maximum_fusion), calls=%async_computation | async-start | bytes 3538944 | tf_op jit(solution)/shard_map/all_to_all | solution.py:321
  43.5 81.3 %copy-start.13 = (bf16[128,4096]{1,0:T(8,128)(2,1)}, bf16[128,4096]{1,0:T(8,128)(2,1)S(1)}, u32[]{:S(2)}) copy-start(bf16[128,4096]{1,0:T(8,128)(2,1)S(1)} %fusion.2.refs_0_) | copy-start | bytes 3145732
  43.5 53.5 %collective-permute-start.6 = (bf16[128,4096]{1,0:T(8,128)(2,1)S(1)}, bf16[128,4096]{1,0:T(8,128)(2,1)}, u32[]{:S(2)}, u32[]{:S(2)}) collective-permute-start(bf16[128,4096]{1,0:T(8,128)(2,1)S(1)} %fusion.2.refs_0_), channel_id=1, source_target_pairs={{0,8},{8,0},{1,9},{9,1},{2,10},{10,2},{3,11},{11,3},{4,12},{12,4},... | collective-permute-start | bytes 3145736 | tf_op jit(solution)/shard_map/ppermute | solution.py:33
  45.7 77.6 %collective-permute-start.4 = (bf16[128,4096]{1,0:T(8,128)(2,1)S(1)}, bf16[128,4096]{1,0:T(8,128)(2,1)}, u32[]{:S(2)}, u32[]{:S(2)}) collective-permute-start(bf16[128,4096]{1,0:T(8,128)(2,1)S(1)} %fusion.2.refs_0_), channel_id=1, source_target_pairs={{0,2},{2,0},{1,3},{3,1},{4,6},{6,4},{5,7},{7,5},{8,10},{10,8},{9,1... | collective-permute-start | bytes 3145736 | tf_op jit(solution)/shard_map/ppermute | solution.py:33
  47.1 77.6 %collective-permute-start.3 = (bf16[128,4096]{1,0:T(8,128)(2,1)S(1)}, bf16[128,4096]{1,0:T(8,128)(2,1)S(1)}, u32[]{:S(2)}, u32[]{:S(2)}) collective-permute-start(bf16[128,4096]{1,0:T(8,128)(2,1)S(1)} %fusion.2.refs_0_), channel_id=1, source_target_pairs={{0,1},{1,0},{2,3},{3,2},{4,5},{5,4},{6,7},{7,6},{8,9},{9,8},{10,11... | collective-permute-start | bytes 3145736 | tf_op jit(solution)/shard_map/ppermute | solution.py:33
  47.2 54.2 %collective-permute-start.11 = (bf16[512,512]{1,0:T(8,128)(2,1)S(1)}, bf16[512,512]{1,0:T(8,128)(2,1)S(1)}, u32[]{:S(2)}, u32[]{:S(2)}) collective-permute-start(bf16[512,512]{1,0:T(8,128)(2,1)S(1)} %bitcast.31), channel_id=1, source_target_pairs={{0,16},{16,0},{1,17},{17,1},{2,18},{18,2},{3,19},{19,3},{4,20},{20... | collective-permute-start | bytes 1572872 | tf_op jit(solution)/shard_map/ppermute | solution.py:33
  97.0 28.8 %collective-permute-start.8 = (bf16[128,4096]{1,0:T(8,128)(2,1)}, bf16[128,4096]{1,0:T(8,128)(2,1)}, u32[]{:S(2)}, u32[]{:S(2)}) collective-permute-start(bf16[128,4096]{1,0:T(8,128)(2,1)} %collective-permute-done.6.refs_4_), channel_id=1, source_target_pairs={{0,2},{2,0},{1,3},{3,1},{4,6},{6,4},{5,7},{7,5},{8,10},{10,8},{9,1... | collective-permute-start | bytes 3145736 | tf_op jit(solution)/shard_map/ppermute | solution.py:33
  98.6 24.1 %collective-permute-start.12 = (bf16[512,512]{1,0:T(8,128)(2,1)S(1)}, bf16[512,512]{1,0:T(8,128)(2,1)S(1)}, u32[]{:S(2)}, u32[]{:S(2)}) collective-permute-start(bf16[512,512]{1,0:T(8,128)(2,1)S(1)} %bitcast.30), channel_id=1, source_target_pairs={{0,16},{16,0},{1,17},{17,1},{2,18},{18,2},{3,19},{19,3},{4,20},{20... | collective-permute-start | bytes 1572872 | tf_op jit(solution)/shard_map/ppermute | solution.py:33
  101.4 23.4 %collective-permute-start.13 = (bf16[512,512]{1,0:T(8,128)(2,1)S(1)}, bf16[512,512]{1,0:T(8,128)(2,1)S(1)}, u32[]{:S(2)}, u32[]{:S(2)}) collective-permute-start(bf16[512,512]{1,0:T(8,128)(2,1)S(1)} %collective-permute-done.11.refs_10_), channel_id=1, source_target_pairs={{0,4},{4,0},{1,5},{5,1},{2,6},{6,2},{3,7},{7,3},{8,12},{12,8},{9,1... | collective-permute-start | bytes 1572872 | tf_op jit(solution)/shard_map/ppermute | solution.py:33
  122.7 14.8 %collective-permute-start.14 = (bf16[512,512]{1,0:T(8,128)(2,1)S(1)}, bf16[512,512]{1,0:T(8,128)(2,1)S(1)}, u32[]{:S(2)}, u32[]{:S(2)}) collective-permute-start(bf16[512,512]{1,0:T(8,128)(2,1)S(1)} %collective-permute-done.12.refs_11_), channel_id=1, source_target_pairs={{0,4},{4,0},{1,5},{5,1},{2,6},{6,2},{3,7},{7,3},{8,12},{12,8},{9,1... | collective-permute-start | bytes 1572872 | tf_op jit(solution)/shard_map/ppermute | solution.py:33
  123.2 36.9 %collective-permute-start.10 = (bf16[1024,512]{1,0:T(8,128)(2,1)}, bf16[1024,512]{1,0:T(8,128)(2,1)}, u32[]{:S(2)}, u32[]{:S(2)}) collective-permute-start(bf16[1024,512]{1,0:T(8,128)(2,1)} %bitcast.25), channel_id=1, source_target_pairs={{0,4},{4,0},{1,5},{5,1},{2,6},{6,2},{3,7},{7,3},{8,12},{12,8},{9,1... | collective-permute-start | bytes 3145736 | tf_op jit(solution)/shard_map/ppermute | solution.py:33
  124.8 1.0 copy-start.18
  124.8 35.3 %collective-permute-start.7 = (bf16[128,4096]{1,0:T(8,128)(2,1)}, bf16[128,4096]{1,0:T(8,128)(2,1)}, u32[]{:S(2)}, u32[]{:S(2)}) collective-permute-start(bf16[128,4096]{1,0:T(8,128)(2,1)} %collective-permute-done.6.refs_4_), channel_id=1, source_target_pairs={{0,1},{1,0},{2,3},{3,2},{4,5},{5,4},{6,7},{7,6},{8,9},{9,8},{10,11... | collective-permute-start | bytes 3145736 | tf_op jit(solution)/shard_map/ppermute | solution.py:33
  124.8 15.6 %copy-start.5 = (bf16[512,512]{1,0:T(8,128)(2,1)}, bf16[512,512]{1,0:T(8,128)(2,1)S(1)}, u32[]{:S(2)}) copy-start(bf16[512,512]{1,0:T(8,128)(2,1)S(1)} %collective-permute-done.13.refs_12_) | copy-start | bytes 1572868
  124.8 35.3 %collective-permute-start.5 = (bf16[128,4096]{1,0:T(8,128)(2,1)}, bf16[128,4096]{1,0:T(8,128)(2,1)}, u32[]{:S(2)}, u32[]{:S(2)}) collective-permute-start(bf16[128,4096]{1,0:T(8,128)(2,1)} %collective-permute-done.4.refs_2_), channel_id=1, source_target_pairs={{0,1},{1,0},{2,3},{3,2},{4,5},{5,4},{6,7},{7,6},{8,9},{9,8},{10,11... | collective-permute-start | bytes 3145736 | tf_op jit(solution)/shard_map/ppermute | solution.py:33
  125.8 45.9 %collective-permute-start.9 = (bf16[128,4096]{1,0:T(8,128)(2,1)}, bf16[128,4096]{1,0:T(8,128)(2,1)}, u32[]{:S(2)}, u32[]{:S(2)}) collective-permute-start(bf16[128,4096]{1,0:T(8,128)(2,1)} %collective-permute-done.8.refs_6_), channel_id=1, source_target_pairs={{0,1},{1,0},{2,3},{3,2},{4,5},{5,4},{6,7},{7,6},{8,9},{9,8},{10,11... | collective-permute-start | bytes 3145736 | tf_op jit(solution)/shard_map/ppermute | solution.py:33
  137.5 2.9 copy-start.7
  137.5 34.2 %collective-permute-start.2 = (bf16[8,144,256]{2,1,0:T(8,128)(2,1)S(1)}, bf16[8,144,256]{2,1,0:T(8,128)(2,1)S(1)}, u32[]{:S(2)}, u32[]{:S(2)}) collective-permute-start(bf16[8,144,256]{2,1,0:T(8,128)(2,1)S(1)} %slice.55), channel_id=1, source_target_pairs={{0,4},{4,0},{1,5},{5,1},{2,6},{6,2},{3,7},{7,3},{8,12},{12,8},{9,1... | collective-permute-start | bytes 1769480 | tf_op jit(solution)/shard_map/ppermute | solution.py:33
  140.2 51.2 %copy-start.14 = (bf16[4096,128]{1,0:T(8,128)(2,1)S(1)}, bf16[4096,128]{1,0:T(8,128)(2,1)}, u32[]{:S(2)}) copy-start(bf16[4096,128]{1,0:T(8,128)(2,1)} %param.12) | copy-start | bytes 3145732
  171.7 16.2 %copy-start.4 = (bf16[8,144,256]{2,1,0:T(8,128)(2,1)}, bf16[8,144,256]{2,1,0:T(8,128)(2,1)S(1)}, u32[]{:S(2)}) copy-start(bf16[8,144,256]{2,1,0:T(8,128)(2,1)S(1)} %collective-permute-done.2.refs_15_) | copy-start | bytes 1769476
  171.7 1.3 copy-start.6
  173.0 1.0 copy-start.8
  187.9 47.1 %collective-permute-start.15 = (bf16[1024,256]{1,0:T(8,128)(2,1)}, bf16[1024,256]{1,0:T(8,128)(2,1)}, u32[]{:S(2)}, u32[]{:S(2)}) collective-permute-start(bf16[1024,256]{1,0:T(8,128)(2,1)} %get-tuple-element.13.kv_own), channel_id=1, source_target_pairs={{0,16},{16,0},{1,17},{17,1},{2,18},{18,2},{3,19},{19,3},{4,20},{20... | collective-permute-start | bytes 1572872 | tf_op jit(solution)/shard_map/ppermute | solution.py:33
  192.2 53.9 %collective-permute-start.26 = (bf16[2048,128]{1,0:T(8,128)(2,1)S(1)}, bf16[2048,128]{1,0:T(8,128)(2,1)S(1)}, u32[]{:S(2)}, u32[]{:S(2)}) collective-permute-start(bf16[2048,128]{1,0:T(8,128)(2,1)S(1)} %get-tuple-element.21.refs_8_), channel_id=1, source_target_pairs={{0,16},{16,0},{1,17},{17,1},{2,18},{18,2},{3,19},{19,3},{4,20},{20... | collective-permute-start | bytes 1572872 | tf_op jit(solution)/shard_map/ppermute | solution.py:33
  192.2 65.1 %collective-permute-start.29 = (bf16[2048,128]{1,0:T(8,128)(2,1)}, bf16[2048,128]{1,0:T(8,128)(2,1)}, u32[]{:S(2)}, u32[]{:S(2)}) collective-permute-start(bf16[2048,128]{1,0:T(8,128)(2,1)} %get-tuple-element.20.refs_12_), channel_id=1, source_target_pairs={{0,16},{16,0},{1,17},{17,1},{2,18},{18,2},{3,19},{19,3},{4,20},{20... | collective-permute-start | bytes 1572872 | tf_op jit(solution)/shard_map/ppermute | solution.py:33
  195.1 62.7 %collective-permute-start.17 = (bf16[1024,256]{1,0:T(8,128)(2,1)}, bf16[1024,256]{1,0:T(8,128)(2,1)}, u32[]{:S(2)}, u32[]{:S(2)}) collective-permute-start(bf16[1024,256]{1,0:T(8,128)(2,1)} %get-tuple-element.13.kv_own), channel_id=1, source_target_pairs={{0,4},{4,0},{1,5},{5,1},{2,6},{6,2},{3,7},{7,3},{8,12},{12,8},{9,1... | collective-permute-start | bytes 1572872 | tf_op jit(solution)/shard_map/ppermute | solution.py:33
  195.6 92.8 %collective-permute-start.25 = (bf16[2048,128]{1,0:T(8,128)(2,1)S(1)}, bf16[2048,128]{1,0:T(8,128)(2,1)}, u32[]{:S(2)}, u32[]{:S(2)}) collective-permute-start(bf16[2048,128]{1,0:T(8,128)(2,1)S(1)} %get-tuple-element.21.refs_8_), channel_id=1, source_target_pairs={{0,4},{4,0},{1,5},{5,1},{2,6},{6,2},{3,7},{7,3},{8,12},{12,8},{9,1... | collective-permute-start | bytes 1572872 | tf_op jit(solution)/shard_map/ppermute | solution.py:33
  235.0 35.1 %collective-permute-start.16 = (bf16[1024,256]{1,0:T(8,128)(2,1)}, bf16[1024,256]{1,0:T(8,128)(2,1)}, u32[]{:S(2)}, u32[]{:S(2)}) collective-permute-start(bf16[1024,256]{1,0:T(8,128)(2,1)} %collective-permute-done.15.kv_z), channel_id=1, source_target_pairs={{0,4},{4,0},{1,5},{5,1},{2,6},{6,2},{3,7},{7,3},{8,12},{12,8},{9,1... | collective-permute-start | bytes 1572872 | tf_op jit(solution)/shard_map/ppermute | solution.py:33
  246.1 23.9 %copy-start.1 = (bf16[2048,128]{1,0:T(8,128)(2,1)}, bf16[2048,128]{1,0:T(8,128)(2,1)S(1)}, u32[]{:S(2)}) copy-start(bf16[2048,128]{1,0:T(8,128)(2,1)S(1)} %collective-permute-done.26.refs_10_) | copy-start | bytes 1572868
  246.1 45.8 %collective-permute-start.28 = (bf16[2048,128]{1,0:T(8,128)(2,1)}, bf16[2048,128]{1,0:T(8,128)(2,1)S(1)}, u32[]{:S(2)}, u32[]{:S(2)}) collective-permute-start(bf16[2048,128]{1,0:T(8,128)(2,1)} %get-tuple-element.20.refs_12_), channel_id=1, source_target_pairs={{0,4},{4,0},{1,5},{5,1},{2,6},{6,2},{3,7},{7,3},{8,12},{12,8},{9,1... | collective-permute-start | bytes 1572872 | tf_op jit(solution)/shard_map/ppermute | solution.py:33
  257.3 34.5 %collective-permute-start.27 = (bf16[2048,128]{1,0:T(8,128)(2,1)S(1)}, bf16[2048,128]{1,0:T(8,128)(2,1)S(1)}, u32[]{:S(2)}, u32[]{:S(2)}) collective-permute-start(bf16[2048,128]{1,0:T(8,128)(2,1)S(1)} %collective-permute-done.26.refs_10_), channel_id=1, source_target_pairs={{0,4},{4,0},{1,5},{5,1},{2,6},{6,2},{3,7},{7,3},{8,12},{12,8},{9,1... | collective-permute-start | bytes 1572872 | tf_op jit(solution)/shard_map/ppermute | solution.py:33
  257.9 39.3 %collective-permute-start.30 = (bf16[2048,128]{1,0:T(8,128)(2,1)}, bf16[2048,128]{1,0:T(8,128)(2,1)S(1)}, u32[]{:S(2)}, u32[]{:S(2)}) collective-permute-start(bf16[2048,128]{1,0:T(8,128)(2,1)} %collective-permute-done.29.refs_14_), channel_id=1, source_target_pairs={{0,4},{4,0},{1,5},{5,1},{2,6},{6,2},{3,7},{7,3},{8,12},{12,8},{9,1... | collective-permute-start | bytes 1572872 | tf_op jit(solution)/shard_map/ppermute | solution.py:33
  280.6 13.4 %collective-permute-start.32 = (bf16[512,512]{1,0:T(8,128)(2,1)S(1)}, bf16[512,512]{1,0:T(8,128)(2,1)S(1)}, u32[]{:S(2)}, u32[]{:S(2)}) collective-permute-start(bf16[512,512]{1,0:T(8,128)(2,1)S(1)} %shard_map.76.refs_0_), channel_id=1, source_target_pairs={{0,2},{2,0},{1,3},{3,1},{4,6},{6,4},{5,7},{7,5},{8,10},{10,8},{9,1... | collective-permute-start | bytes 1572872 | tf_op jit(solution)/shard_map/ppermute | solution.py:33
  288.4 45.6 %copy-start.2 = (bf16[2048,128]{1,0:T(8,128)(2,1)S(1)}, bf16[2048,128]{1,0:T(8,128)(2,1)}, u32[]{:S(2)}) copy-start(bf16[2048,128]{1,0:T(8,128)(2,1)} %copy-done.1) | copy-start | bytes 1572868
  288.5 16.2 %collective-permute-start.34 = (bf16[512,512]{1,0:T(8,128)(2,1)S(1)}, bf16[512,512]{1,0:T(8,128)(2,1)S(1)}, u32[]{:S(2)}, u32[]{:S(2)}) collective-permute-start(bf16[512,512]{1,0:T(8,128)(2,1)S(1)} %shard_map.76.refs_0_), channel_id=1, source_target_pairs={{0,8},{8,0},{1,9},{9,1},{2,10},{10,2},{3,11},{11,3},{4,12},{12,4},... | collective-permute-start | bytes 1572872 | tf_op jit(solution)/shard_map/ppermute | solution.py:33
  291.9 35.7 %copy-start.10 = (bf16[2048,128]{1,0:T(8,128)(2,1)}, bf16[2048,128]{1,0:T(8,128)(2,1)S(1)}, u32[]{:S(2)}) copy-start(bf16[2048,128]{1,0:T(8,128)(2,1)S(1)} %collective-permute-done.28.refs_13_) | copy-start | bytes 1572868
  291.9 12.8 %collective-permute-start.31 = (bf16[512,512]{1,0:T(8,128)(2,1)S(1)}, bf16[512,512]{1,0:T(8,128)(2,1)S(1)}, u32[]{:S(2)}, u32[]{:S(2)}) collective-permute-start(bf16[512,512]{1,0:T(8,128)(2,1)S(1)} %shard_map.76.refs_0_), channel_id=1, source_target_pairs={{0,1},{1,0},{2,3},{3,2},{4,5},{5,4},{6,7},{7,6},{8,9},{9,8},{10,11... | collective-permute-start | bytes 1572872 | tf_op jit(solution)/shard_map/ppermute | solution.py:33
  291.9 35.6 %copy-start.11 = (bf16[2048,128]{1,0:T(8,128)(2,1)}, bf16[2048,128]{1,0:T(8,128)(2,1)S(1)}, u32[]{:S(2)}) copy-start(bf16[2048,128]{1,0:T(8,128)(2,1)S(1)} %collective-permute-done.27.refs_11_) | copy-start | bytes 1572868
  291.9 24.0 %collective-permute-start.21 = (bf16[512,512]{1,0:T(8,128)(2,1)S(1)}, bf16[512,512]{1,0:T(8,128)(2,1)S(1)}, u32[]{:S(2)}, u32[]{:S(2)}) collective-permute-start(bf16[512,512]{1,0:T(8,128)(2,1)S(1)} %shard_map.75.refs_0_), channel_id=1, source_target_pairs={{0,8},{8,0},{1,9},{9,1},{2,10},{10,2},{3,11},{11,3},{4,12},{12,4},... | collective-permute-start | bytes 1572872 | tf_op jit(solution)/shard_map/ppermute | solution.py:33
  293.9 31.7 %collective-permute-start.36 = (bf16[512,512]{1,0:T(8,128)(2,1)S(1)}, bf16[512,512]{1,0:T(8,128)(2,1)S(1)}, u32[]{:S(2)}, u32[]{:S(2)}) collective-permute-start(bf16[512,512]{1,0:T(8,128)(2,1)S(1)} %collective-permute-done.32.refs_2_), channel_id=1, source_target_pairs={{0,8},{8,0},{1,9},{9,1},{2,10},{10,2},{3,11},{11,3},{4,12},{12,4},... | collective-permute-start | bytes 1572872 | tf_op jit(solution)/shard_map/ppermute | solution.py:33
  297.1 30.4 %copy-start.12 = (bf16[2048,128]{1,0:T(8,128)(2,1)}, bf16[2048,128]{1,0:T(8,128)(2,1)S(1)}, u32[]{:S(2)}) copy-start(bf16[2048,128]{1,0:T(8,128)(2,1)S(1)} %collective-permute-done.30.refs_15_) | copy-start | bytes 1572868
  297.1 28.5 %collective-permute-start.19 = (bf16[512,512]{1,0:T(8,128)(2,1)S(1)}, bf16[512,512]{1,0:T(8,128)(2,1)S(1)}, u32[]{:S(2)}, u32[]{:S(2)}) collective-permute-start(bf16[512,512]{1,0:T(8,128)(2,1)S(1)} %shard_map.75.refs_0_), channel_id=1, source_target_pairs={{0,2},{2,0},{1,3},{3,1},{4,6},{6,4},{5,7},{7,5},{8,10},{10,8},{9,1... | collective-permute-start | bytes 1572872 | tf_op jit(solution)/shard_map/ppermute | solution.py:33
  304.6 21.5 %collective-permute-start.33 = (bf16[512,512]{1,0:T(8,128)(2,1)S(1)}, bf16[512,512]{1,0:T(8,128)(2,1)S(1)}, u32[]{:S(2)}, u32[]{:S(2)}) collective-permute-start(bf16[512,512]{1,0:T(8,128)(2,1)S(1)} %collective-permute-done.32.refs_2_), channel_id=1, source_target_pairs={{0,1},{1,0},{2,3},{3,2},{4,5},{5,4},{6,7},{7,6},{8,9},{9,8},{10,11... | collective-permute-start | bytes 1572872 | tf_op jit(solution)/shard_map/ppermute | solution.py:33
  304.6 21.5 %collective-permute-start.35 = (bf16[512,512]{1,0:T(8,128)(2,1)S(1)}, bf16[512,512]{1,0:T(8,128)(2,1)S(1)}, u32[]{:S(2)}, u32[]{:S(2)}) collective-permute-start(bf16[512,512]{1,0:T(8,128)(2,1)S(1)} %collective-permute-done.34.refs_4_), channel_id=1, source_target_pairs={{0,1},{1,0},{2,3},{3,2},{4,5},{5,4},{6,7},{7,6},{8,9},{9,8},{10,11... | collective-permute-start | bytes 1572872 | tf_op jit(solution)/shard_map/ppermute | solution.py:33
  315.9 10.9 %collective-permute-start.23 = (bf16[512,512]{1,0:T(8,128)(2,1)S(1)}, bf16[512,512]{1,0:T(8,128)(2,1)S(1)}, u32[]{:S(2)}, u32[]{:S(2)}) collective-permute-start(bf16[512,512]{1,0:T(8,128)(2,1)S(1)} %collective-permute-done.21.refs_4_), channel_id=1, source_target_pairs={{0,2},{2,0},{1,3},{3,1},{4,6},{6,4},{5,7},{7,5},{8,10},{10,8},{9,1... | collective-permute-start | bytes 1572872 | tf_op jit(solution)/shard_map/ppermute | solution.py:33
  325.6 1.9 collective-permute-start.37
  325.6 8.5 %collective-permute-start.18 = (bf16[512,512]{1,0:T(8,128)(2,1)S(1)}, bf16[512,512]{1,0:T(8,128)(2,1)S(1)}, u32[]{:S(2)}, u32[]{:S(2)}) collective-permute-start(bf16[512,512]{1,0:T(8,128)(2,1)S(1)} %shard_map.75.refs_0_), channel_id=1, source_target_pairs={{0,1},{1,0},{2,3},{3,2},{4,5},{5,4},{6,7},{7,6},{8,9},{9,8},{10,11... | collective-permute-start | bytes 1572872 | tf_op jit(solution)/shard_map/ppermute | solution.py:33
  326.1 8.0 %collective-permute-start.22 = (bf16[512,512]{1,0:T(8,128)(2,1)S(1)}, bf16[512,512]{1,0:T(8,128)(2,1)S(1)}, u32[]{:S(2)}, u32[]{:S(2)}) collective-permute-start(bf16[512,512]{1,0:T(8,128)(2,1)S(1)} %collective-permute-done.21.refs_4_), channel_id=1, source_target_pairs={{0,1},{1,0},{2,3},{3,2},{4,5},{5,4},{6,7},{7,6},{8,9},{9,8},{10,11... | collective-permute-start | bytes 1572872 | tf_op jit(solution)/shard_map/ppermute | solution.py:33
  326.2 7.9 %collective-permute-start.20 = (bf16[512,512]{1,0:T(8,128)(2,1)S(1)}, bf16[512,512]{1,0:T(8,128)(2,1)S(1)}, u32[]{:S(2)}, u32[]{:S(2)}) collective-permute-start(bf16[512,512]{1,0:T(8,128)(2,1)S(1)} %collective-permute-done.19.refs_2_), channel_id=1, source_target_pairs={{0,1},{1,0},{2,3},{3,2},{4,5},{5,4},{6,7},{7,6},{8,9},{9,8},{10,11... | collective-permute-start | bytes 1572872 | tf_op jit(solution)/shard_map/ppermute | solution.py:33
  326.8 7.3 %collective-permute-start.24 = (bf16[512,512]{1,0:T(8,128)(2,1)S(1)}, bf16[512,512]{1,0:T(8,128)(2,1)S(1)}, u32[]{:S(2)}, u32[]{:S(2)}) collective-permute-start(bf16[512,512]{1,0:T(8,128)(2,1)S(1)} %collective-permute-done.23.refs_6_), channel_id=1, source_target_pairs={{0,1},{1,0},{2,3},{3,2},{4,5},{5,4},{6,7},{7,6},{8,9},{9,8},{10,11... | collective-permute-start | bytes 1572872 | tf_op jit(solution)/shard_map/ppermute | solution.py:33
  333.3 0.8 copy-start.3

commit v2 on v1

--- a/solution.py
+++ b/solution.py
@@ -70,33 +70,62 @@
     return pl.multiple_of(value, step)
 
 
-def project_kernel(where, *refs):
-    tok_refs = dict(zip(OFFSETS, refs[:8]))
-    wq_own, wq_y, wq_z0, wq_z1, wq_zy0, wq_zy1, wkv_near, wkv_far, cos_ref, sin_ref = refs[8:18]
-    q_out, kv_out, xs, wq, wkv, sems = refs[18:]
-    zh, zl, y, x, c = (where[i] for i in range(5))
-
-    def rows_of(dzh, dy, zlp):
-        return aligned((4 * (zh ^ dzh) + 2 * zlp + (y ^ dy)) * 512, 512)
-
-    def token_copies(dzl):
-        copies = []
-        for dx in range(2):
-            for dc in range(2):
-                slot = 4 * (zl ^ dzl) + 2 * (x ^ dx) + (c ^ dc)
-                dst = xs.at[pl.ds(aligned(slot * 128, 128), 128), :]
-                copies.append((tok_refs[dzl, dx, dc], dst))
-        return copies
-
-    kv_copies = []
-    for slot, (dzh, dy) in enumerate(((0, 0), (0, 1), (1, 0), (1, 1))):
+TOKEN_PIECES = [
+    (dzl, dx, dc, first, rows)
+    for dzl, dx, first, rows in (
+        (0, 0, 0, 128),
+        (0, 1, 0, 128),
+        (1, 0, 0, 64),
+        (1, 0, 64, 64),
+        (1, 1, 0, 64),
+        (1, 1, 64, 64),
+    )
+    for dc in range(2)
+]
+
+
+def token_copies(dzl, where, tok_refs, xs):
+    zl, x, c = where[1], where[3], where[4]
+    copies = []
+    for (piece_dzl, dx, dc, first, rows), ref in zip(TOKEN_PIECES, tok_refs):
+        if piece_dzl == dzl:
+            slot = 4 * (zl ^ dzl) + 2 * (x ^ dx) + (c ^ dc)
+            copies.append((ref, xs.at[pl.ds(aligned(slot * 128 + first, 64), rows), :]))
+    return copies
+
+
+def weight_row(where, dzh, dy, zlp):
+    return aligned((4 * (where[0] ^ dzh) + 2 * zlp + (where[2] ^ dy)) * 512, 512)
+
+
+def turn(part, cos_ref, sin_ref, rows):
+    return part * cos_ref[rows, :] + pltpu.roll(part, 64, axis=1) * sin_ref[rows, :]
+
+
+def project_kv_kernel(where, *refs):
+    tok_refs, wkv_refs, (cos_ref, sin_ref) = refs[:12], refs[12:16], refs[16:18]
+    kv_out, xs, wkv, sems = refs[18:]
+    copies = []
+    for (dzh, dy), ref in zip(((0, 0), (0, 1), (1, 0), (1, 1)), wkv_refs):
         for j in range(8):
-            src = wkv_far.at[j, pl.ds(0, 128), :]
-            if slot < 3:
-                src = wkv_near.at[j, pl.ds(slot * (128 + EXTRA), 128), :]
-            row = aligned(rows_of(dzh, dy, j // 4) + (j % 4) * 128, 128)
-            kv_copies.append((src, wkv.at[pl.ds(row, 128), :]))
-    q_copies = []
+            row = aligned(weight_row(where, dzh, dy, j // 4) + (j % 4) * 128, 128)
+            copies.append((ref.at[j, pl.ds(0, 128), :], wkv.at[pl.ds(row, 128), :]))
+    near = start_copies(token_copies(0, where, tok_refs, xs), sems)
+    near += start_copies(copies, sems, 4)
+    far = start_copies(token_copies(1, where, tok_refs, xs), sems, 36)
+    for dzl, waits in enumerate((near, far)):
+        wait_all(waits)
+        rows = pl.ds(aligned((where[1] ^ dzl) * 512, 512), 512)
+        acc = jnp.dot(xs[rows, :], wkv[...], preferred_element_type=jnp.float32)
+        kv_out[rows, :128] = turn(acc[:, :128], cos_ref, sin_ref, rows).astype(jnp.bfloat16)
+        kv_out[rows, 128:] = acc[:, 128:].astype(jnp.bfloat16)
+
+
+def project_q_kernel(where, *refs):
+    tok_refs = refs[:12]
+    wq_own, wq_y, wq_z0, wq_z1, wq_zy0, wq_zy1, cos_ref, sin_ref = refs[12:20]
+    q_out, xs, wq, sems = refs[20:]
+    copies = []
     for zlp in range(2):
         for dzh, dy, src in (
             (0, 0, wq_own.at[pl.ds(zlp * 512, 512), :]),
@@ -104,40 +133,21 @@
             (1, 0, (wq_z0, wq_z1)[zlp]),
             (1, 1, (wq_zy0, wq_zy1)[zlp]),
         ):
-            q_copies.append((src, wq.at[pl.ds(rows_of(dzh, dy, zlp), 512), :]))
-    near = start_copies(token_copies(0), sems)
-    near += start_copies(kv_copies, sems, 4)
-    then = start_copies(q_copies, sems, 36)
-    far = start_copies(token_copies(1), sems, 44)
-
-    def turn(part, rows):
-        return part * cos_ref[rows, :] + pltpu.roll(part, 64, axis=1) * sin_ref[rows, :]
-
-    def rows_at(dzl):
-        return pl.ds(aligned((zl ^ dzl) * 512, 512), 512)
-
-    def kv_part(rows):
-        acc = jnp.dot(xs[rows, :], wkv[...], preferred_element_type=jnp.float32)
-        kv_out[rows, :128] = turn(acc[:, :128], rows).astype(jnp.bfloat16)
-        kv_out[rows, 128:] = acc[:, 128:].astype(jnp.bfloat16)
-
-    def q_part(rows):
+            copies.append((src, wq.at[pl.ds(weight_row(where, dzh, dy, zlp), 512), :]))
+    near = start_copies(token_copies(0, where, tok_refs, xs), sems)
+    near += start_copies(copies, sems, 4)
+    far = start_copies(token_copies(1, where, tok_refs, xs), sems, 12)
+    for dzl, waits in enumerate((near, far)):
+        wait_all(waits)
+        rows = pl.ds(aligned((where[1] ^ dzl) * 512, 512), 512)
         for n in range(2):
             acc = jnp.dot(
                 xs[rows, :], wq[:, 256 * n : 256 * n + 256], preferred_element_type=jnp.float32
             )
             for k in range(2):
+                part = turn(acc[:, 128 * k : 128 * k + 128], cos_ref, sin_ref, rows)
                 columns = slice(256 * n + 128 * k, 256 * n + 128 * k + 128)
-                part = acc[:, 128 * k : 128 * k + 128]
-                q_out[rows, columns] = turn(part, rows).astype(jnp.bfloat16)
-
-    wait_all(near)
-    kv_part(rows_at(0))
-    wait_all(then)
-    q_part(rows_at(0))
-    wait_all(far)
-    kv_part(rows_at(1))
-    q_part(rows_at(1))
+                q_out[rows, columns] = part.astype(jnp.bfloat16)
 
 
 FACTOR = math.log2(math.e) / math.sqrt(HEAD_WIDTH)
@@ -305,26 +315,27 @@
     ).astype(bf16)
     wkv = jnp.concatenate([wk.reshape(128, 8, 128), wv.reshape(128, 8, 128)], axis=2)
     wkv = jnp.concatenate([wkv, jnp.broadcast_to(below, (EXTRA, 8, 256))], axis=0)
-    wkv = jnp.transpose(wkv, (1, 0, 2))
+    wkv = lax.all_to_all(jnp.transpose(wkv, (1, 0, 2)), QUAD, 0, 0, tiled=True)
     wkv_z = swap(wkv, "zh")
-    wkv_y = swap(wkv, "y")
+    wkvs = [wkv, swap(wkv, "y"), wkv_z, swap(wkv_z, "y")]
 
     wqs = jnp.transpose(wq.reshape(128, 8, 512), (1, 0, 2))
-    wqs = lax.all_to_all(wqs, QUAD, 0, 0, tiled=True).reshape(1024, 512)
+    wqs = lax.all_to_all(after(wqs, wkv), QUAD, 0, 0, tiled=True).reshape(1024, 512)
     wq_z0 = swap(wqs[:512], "zh")
     wq_z1 = swap(wqs[512:], "zh")
     wq_y = swap(wqs, "y")
     wq_zy0 = swap(wq_z0, "y")
     wq_zy1 = swap(wq_z1, "y")
 
-    near = jnp.concatenate([wkv, wkv_y, wkv_z], axis=1)
-    near = lax.all_to_all(near, QUAD, 0, 0, tiled=True)
-    far = swap(near[:, 2 * (128 + EXTRA) :], "y")
-
     source = tokens.astype(f32)
     mean_sq = jnp.mean(source * source, axis=1, keepdims=True)
     normed = (source * lax.rsqrt(mean_sq + 1e-05) * norm_gain[None, :]).astype(bf16)
-    tok = quad_gather(after(normed, wqs), True)
+    normed = after(normed, wqs)
+    tok_z = [swap(normed[64 * i : 64 * i + 64], "zl") for i in range(2)]
+    tok_far = [swap(tok_z[i], "x") for i in range(2)]
+    tok = []
+    for piece in [normed, swap(normed, "x"), *tok_z, *tok_far]:
+        tok += [piece, swap(piece, "c")]
 
     token = jnp.arange(1024, dtype=jnp.int32)
     positions = (2 * zh + token // 512) * 1024 + y * 512 + token % 512
@@ -334,8 +345,8 @@
     cosine = jnp.concatenate([cosine, cosine], axis=1)
     sine = jnp.concatenate([-sine, sine], axis=1)
 
-    counts = [near[:, 128 + i * (128 + EXTRA), :DOCS] for i in range(3)] + [far[:, 128, :DOCS]]
-    starts = jnp.sum(jnp.concatenate(counts, axis=0).astype(f32), axis=0).astype(jnp.int32)
+    counts = jnp.concatenate([piece[:, 128, :DOCS] for piece in wkvs], axis=0)
+    starts = jnp.sum(counts.astype(f32), axis=0).astype(jnp.int32)
     query_start = jnp.max(
         jnp.where(positions[:, None] >= starts[None, :], starts[None, :], 0), axis=1
     )
@@ -343,24 +354,28 @@
     tile_hi = query_start[QT - 1 :: QT]
     start_col = jnp.broadcast_to(query_start[:, None], (1024, 128))
 
-    queries, keys_values = call(
-        project_kernel,
-        (
-            jax.ShapeDtypeStruct((1024, 512), bf16),
-            jax.ShapeDtypeStruct((1024, 256), bf16),
-        ),
+    keys_values = call(
+        project_kv_kernel,
+        jax.ShapeDtypeStruct((1024, 256), bf16),
         [SMEM] + [ANY] * 16 + [VMEM, VMEM],
         [
             pltpu.VMEM((1024, 4096), bf16),
+            pltpu.VMEM((4096, 256), bf16),
+            pltpu.SemaphoreType.DMA((44,)),
+        ],
+        (2 * 1024 * 4096 * 256, 11 << 20),
+    )(where, *tok, *wkvs, cosine, sine)
+    queries = call(
+        project_q_kernel,
+        jax.ShapeDtypeStruct((1024, 512), bf16),
+        [SMEM] + [ANY] * 18 + [VMEM, VMEM],
+        [
+            pltpu.VMEM((1024, 4096), bf16),
             pltpu.VMEM((4096, 512), bf16),
-            pltpu.VMEM((4096, 256), bf16),
-            pltpu.SemaphoreType.DMA((48,)),
+            pltpu.SemaphoreType.DMA((20,)),
         ],
-        (2 * 1024 * 4096 * 768, 17 << 20),
-    )(
-        where, *[tok[at] for at in OFFSETS],
-        wqs, wq_y, wq_z0, wq_z1, wq_zy0, wq_zy1, near, far, cosine, sine,
-    )
+        (2 * 1024 * 4096 * 512, 14 << 20),
+    )(where, *tok, wqs, wq_y, wq_z0, wq_z1, wq_zy0, wq_zy1, cosine, sine)
 
     kv_y = swap(keys_values, "y")
     kv_z = swap(keys_values, "zh")
@@ -416,6 +431,9 @@
     def output(half, first):
         att = quad_gather(attended[half], half == 1)
         rows = 1024 if first else 512
+        return output_call(att, first, rows)
+
+    def output_call(att, first, rows):
         return call(
             functools.partial(output_kernel, bool(first)),
             jax.ShapeDtypeStruct((rows, 512), bf16),

time: 362 us -> 309 us (0.85)
  waiting for transfers between devices: 223 us -> 153 us
  local copies, waits for them, and re-layouts: 11 us -> 20 us
  starting transfers between devices: 47.6 us -> 51.4 us
    ppermute x38 -> x42, waiting for transfers between devices: 223 us -> 144 us  [swap(): return lax.ppermute(value, axis, SWAP)]
    unnamed x42 -> x66, local copies, waits for them, and re-layouts: 3.92 us -> 12.6 us
    all_to_all x2, waiting for transfers between devices: 0.01 us -> 8.42 us  [the longest x1 8.41 us: split_body(): wkv = lax.all_to_all(jnp.transpose(wkv, (1, 0, 2)), QUAD, 0, 0, tiled=True)]
    ppermute x38 -> x42, starting transfers between devices: 36.7 us -> 43.6 us  [swap(): return lax.ppermute(value, axis, SWAP)]
    pallas_call x3 -> x4, Pallas kernels: 26.7 us -> 32.4 us  [the longest x2 12.8 us: output_call(): call(functools.partial(output_kernel, bool(first)), jax.ShapeDtypeStruct(...]
  transfers between devices with their start and end apart: 40 -> 44, of which waited for: 16 -> 18; matrix products, arithmetic and copies ran while one was open for 3% -> 4% of each run, Pallas kernels for 9% -> 16%
where the time goes in v2:
time: 309 us; the launch traced here: 308 us
  waiting for transfers between devices  153 us (50%)
  Pallas kernels  59.1 us (19%)
  starting transfers between devices  51.4 us (17%)
  local copies, waits for them, and re-layouts  20 us (6%)
  blocking collectives  18.4 us (6%)
  other arithmetic  5.77 us (2%)
    ppermute x42, waiting for transfers between devices, swap(): return lax.ppermute(value, axis, SWAP)  144 us
    ppermute x42, starting transfers between devices, swap(): return lax.ppermute(value, axis, SWAP)  43.6 us
    all_to_all x1, blocking collectives, split_body(): home = lax.all_to_all(sent.reshape(8, 128, 512), QUAD, 0, 0, tiled=True)  18.4 us
    pallas_call x2, Pallas kernels, far_call(): call(functools.partial(far_kernel, half), jax.ShapeDtypeStruct((512, 512)...  15.5 us
    pallas_call x2, Pallas kernels, output_call(): call(functools.partial(output_kernel, bool(first)), jax.ShapeDtypeStruct(...  12.8 us
    unnamed x66, local copies, waits for them, and re-layouts  12.6 us
    pallas_call x1, Pallas kernels, split_body(): call(project_q_kernel, jax.ShapeDtypeStruct((1024, 512), bf16), [SMEM] +...  10.4 us
    pallas_call x1, Pallas kernels, split_body(): call(near_kernel, [jax.ShapeDtypeStruct((4, 4 * QT, 128), f32)] * 3, [SME...  9.94 us
  transfers between devices with their start and end apart: 44, of which 18 were waited for; matrix products, arithmetic and copies ran while one was open for 4% of the time, Pallas kernels for 16%

profile of v2, /device:TPU:16, one launch (start us, length us, event | category | flops | bytes accessed | tf_op | source)
XLA Modules:
  0.0 307.7 jit_solution(11761425628534776182)
XLA Ops:
  0.8 1.1 copy.24
  2.1 1.2 copy.23
  3.5 0.9 maximum_bitcast_fusion
  4.4 4.2 %all-to-all-start = ((bf16[8,144,256]{2,1,0:T(8,128)(2,1)}), bf16[8,144,256]{2,1,0:T(8,128)(2,1)}, u32[]{:S(2)}, u32[]{:S(2)}) async-start(bf16[8,144,256]{2,1,0:T(8,128)(2,1)} %maximum_bitcast_fusion), calls=%async_computation | async-start | bytes 1179648 | tf_op jit(solution)/shard_map/all_to_all | solution.py:318
  8.6 1.1 copy.38
  9.8 8.4 %all-to-all-done.refs_12_ = bf16[8,144,256]{2,1,0:T(8,128)(2,1)} async-done(((bf16[8,144,256]{2,1,0:T(8,128)(2,1)}), bf16[8,144,256]{2,1,0:T(8,128)(2,1)}, u32[]{:S(2)}, u32[]{:S(2)}) %all-to-all-start) | async-done | bytes 589856 | tf_op jit(solution)/shard_map/all_to_all | solution.py:318
  18.2 3.6 %all-to-all-start.1 = ((bf16[8,128,512]{2,1,0:T(8,128)(2,1)}), bf16[8,128,512]{2,1,0:T(8,128)(2,1)S(1)}, u32[]{:S(2)}, u32[]{:S(2)}) async-start(bf16[8,128,512]{2,1,0:T(8,128)(2,1)} %bitcast.23), calls=%async_computation.1 | async-start | bytes 2097152 | tf_op jit(solution)/shard_map/all_to_all | solution.py:323
  22.1 1.3 fusion.2.refs_0_
  23.4 1.8 collective-permute-start
  25.3 23.3 %collective-permute-done.1.refs_14_ = bf16[8,144,256]{2,1,0:T(8,128)(2,1)} collective-permute-done((bf16[8,144,256]{2,1,0:T(8,128)(2,1)}, bf16[8,144,256]{2,1,0:T(8,128)(2,1)}, u32[]{:S(2)}, u32[]{:S(2)}) %collective-permute-start.1) | collective-permute-done | bytes 589856 | tf_op jit(solution)/shard_map/ppermute | solution.py:33
  48.6 1.5 collective-permute-start.2
  50.1 1.6 collective-permute-start.4
  51.8 1.3 fusion.18
  53.0 4.6 %collective-permute-start.6 = (bf16[64,4096]{1,0:T(8,128)(2,1)S(1)}, bf16[64,4096]{1,0:T(8,128)(2,1)S(1)}, u32[]{:S(2)}, u32[]{:S(2)}) collective-permute-start(bf16[64,4096]{1,0:T(8,128)(2,1)S(1)} %get-tuple-element.20), channel_id=1, source_target_pairs={{0,8},{8,0},{1,9},{9,1},{2,10},{10,2},{3,11},{11,3},{4,12},{12,4},... | collective-permute-start | bytes 1572872 | tf_op jit(solution)/shard_map/ppermute | solution.py:33
  57.8 0.9 collective-permute-start.15
  58.7 4.1 %collective-permute-done.2.refs_15_ = bf16[8,144,256]{2,1,0:T(8,128)(2,1)} collective-permute-done((bf16[8,144,256]{2,1,0:T(8,128)(2,1)}, bf16[8,144,256]{2,1,0:T(8,128)(2,1)}, u32[]{:S(2)}, u32[]{:S(2)}) %collective-permute-start.2) | collective-permute-done | bytes 589856 | tf_op jit(solution)/shard_map/ppermute | solution.py:33
  62.8 4.5 %collective-permute-start.16 = (bf16[512,512]{1,0:T(8,128)(2,1)S(1)}, bf16[512,512]{1,0:T(8,128)(2,1)S(1)}, u32[]{:S(2)}, u32[]{:S(2)}) collective-permute-start(bf16[512,512]{1,0:T(8,128)(2,1)S(1)} %bitcast.30), channel_id=1, source_target_pairs={{0,16},{16,0},{1,17},{17,1},{2,18},{18,2},{3,19},{19,3},{4,20},{20... | collective-permute-start | bytes 1572872 | tf_op jit(solution)/shard_map/ppermute | solution.py:33
  67.3 21.6 %collective-permute-done.6.refs_4_ = bf16[64,4096]{1,0:T(8,128)(2,1)S(1)} collective-permute-done((bf16[64,4096]{1,0:T(8,128)(2,1)S(1)}, bf16[64,4096]{1,0:T(8,128)(2,1)S(1)}, u32[]{:S(2)}, u32[]{:S(2)}) %collective-permute-start.6) | collective-permute-done | bytes 524320 | tf_op jit(solution)/shard_map/ppermute | solution.py:33
  88.9 9.0 %collective-permute-done.8.refs_6_ = bf16[64,4096]{1,0:T(8,128)(2,1)S(1)} collective-permute-done((bf16[64,4096]{1,0:T(8,128)(2,1)S(1)}, bf16[64,4096]{1,0:T(8,128)(2,1)S(1)}, u32[]{:S(2)}, u32[]{:S(2)}) %collective-permute-start.8) | collective-permute-done | bytes 524320 | tf_op jit(solution)/shard_map/ppermute | solution.py:33
  98.6 1.4 collective-permute-start.12
  99.9 1.8 collective-permute-done.16.refs_15_
  102.3 10.5 %collective-permute-done.10.refs_8_ = bf16[64,4096]{1,0:T(8,128)(2,1)} collective-permute-done((bf16[64,4096]{1,0:T(8,128)(2,1)S(1)}, bf16[64,4096]{1,0:T(8,128)(2,1)}, u32[]{:S(2)}, u32[]{:S(2)}) %collective-permute-start.10) | collective-permute-done | bytes 524320 | tf_op jit(solution)/shard_map/ppermute | solution.py:33
  112.8 8.1 %collective-permute-done.12.refs_10_ = bf16[64,4096]{1,0:T(8,128)(2,1)} collective-permute-done((bf16[64,4096]{1,0:T(8,128)(2,1)S(1)}, bf16[64,4096]{1,0:T(8,128)(2,1)}, u32[]{:S(2)}, u32[]{:S(2)}) %collective-permute-start.12) | collective-permute-done | bytes 524320 | tf_op jit(solution)/shard_map/ppermute | solution.py:33
  121.1 1.9 fusion.3
  123.0 0.8 copy-done.13
  124.7 1.6 collective-permute-start.17
  126.8 9.2 %shard_map.74.kv_own = bf16[1024,256]{1,0:T(8,128)(2,1)} custom-call(s32[5]{0:T(128)S(1)} %stack.23.where, bf16[128,4096]{1,0:T(8,128)(2,1)} %fusion.2.refs_0_, bf16[128,4096]{1,0:T(8,128)(2,1)} %collective-permute-done.3.refs_1_, bf16[128,4096]{1,0:T(8,128)(2,1)} %collective-permute-done.4.refs_2_, bf16[128,4096]{1,0:T(8,128)(2,1)} %collective-permute-done.5.refs_3_, ...), custom_call_target="tpu_custom_call" | custom-call | flops 2147483648 | bytes 11534336 | tf_op jit(solution)/shard_map/pallas_call | solution.py:357
  136.1 4.5 %collective-permute-start.19 = (bf16[1024,256]{1,0:T(8,128)(2,1)}, bf16[1024,256]{1,0:T(8,128)(2,1)S(1)}, u32[]{:S(2)}, u32[]{:S(2)}) collective-permute-start(bf16[1024,256]{1,0:T(8,128)(2,1)} %shard_map.74.kv_own), channel_id=1, source_target_pairs={{0,16},{16,0},{1,17},{17,1},{2,18},{18,2},{3,19},{19,3},{4,20},{20... | collective-permute-start | bytes 1572872 | tf_op jit(solution)/shard_map/ppermute | solution.py:33
  140.6 0.9 fusion.16
  141.5 19.8 %collective-permute-done.17.refs_16_ = bf16[512,512]{1,0:T(8,128)(2,1)S(1)} collective-permute-done((bf16[512,512]{1,0:T(8,128)(2,1)S(1)}, bf16[512,512]{1,0:T(8,128)(2,1)S(1)}, u32[]{:S(2)}, u32[]{:S(2)}) %collective-permute-start.17) | collective-permute-done | bytes 524320 | tf_op jit(solution)/shard_map/ppermute | solution.py:33
  161.3 0.8 copy-done.22
  162.1 3.3 %collective-permute-start.33 = (bf16[2048,128]{1,0:T(8,128)(2,1)}, bf16[2048,128]{1,0:T(8,128)(2,1)}, u32[]{:S(2)}, u32[]{:S(2)}) collective-permute-start(bf16[2048,128]{1,0:T(8,128)(2,1)} %get-tuple-element.15.refs_12_), channel_id=1, source_target_pairs={{0,16},{16,0},{1,17},{17,1},{2,18},{18,2},{3,19},{19,3},{4,20},{20... | collective-permute-start | bytes 1572872 | tf_op jit(solution)/shard_map/ppermute | solution.py:33
  165.4 6.7 %collective-permute-done.18.refs_17_ = bf16[512,512]{1,0:T(8,128)(2,1)S(1)} collective-permute-done((bf16[512,512]{1,0:T(8,128)(2,1)S(1)}, bf16[512,512]{1,0:T(8,128)(2,1)S(1)}, u32[]{:S(2)}, u32[]{:S(2)}) %collective-permute-start.18) | collective-permute-done | bytes 524320 | tf_op jit(solution)/shard_map/ppermute | solution.py:33
  176.5 1.3 collective-permute-start.29
  177.8 6.8 %collective-permute-done.19.kv_z = bf16[1024,256]{1,0:T(8,128)(2,1)S(1)} collective-permute-done((bf16[1024,256]{1,0:T(8,128)(2,1)}, bf16[1024,256]{1,0:T(8,128)(2,1)S(1)}, u32[]{:S(2)}, u32[]{:S(2)}) %collective-permute-start.19) | collective-permute-done | bytes 524320 | tf_op jit(solution)/shard_map/ppermute | solution.py:33
  185.1 1.0 copy-done.10
  186.1 1.0 copy-done.12
  187.2 1.0 copy-done.15
  188.2 1.0 copy-done.18
  189.3 1.0 copy-done.21
  190.3 1.0 copy-done.23
  191.3 10.4 %shard_map.73.q_ref = bf16[1024,512]{1,0:T(8,128)(2,1)} custom-call(s32[5]{0:T(128)S(1)} %stack.23.where, bf16[128,4096]{1,0:T(8,128)(2,1)} %fusion.2.refs_0_, bf16[128,4096]{1,0:T(8,128)(2,1)} %collective-permute-done.3.refs_1_, bf16[128,4096]{1,0:T(8,128)(2,1)} %collective-permute-done.4.refs_2_, bf16[128,4096]{1,0:T(8,128)(2,1)} %collective-permute-done.5.refs_3_, ...), custom_call_target="tpu_custom_call" | custom-call | flops 4294967296 | bytes 14680064 | tf_op jit(solution)/shard_map/pallas_call | solution.py:368
  201.8 1.7 collective-permute-start.32
  203.4 3.6 %collective-permute-done.33.refs_14_ = bf16[2048,128]{1,0:T(8,128)(2,1)} collective-permute-done((bf16[2048,128]{1,0:T(8,128)(2,1)}, bf16[2048,128]{1,0:T(8,128)(2,1)}, u32[]{:S(2)}, u32[]{:S(2)}) %collective-permute-start.33) | collective-permute-done | bytes 524320 | tf_op jit(solution)/shard_map/ppermute | solution.py:33
  207.5 1.6 collective-permute-start.34
  209.3 1.2 copy-done.1
  210.5 9.9 %shard_map.75 = (f32[4,1024,128]{2,1,0:T(8,128)S(1)}, f32[4,1024,128]{2,1,0:T(8,128)}, f32[4,1024,128]{2,1,0:T(8,128)}) custom-call(s32[5]{0:T(128)S(1)} %stack.23.where, s32[4]{0:T(128)S(1)} %slice.46.tile_lo, s32[4]{0:T(128)S(1)} %slice.47.tile_hi, bf16[1024,512]{1,0:T(8,128)(2,1)S(1)} %copy-done.1, s32[1024,128]{1,0:T(8,128)S(1)} %broadcast_in_dim.12.start_ref, ...), custom_call_target="tpu_custom_call" | custom-call | flops 4294967296 | bytes 8388608 | tf_op jit(solution)/shard_map/pallas_call | solution.py:390
  220.5 9.4 %shard_map.77.refs_0_ = bf16[512,512]{1,0:T(8,128)(2,1)S(1)} custom-call(s32[5]{0:T(128)S(1)} %stack.23.where, s32[4]{0:T(128)S(1)} %slice.46.tile_lo, s32[4]{0:T(128)S(1)} %slice.47.tile_hi, bf16[1024,512]{1,0:T(8,128)(2,1)S(1)} %copy-done.1, s32[1024,128]{1,0:T(8,128)S(1)} %broadcast_in_dim.12.start_ref, ...), custom_call_target="tpu_custom_call" | custom-call | flops 2147483648 | bytes 8388608 | tf_op jit(solution)/shard_map/pallas_call | solution.py:405
  229.9 1.0 collective-permute-start.36
  230.9 6.1 %shard_map.76.refs_0_ = bf16[512,512]{1,0:T(8,128)(2,1)S(1)} custom-call(s32[5]{0:T(128)S(1)} %stack.23.where, s32[4]{0:T(128)S(1)} %slice.46.tile_lo, s32[4]{0:T(128)S(1)} %slice.47.tile_hi, bf16[1024,512]{1,0:T(8,128)(2,1)S(1)} %copy-done.1, s32[1024,128]{1,0:T(8,128)S(1)} %broadcast_in_dim.12.start_ref, ...), custom_call_target="tpu_custom_call" | custom-call | flops 2147483648 | bytes 8388608 | tf_op jit(solution)/shard_map/pallas_call | solution.py:405
  237.0 2.4 collective-permute-start.25
  239.4 1.3 collective-permute-start.23
  240.7 4.0 %collective-permute-done.36.refs_2_ = bf16[512,512]{1,0:T(8,128)(2,1)S(1)} collective-permute-done((bf16[512,512]{1,0:T(8,128)(2,1)S(1)}, bf16[512,512]{1,0:T(8,128)(2,1)S(1)}, u32[]{:S(2)}, u32[]{:S(2)}) %collective-permute-start.36) | collective-permute-done | bytes 524320 | tf_op jit(solution)/shard_map/ppermute | solution.py:33
  244.8 2.5 collective-permute-start.40
  247.3 4.9 %collective-permute-done.25.refs_4_ = bf16[512,512]{1,0:T(8,128)(2,1)S(1)} collective-permute-done((bf16[512,512]{1,0:T(8,128)(2,1)S(1)}, bf16[512,512]{1,0:T(8,128)(2,1)S(1)}, u32[]{:S(2)}, u32[]{:S(2)}) %collective-permute-start.25) | collective-permute-done | bytes 524320 | tf_op jit(solution)/shard_map/ppermute | solution.py:33
  252.1 1.3 collective-permute-start.27
  253.4 2.6 collective-permute-done.23.refs_2_
  256.0 7.4 %collective-permute-done.38.refs_4_ = bf16[512,512]{1,0:T(8,128)(2,1)S(1)} collective-permute-done((bf16[512,512]{1,0:T(8,128)(2,1)S(1)}, bf16[512,512]{1,0:T(8,128)(2,1)S(1)}, u32[]{:S(2)}, u32[]{:S(2)}) %collective-permute-start.38) | collective-permute-done | bytes 524320 | tf_op jit(solution)/shard_map/ppermute | solution.py:33
  263.4 9.2 %collective-permute-done.40.refs_6_ = bf16[512,512]{1,0:T(8,128)(2,1)S(1)} collective-permute-done((bf16[512,512]{1,0:T(8,128)(2,1)S(1)}, bf16[512,512]{1,0:T(8,128)(2,1)S(1)}, u32[]{:S(2)}, u32[]{:S(2)}) %collective-permute-start.40) | collective-permute-done | bytes 524320 | tf_op jit(solution)/shard_map/ppermute | solution.py:33
  273.6 0.8 collective-permute-done.41.refs_7_
  274.5 5.7 %shard_map.78.refs_16_ = bf16[512,512]{1,0:T(8,128)(2,1)S(1)} custom-call(s32[5]{0:T(128)S(1)} %stack.23.where, bf16[512,512]{1,0:T(8,128)(2,1)S(1)} %shard_map.77.refs_0_, bf16[512,512]{1,0:T(8,128)(2,1)S(1)} %collective-permute-done.35.refs_1_, bf16[512,512]{1,0:T(8,128)(2,1)S(1)} %collective-permute-done.36.refs_2_, ...), custom_call_target="tpu_custom_call" | custom-call | flops 2147483648 | bytes 9437184 | tf_op jit(solution)/shard_map/pallas_call | solution.py:437
  281.0 7.1 %shard_map.79 = bf16[1024,512]{1,0:T(8,128)(2,1)} custom-call(s32[5]{0:T(128)S(1)} %stack.23.where, bf16[512,512]{1,0:T(8,128)(2,1)S(1)} %shard_map.76.refs_0_, bf16[512,512]{1,0:T(8,128)(2,1)S(1)} %collective-permute-done.22.refs_1_, bf16[512,512]{1,0:T(8,128)(2,1)S(1)} %collective-permute-done.23.refs_2_, ...), custom_call_target="tpu_custom_call" | custom-call | flops 2147483648 | bytes 9437184 | tf_op jit(solution)/shard_map/pallas_call | solution.py:437
  288.1 18.4 %all_to_all.15.sent_ref = bf16[8,128,512]{2,1,0:T(8,128)(2,1)S(1)} all-to-all(bf16[8,128,512]{2,1,0:T(8,128)(2,1)} %bitcast.24), channel_id=1, replica_groups=mesh['zh'=2,'zl'=2,'y'=2,'x'=2,'c'=2] {'zl','x','c'}, dimensions={0} | all-to-all | bytes 2097152 | tf_op jit(solution)/shard_map/all_to_all | solution.py:450
  306.4 1.3 shard_map.80
  (132 shorter events, 12.0 us)
Async XLA Ops:
  1.9 6.7 %copy-start.28 = (bf16[128,4096]{1,0:T(8,128)(2,1)S(1)}, bf16[128,4096]{1,0:T(8,128)(2,1)}, u32[]{:S(2)}) copy-start(bf16[128,4096]{1,0:T(8,128)(2,1)} %param.9) | copy-start | bytes 3145732
  4.4 13.8 %all-to-all-start = ((bf16[8,144,256]{2,1,0:T(8,128)(2,1)}), bf16[8,144,256]{2,1,0:T(8,128)(2,1)}, u32[]{:S(2)}, u32[]{:S(2)}) async-start(bf16[8,144,256]{2,1,0:T(8,128)(2,1)} %maximum_bitcast_fusion), calls=%async_computation | async-start | bytes 1179648 | tf_op jit(solution)/shard_map/all_to_all | solution.py:318
  8.6 13.1 %copy-start = (bf16[128,4096]{1,0:T(8,128)(2,1)S(1)}, bf16[128,4096]{1,0:T(8,128)(2,1)}, u32[]{:S(2)}) copy-start(bf16[128,4096]{1,0:T(8,128)(2,1)} %tok_ref.1) | copy-start | bytes 3145732
  9.7 12.4 %copy-start.30 = (f32[4096]{0:T(1024)S(1)}, f32[4096]{0:T(1024)}, u32[]{:S(2)}) copy-start(f32[4096]{0:T(1024)} %param.8) | copy-start | bytes 49156
  18.2 31.9 %all-to-all-start.1 = ((bf16[8,128,512]{2,1,0:T(8,128)(2,1)}), bf16[8,128,512]{2,1,0:T(8,128)(2,1)S(1)}, u32[]{:S(2)}, u32[]{:S(2)}) async-start(bf16[8,128,512]{2,1,0:T(8,128)(2,1)} %bitcast.23), calls=%async_computation.1 | async-start | bytes 2097152 | tf_op jit(solution)/shard_map/all_to_all | solution.py:323
  22.0 26.5 %collective-permute-start.1 = (bf16[8,144,256]{2,1,0:T(8,128)(2,1)}, bf16[8,144,256]{2,1,0:T(8,128)(2,1)}, u32[]{:S(2)}, u32[]{:S(2)}) collective-permute-start(bf16[8,144,256]{2,1,0:T(8,128)(2,1)} %all-to-all-done.refs_12_), channel_id=1, source_target_pairs={{0,16},{16,0},{1,17},{17,1},{2,18},{18,2},{3,19},{19,3},{4,20},{20... | collective-permute-start | bytes 1769480 | tf_op jit(solution)/shard_map/ppermute | solution.py:33
  23.4 34.4 %collective-permute-start = (bf16[8,144,256]{2,1,0:T(8,128)(2,1)}, bf16[8,144,256]{2,1,0:T(8,128)(2,1)}, u32[]{:S(2)}, u32[]{:S(2)}) collective-permute-start(bf16[8,144,256]{2,1,0:T(8,128)(2,1)} %all-to-all-done.refs_12_), channel_id=1, source_target_pairs={{0,4},{4,0},{1,5},{5,1},{2,6},{6,2},{3,7},{7,3},{8,12},{12,8},{9,1... | collective-permute-start | bytes 1769480 | tf_op jit(solution)/shard_map/ppermute | solution.py:33
  48.6 14.2 %collective-permute-start.2 = (bf16[8,144,256]{2,1,0:T(8,128)(2,1)}, bf16[8,144,256]{2,1,0:T(8,128)(2,1)}, u32[]{:S(2)}, u32[]{:S(2)}) collective-permute-start(bf16[8,144,256]{2,1,0:T(8,128)(2,1)} %collective-permute-done.1.refs_14_), channel_id=1, source_target_pairs={{0,4},{4,0},{1,5},{5,1},{2,6},{6,2},{3,7},{7,3},{8,12},{12,8},{9,1... | collective-permute-start | bytes 1769480 | tf_op jit(solution)/shard_map/ppermute | solution.py:33
  50.1 7.7 %copy-start.24 = (bf16[8,128,512]{2,1,0:T(8,128)(2,1)}, bf16[8,128,512]{2,1,0:T(8,128)(2,1)S(1)}, u32[]{:S(2)}) copy-start(bf16[8,128,512]{2,1,0:T(8,128)(2,1)S(1)} %all-to-all-done.1) | copy-start | bytes 3145732
  50.1 51.6 %collective-permute-start.4 = (bf16[128,4096]{1,0:T(8,128)(2,1)}, bf16[128,4096]{1,0:T(8,128)(2,1)}, u32[]{:S(2)}, u32[]{:S(2)}) collective-permute-start(bf16[128,4096]{1,0:T(8,128)(2,1)} %fusion.2.refs_0_), channel_id=1, source_target_pairs={{0,2},{2,0},{1,3},{3,1},{4,6},{6,4},{5,7},{7,5},{8,10},{10,8},{9,1... | collective-permute-start | bytes 3145736 | tf_op jit(solution)/shard_map/ppermute | solution.py:33
  53.0 35.9 %collective-permute-start.6 = (bf16[64,4096]{1,0:T(8,128)(2,1)S(1)}, bf16[64,4096]{1,0:T(8,128)(2,1)S(1)}, u32[]{:S(2)}, u32[]{:S(2)}) collective-permute-start(bf16[64,4096]{1,0:T(8,128)(2,1)S(1)} %get-tuple-element.20), channel_id=1, source_target_pairs={{0,8},{8,0},{1,9},{9,1},{2,10},{10,2},{3,11},{11,3},{4,12},{12,4},... | collective-permute-start | bytes 1572872 | tf_op jit(solution)/shard_map/ppermute | solution.py:33
  57.6 40.3 %collective-permute-start.8 = (bf16[64,4096]{1,0:T(8,128)(2,1)S(1)}, bf16[64,4096]{1,0:T(8,128)(2,1)S(1)}, u32[]{:S(2)}, u32[]{:S(2)}) collective-permute-start(bf16[64,4096]{1,0:T(8,128)(2,1)S(1)} %get-tuple-element.19), channel_id=1, source_target_pairs={{0,8},{8,0},{1,9},{9,1},{2,10},{10,2},{3,11},{11,3},{4,12},{12,4},... | collective-permute-start | bytes 1572872 | tf_op jit(solution)/shard_map/ppermute | solution.py:33
  57.8 40.8 %collective-permute-start.15 = (bf16[512,512]{1,0:T(8,128)(2,1)S(1)}, bf16[512,512]{1,0:T(8,128)(2,1)S(1)}, u32[]{:S(2)}, u32[]{:S(2)}) collective-permute-start(bf16[512,512]{1,0:T(8,128)(2,1)S(1)} %bitcast.31), channel_id=1, source_target_pairs={{0,16},{16,0},{1,17},{17,1},{2,18},{18,2},{3,19},{19,3},{4,20},{20... | collective-permute-start | bytes 1572872 | tf_op jit(solution)/shard_map/ppermute | solution.py:33
  62.8 38.9 %collective-permute-start.16 = (bf16[512,512]{1,0:T(8,128)(2,1)S(1)}, bf16[512,512]{1,0:T(8,128)(2,1)S(1)}, u32[]{:S(2)}, u32[]{:S(2)}) collective-permute-start(bf16[512,512]{1,0:T(8,128)(2,1)S(1)} %bitcast.30), channel_id=1, source_target_pairs={{0,16},{16,0},{1,17},{17,1},{2,18},{18,2},{3,19},{19,3},{4,20},{20... | collective-permute-start | bytes 1572872 | tf_op jit(solution)/shard_map/ppermute | solution.py:33
  88.9 37.9 %copy-start.7 = (bf16[64,4096]{1,0:T(8,128)(2,1)}, bf16[64,4096]{1,0:T(8,128)(2,1)S(1)}, u32[]{:S(2)}) copy-start(bf16[64,4096]{1,0:T(8,128)(2,1)S(1)} %collective-permute-done.6.refs_4_) | copy-start | bytes 1572868
  88.9 13.3 %collective-permute-start.7 = (bf16[64,4096]{1,0:T(8,128)(2,1)S(1)}, bf16[64,4096]{1,0:T(8,128)(2,1)S(1)}, u32[]{:S(2)}, u32[]{:S(2)}) collective-permute-start(bf16[64,4096]{1,0:T(8,128)(2,1)S(1)} %collective-permute-done.6.refs_4_), channel_id=1, source_target_pairs={{0,1},{1,0},{2,3},{3,2},{4,5},{5,4},{6,7},{7,6},{8,9},{9,8},{10,11... | collective-permute-start | bytes 1572872 | tf_op jit(solution)/shard_map/ppermute | solution.py:33
  97.9 28.9 %copy-start.9 = (bf16[64,4096]{1,0:T(8,128)(2,1)}, bf16[64,4096]{1,0:T(8,128)(2,1)S(1)}, u32[]{:S(2)}) copy-start(bf16[64,4096]{1,0:T(8,128)(2,1)S(1)} %collective-permute-done.8.refs_6_) | copy-start | bytes 1572868
  97.9 14.9 %collective-permute-start.10 = (bf16[64,4096]{1,0:T(8,128)(2,1)S(1)}, bf16[64,4096]{1,0:T(8,128)(2,1)}, u32[]{:S(2)}, u32[]{:S(2)}) collective-permute-start(bf16[64,4096]{1,0:T(8,128)(2,1)S(1)} %collective-permute-done.6.refs_4_), channel_id=1, source_target_pairs={{0,2},{2,0},{1,3},{3,1},{4,6},{6,4},{5,7},{7,5},{8,10},{10,8},{9,1... | collective-permute-start | bytes 1572872 | tf_op jit(solution)/shard_map/ppermute | solution.py:33
  98.6 22.4 %copy-start.16 = (bf16[512,512]{1,0:T(8,128)(2,1)}, bf16[512,512]{1,0:T(8,128)(2,1)S(1)}, u32[]{:S(2)}) copy-start(bf16[512,512]{1,0:T(8,128)(2,1)S(1)} %collective-permute-done.15.refs_14_) | copy-start | bytes 1572868
  98.6 22.4 %collective-permute-start.12 = (bf16[64,4096]{1,0:T(8,128)(2,1)S(1)}, bf16[64,4096]{1,0:T(8,128)(2,1)}, u32[]{:S(2)}, u32[]{:S(2)}) collective-permute-start(bf16[64,4096]{1,0:T(8,128)(2,1)S(1)} %collective-permute-done.8.refs_6_), channel_id=1, source_target_pairs={{0,2},{2,0},{1,3},{3,1},{4,6},{6,4},{5,7},{7,5},{8,10},{10,8},{9,1... | collective-permute-start | bytes 1572872 | tf_op jit(solution)/shard_map/ppermute | solution.py:33
  101.7 19.2 %copy-start.19 = (bf16[512,512]{1,0:T(8,128)(2,1)}, bf16[512,512]{1,0:T(8,128)(2,1)S(1)}, u32[]{:S(2)}) copy-start(bf16[512,512]{1,0:T(8,128)(2,1)S(1)} %collective-permute-done.16.refs_15_) | copy-start | bytes 1572868
  101.7 23.0 %collective-permute-start.3 = (bf16[128,4096]{1,0:T(8,128)(2,1)}, bf16[128,4096]{1,0:T(8,128)(2,1)}, u32[]{:S(2)}, u32[]{:S(2)}) collective-permute-start(bf16[128,4096]{1,0:T(8,128)(2,1)} %fusion.2.refs_0_), channel_id=1, source_target_pairs={{0,1},{1,0},{2,3},{3,2},{4,5},{5,4},{6,7},{7,6},{8,9},{9,8},{10,11... | collective-permute-start | bytes 3145736 | tf_op jit(solution)/shard_map/ppermute | solution.py:33
  101.7 25.1 %collective-permute-start.5 = (bf16[128,4096]{1,0:T(8,128)(2,1)}, bf16[128,4096]{1,0:T(8,128)(2,1)}, u32[]{:S(2)}, u32[]{:S(2)}) collective-permute-start(bf16[128,4096]{1,0:T(8,128)(2,1)} %collective-permute-done.4.refs_2_), channel_id=1, source_target_pairs={{0,1},{1,0},{2,3},{3,2},{4,5},{5,4},{6,7},{7,6},{8,9},{9,8},{10,11... | collective-permute-start | bytes 3145736 | tf_op jit(solution)/shard_map/ppermute | solution.py:33
  102.2 24.6 %copy-start.11 = (bf16[64,4096]{1,0:T(8,128)(2,1)}, bf16[64,4096]{1,0:T(8,128)(2,1)S(1)}, u32[]{:S(2)}) copy-start(bf16[64,4096]{1,0:T(8,128)(2,1)S(1)} %collective-permute-done.7.refs_5_) | copy-start | bytes 1572868
  102.2 20.7 %collective-permute-start.9 = (bf16[64,4096]{1,0:T(8,128)(2,1)S(1)}, bf16[64,4096]{1,0:T(8,128)(2,1)S(1)}, u32[]{:S(2)}, u32[]{:S(2)}) collective-permute-start(bf16[64,4096]{1,0:T(8,128)(2,1)S(1)} %collective-permute-done.8.refs_6_), channel_id=1, source_target_pairs={{0,1},{1,0},{2,3},{3,2},{4,5},{5,4},{6,7},{7,6},{8,9},{9,8},{10,11... | collective-permute-start | bytes 1572872 | tf_op jit(solution)/shard_map/ppermute | solution.py:33
  112.8 13.5 %collective-permute-start.11 = (bf16[64,4096]{1,0:T(8,128)(2,1)}, bf16[64,4096]{1,0:T(8,128)(2,1)}, u32[]{:S(2)}, u32[]{:S(2)}) collective-permute-start(bf16[64,4096]{1,0:T(8,128)(2,1)} %collective-permute-done.10.refs_8_), channel_id=1, source_target_pairs={{0,1},{1,0},{2,3},{3,2},{4,5},{5,4},{6,7},{7,6},{8,9},{9,8},{10,11... | collective-permute-start | bytes 1572872 | tf_op jit(solution)/shard_map/ppermute | solution.py:33
  120.9 5.9 %collective-permute-start.13 = (bf16[64,4096]{1,0:T(8,128)(2,1)}, bf16[64,4096]{1,0:T(8,128)(2,1)}, u32[]{:S(2)}, u32[]{:S(2)}) collective-permute-start(bf16[64,4096]{1,0:T(8,128)(2,1)} %collective-permute-done.12.refs_10_), channel_id=1, source_target_pairs={{0,1},{1,0},{2,3},{3,2},{4,5},{5,4},{6,7},{7,6},{8,9},{9,8},{10,11... | collective-permute-start | bytes 1572872 | tf_op jit(solution)/shard_map/ppermute | solution.py:33
  121.1 3.6 %copy-start.17 = (bf16[512,512]{1,0:T(8,128)(2,1)S(1)}, bf16[512,512]{1,0:T(8,128)(2,1)}, u32[]{:S(2)}) copy-start(bf16[512,512]{1,0:T(8,128)(2,1)} %copy-done.16) | copy-start | bytes 1572868
  121.1 5.2 %copy-start.20 = (bf16[512,512]{1,0:T(8,128)(2,1)S(1)}, bf16[512,512]{1,0:T(8,128)(2,1)}, u32[]{:S(2)}) copy-start(bf16[512,512]{1,0:T(8,128)(2,1)} %copy-done.19) | copy-start | bytes 1572868
  123.8 52.7 %collective-permute-start.14 = (bf16[1024,512]{1,0:T(8,128)(2,1)}, bf16[1024,512]{1,0:T(8,128)(2,1)}, u32[]{:S(2)}, u32[]{:S(2)}) collective-permute-start(bf16[1024,512]{1,0:T(8,128)(2,1)} %bitcast.25), channel_id=1, source_target_pairs={{0,4},{4,0},{1,5},{5,1},{2,6},{6,2},{3,7},{7,3},{8,12},{12,8},{9,1... | collective-permute-start | bytes 3145736 | tf_op jit(solution)/shard_map/ppermute | solution.py:33
  124.7 11.4 %copy-start.4 = (f32[1024,128]{1,0:T(8,128)}, f32[1024,128]{1,0:T(8,128)S(1)}, u32[]{:S(2)}) copy-start(f32[1024,128]{1,0:T(8,128)S(1)} %get-tuple-element.24.refs_18_.refs_16_) | copy-start | bytes 1572868
  124.7 11.4 %copy-start.5 = (f32[1024,128]{1,0:T(8,128)}, f32[1024,128]{1,0:T(8,128)S(1)}, u32[]{:S(2)}) copy-start(f32[1024,128]{1,0:T(8,128)S(1)} %get-tuple-element.25.refs_19_.refs_17_) | copy-start | bytes 1572868
  124.7 36.6 %collective-permute-start.17 = (bf16[512,512]{1,0:T(8,128)(2,1)S(1)}, bf16[512,512]{1,0:T(8,128)(2,1)S(1)}, u32[]{:S(2)}, u32[]{:S(2)}) collective-permute-start(bf16[512,512]{1,0:T(8,128)(2,1)S(1)} %copy-done.17), channel_id=1, source_target_pairs={{0,4},{4,0},{1,5},{5,1},{2,6},{6,2},{3,7},{7,3},{8,12},{12,8},{9,1... | collective-permute-start | bytes 1572872 | tf_op jit(solution)/shard_map/ppermute | solution.py:33
  126.3 45.8 %collective-permute-start.18 = (bf16[512,512]{1,0:T(8,128)(2,1)S(1)}, bf16[512,512]{1,0:T(8,128)(2,1)S(1)}, u32[]{:S(2)}, u32[]{:S(2)}) collective-permute-start(bf16[512,512]{1,0:T(8,128)(2,1)S(1)} %copy-done.20), channel_id=1, source_target_pairs={{0,4},{4,0},{1,5},{5,1},{2,6},{6,2},{3,7},{7,3},{8,12},{12,8},{9,1... | collective-permute-start | bytes 1572872 | tf_op jit(solution)/shard_map/ppermute | solution.py:33
  126.8 13.7 %copy-start.29 = (bf16[4096,128]{1,0:T(8,128)(2,1)S(1)}, bf16[4096,128]{1,0:T(8,128)(2,1)}, u32[]{:S(2)}) copy-start(bf16[4096,128]{1,0:T(8,128)(2,1)} %param.12) | copy-start | bytes 3145732
  136.1 48.6 %collective-permute-start.19 = (bf16[1024,256]{1,0:T(8,128)(2,1)}, bf16[1024,256]{1,0:T(8,128)(2,1)S(1)}, u32[]{:S(2)}, u32[]{:S(2)}) collective-permute-start(bf16[1024,256]{1,0:T(8,128)(2,1)} %shard_map.74.kv_own), channel_id=1, source_target_pairs={{0,16},{16,0},{1,17},{17,1},{2,18},{18,2},{3,19},{19,3},{4,20},{20... | collective-permute-start | bytes 1572872 | tf_op jit(solution)/shard_map/ppermute | solution.py:33
  140.6 44.5 %copy-start.8 = (bf16[64,4096]{1,0:T(8,128)(2,1)S(1)}, bf16[64,4096]{1,0:T(8,128)(2,1)}, u32[]{:S(2)}) copy-start(bf16[64,4096]{1,0:T(8,128)(2,1)} %copy-done.7) | copy-start | bytes 1572868
  141.4 60.3 %collective-permute-start.30 = (bf16[2048,128]{1,0:T(8,128)(2,1)S(1)}, bf16[2048,128]{1,0:T(8,128)(2,1)S(1)}, u32[]{:S(2)}, u32[]{:S(2)}) collective-permute-start(bf16[2048,128]{1,0:T(8,128)(2,1)S(1)} %get-tuple-element.16.refs_8_), channel_id=1, source_target_pairs={{0,16},{16,0},{1,17},{17,1},{2,18},{18,2},{3,19},{19,3},{4,20},{20... | collective-permute-start | bytes 1572872 | tf_op jit(solution)/shard_map/ppermute | solution.py:33
  162.1 45.0 %collective-permute-start.33 = (bf16[2048,128]{1,0:T(8,128)(2,1)}, bf16[2048,128]{1,0:T(8,128)(2,1)}, u32[]{:S(2)}, u32[]{:S(2)}) collective-permute-start(bf16[2048,128]{1,0:T(8,128)(2,1)} %get-tuple-element.15.refs_12_), channel_id=1, source_target_pairs={{0,16},{16,0},{1,17},{17,1},{2,18},{18,2},{3,19},{19,3},{4,20},{20... | collective-permute-start | bytes 1572872 | tf_op jit(solution)/shard_map/ppermute | solution.py:33
  172.0 35.4 %collective-permute-start.21 = (bf16[1024,256]{1,0:T(8,128)(2,1)}, bf16[1024,256]{1,0:T(8,128)(2,1)}, u32[]{:S(2)}, u32[]{:S(2)}) collective-permute-start(bf16[1024,256]{1,0:T(8,128)(2,1)} %shard_map.74.kv_own), channel_id=1, source_target_pairs={{0,4},{4,0},{1,5},{5,1},{2,6},{6,2},{3,7},{7,3},{8,12},{12,8},{9,1... | collective-permute-start | bytes 1572872 | tf_op jit(solution)/shard_map/ppermute | solution.py:33
  176.5 60.4 %collective-permute-start.29 = (bf16[2048,128]{1,0:T(8,128)(2,1)S(1)}, bf16[2048,128]{1,0:T(8,128)(2,1)S(1)}, u32[]{:S(2)}, u32[]{:S(2)}) collective-permute-start(bf16[2048,128]{1,0:T(8,128)(2,1)S(1)} %get-tuple-element.16.refs_8_), channel_id=1, source_target_pairs={{0,4},{4,0},{1,5},{5,1},{2,6},{6,2},{3,7},{7,3},{8,12},{12,8},{9,1... | collective-permute-start | bytes 1572872 | tf_op jit(solution)/shard_map/ppermute | solution.py:33
  184.7 35.8 %collective-permute-start.20 = (bf16[1024,256]{1,0:T(8,128)(2,1)S(1)}, bf16[1024,256]{1,0:T(8,128)(2,1)S(1)}, u32[]{:S(2)}, u32[]{:S(2)}) collective-permute-start(bf16[1024,256]{1,0:T(8,128)(2,1)S(1)} %collective-permute-done.19.kv_z), channel_id=1, source_target_pairs={{0,4},{4,0},{1,5},{5,1},{2,6},{6,2},{3,7},{7,3},{8,12},{12,8},{9,1... | collective-permute-start | bytes 1572872 | tf_op jit(solution)/shard_map/ppermute | solution.py:33
  201.8 18.7 %copy-start.2 = (bf16[2048,128]{1,0:T(8,128)(2,1)}, bf16[2048,128]{1,0:T(8,128)(2,1)S(1)}, u32[]{:S(2)}) copy-start(bf16[2048,128]{1,0:T(8,128)(2,1)S(1)} %collective-permute-done.30.refs_10_) | copy-start | bytes 1572868
  201.8 37.6 %collective-permute-start.32 = (bf16[2048,128]{1,0:T(8,128)(2,1)}, bf16[2048,128]{1,0:T(8,128)(2,1)S(1)}, u32[]{:S(2)}, u32[]{:S(2)}) collective-permute-start(bf16[2048,128]{1,0:T(8,128)(2,1)} %get-tuple-element.15.refs_12_), channel_id=1, source_target_pairs={{0,4},{4,0},{1,5},{5,1},{2,6},{6,2},{3,7},{7,3},{8,12},{12,8},{9,1... | collective-permute-start | bytes 1572872 | tf_op jit(solution)/shard_map/ppermute | solution.py:33
  207.0 33.6 %collective-permute-start.31 = (bf16[2048,128]{1,0:T(8,128)(2,1)S(1)}, bf16[2048,128]{1,0:T(8,128)(2,1)S(1)}, u32[]{:S(2)}, u32[]{:S(2)}) collective-permute-start(bf16[2048,128]{1,0:T(8,128)(2,1)S(1)} %collective-permute-done.30.refs_10_), channel_id=1, source_target_pairs={{0,4},{4,0},{1,5},{5,1},{2,6},{6,2},{3,7},{7,3},{8,12},{12,8},{9,1... | collective-permute-start | bytes 1572872 | tf_op jit(solution)/shard_map/ppermute | solution.py:33
  207.5 39.8 %collective-permute-start.34 = (bf16[2048,128]{1,0:T(8,128)(2,1)}, bf16[2048,128]{1,0:T(8,128)(2,1)S(1)}, u32[]{:S(2)}, u32[]{:S(2)}) collective-permute-start(bf16[2048,128]{1,0:T(8,128)(2,1)} %collective-permute-done.33.refs_14_), channel_id=1, source_target_pairs={{0,4},{4,0},{1,5},{5,1},{2,6},{6,2},{3,7},{7,3},{8,12},{12,8},{9,1... | collective-permute-start | bytes 1572872 | tf_op jit(solution)/shard_map/ppermute | solution.py:33
  229.9 14.9 %collective-permute-start.36 = (bf16[512,512]{1,0:T(8,128)(2,1)S(1)}, bf16[512,512]{1,0:T(8,128)(2,1)S(1)}, u32[]{:S(2)}, u32[]{:S(2)}) collective-permute-start(bf16[512,512]{1,0:T(8,128)(2,1)S(1)} %shard_map.77.refs_0_), channel_id=1, source_target_pairs={{0,2},{2,0},{1,3},{3,1},{4,6},{6,4},{5,7},{7,5},{8,10},{10,8},{9,1... | collective-permute-start | bytes 1572872 | tf_op jit(solution)/shard_map/ppermute | solution.py:33
  237.0 44.0 %copy-start.3 = (bf16[2048,128]{1,0:T(8,128)(2,1)S(1)}, bf16[2048,128]{1,0:T(8,128)(2,1)}, u32[]{:S(2)}) copy-start(bf16[2048,128]{1,0:T(8,128)(2,1)} %copy-done.2) | copy-start | bytes 1572868
  237.0 15.2 %collective-permute-start.25 = (bf16[512,512]{1,0:T(8,128)(2,1)S(1)}, bf16[512,512]{1,0:T(8,128)(2,1)S(1)}, u32[]{:S(2)}, u32[]{:S(2)}) collective-permute-start(bf16[512,512]{1,0:T(8,128)(2,1)S(1)} %shard_map.76.refs_0_), channel_id=1, source_target_pairs={{0,8},{8,0},{1,9},{9,1},{2,10},{10,2},{3,11},{11,3},{4,12},{12,4},... | collective-permute-start | bytes 1572872 | tf_op jit(solution)/shard_map/ppermute | solution.py:33
  239.4 35.1 %copy-start.25 = (bf16[2048,128]{1,0:T(8,128)(2,1)}, bf16[2048,128]{1,0:T(8,128)(2,1)S(1)}, u32[]{:S(2)}) copy-start(bf16[2048,128]{1,0:T(8,128)(2,1)S(1)} %collective-permute-done.32.refs_13_) | copy-start | bytes 1572868
  239.4 16.6 %collective-permute-start.23 = (bf16[512,512]{1,0:T(8,128)(2,1)S(1)}, bf16[512,512]{1,0:T(8,128)(2,1)S(1)}, u32[]{:S(2)}, u32[]{:S(2)}) collective-permute-start(bf16[512,512]{1,0:T(8,128)(2,1)S(1)} %shard_map.76.refs_0_), channel_id=1, source_target_pairs={{0,2},{2,0},{1,3},{3,1},{4,6},{6,4},{5,7},{7,5},{8,10},{10,8},{9,1... | collective-permute-start | bytes 1572872 | tf_op jit(solution)/shard_map/ppermute | solution.py:33
  240.6 33.8 %copy-start.26 = (bf16[2048,128]{1,0:T(8,128)(2,1)}, bf16[2048,128]{1,0:T(8,128)(2,1)S(1)}, u32[]{:S(2)}) copy-start(bf16[2048,128]{1,0:T(8,128)(2,1)S(1)} %collective-permute-done.31.refs_11_) | copy-start | bytes 1572868
  240.6 22.7 %collective-permute-start.38 = (bf16[512,512]{1,0:T(8,128)(2,1)S(1)}, bf16[512,512]{1,0:T(8,128)(2,1)S(1)}, u32[]{:S(2)}, u32[]{:S(2)}) collective-permute-start(bf16[512,512]{1,0:T(8,128)(2,1)S(1)} %shard_map.77.refs_0_), channel_id=1, source_target_pairs={{0,8},{8,0},{1,9},{9,1},{2,10},{10,2},{3,11},{11,3},{4,12},{12,4},... | collective-permute-start | bytes 1572872 | tf_op jit(solution)/shard_map/ppermute | solution.py:33
  244.8 27.8 %collective-permute-start.40 = (bf16[512,512]{1,0:T(8,128)(2,1)S(1)}, bf16[512,512]{1,0:T(8,128)(2,1)S(1)}, u32[]{:S(2)}, u32[]{:S(2)}) collective-permute-start(bf16[512,512]{1,0:T(8,128)(2,1)S(1)} %collective-permute-done.36.refs_2_), channel_id=1, source_target_pairs={{0,8},{8,0},{1,9},{9,1},{2,10},{10,2},{3,11},{11,3},{4,12},{12,4},... | collective-permute-start | bytes 1572872 | tf_op jit(solution)/shard_map/ppermute | solution.py:33
  247.2 27.2 %copy-start.27 = (bf16[2048,128]{1,0:T(8,128)(2,1)}, bf16[2048,128]{1,0:T(8,128)(2,1)S(1)}, u32[]{:S(2)}) copy-start(bf16[2048,128]{1,0:T(8,128)(2,1)S(1)} %collective-permute-done.34.refs_15_) | copy-start | bytes 1572868
  247.2 25.3 %collective-permute-start.35 = (bf16[512,512]{1,0:T(8,128)(2,1)S(1)}, bf16[512,512]{1,0:T(8,128)(2,1)S(1)}, u32[]{:S(2)}, u32[]{:S(2)}) collective-permute-start(bf16[512,512]{1,0:T(8,128)(2,1)S(1)} %shard_map.77.refs_0_), channel_id=1, source_target_pairs={{0,1},{1,0},{2,3},{3,2},{4,5},{5,4},{6,7},{7,6},{8,9},{9,8},{10,11... | collective-permute-start | bytes 1572872 | tf_op jit(solution)/shard_map/ppermute | solution.py:33
  252.1 20.9 %collective-permute-start.27 = (bf16[512,512]{1,0:T(8,128)(2,1)S(1)}, bf16[512,512]{1,0:T(8,128)(2,1)S(1)}, u32[]{:S(2)}, u32[]{:S(2)}) collective-permute-start(bf16[512,512]{1,0:T(8,128)(2,1)S(1)} %collective-permute-done.25.refs_4_), channel_id=1, source_target_pairs={{0,2},{2,0},{1,3},{3,1},{4,6},{6,4},{5,7},{7,5},{8,10},{10,8},{9,1... | collective-permute-start | bytes 1572872 | tf_op jit(solution)/shard_map/ppermute | solution.py:33
  256.0 17.1 %collective-permute-start.37 = (bf16[512,512]{1,0:T(8,128)(2,1)S(1)}, bf16[512,512]{1,0:T(8,128)(2,1)S(1)}, u32[]{:S(2)}, u32[]{:S(2)}) collective-permute-start(bf16[512,512]{1,0:T(8,128)(2,1)S(1)} %collective-permute-done.36.refs_2_), channel_id=1, source_target_pairs={{0,1},{1,0},{2,3},{3,2},{4,5},{5,4},{6,7},{7,6},{8,9},{9,8},{10,11... | collective-permute-start | bytes 1572872 | tf_op jit(solution)/shard_map/ppermute | solution.py:33
  263.4 10.2 %collective-permute-start.39 = (bf16[512,512]{1,0:T(8,128)(2,1)S(1)}, bf16[512,512]{1,0:T(8,128)(2,1)S(1)}, u32[]{:S(2)}, u32[]{:S(2)}) collective-permute-start(bf16[512,512]{1,0:T(8,128)(2,1)S(1)} %collective-permute-done.38.refs_4_), channel_id=1, source_target_pairs={{0,1},{1,0},{2,3},{3,2},{4,5},{5,4},{6,7},{7,6},{8,9},{9,8},{10,11... | collective-permute-start | bytes 1572872 | tf_op jit(solution)/shard_map/ppermute | solution.py:33
  272.5 1.9 collective-permute-start.41
  272.5 8.4 %collective-permute-start.22 = (bf16[512,512]{1,0:T(8,128)(2,1)S(1)}, bf16[512,512]{1,0:T(8,128)(2,1)S(1)}, u32[]{:S(2)}, u32[]{:S(2)}) collective-permute-start(bf16[512,512]{1,0:T(8,128)(2,1)S(1)} %shard_map.76.refs_0_), channel_id=1, source_target_pairs={{0,1},{1,0},{2,3},{3,2},{4,5},{5,4},{6,7},{7,6},{8,9},{9,8},{10,11... | collective-permute-start | bytes 1572872 | tf_op jit(solution)/shard_map/ppermute | solution.py:33
  273.1 7.9 %collective-permute-start.26 = (bf16[512,512]{1,0:T(8,128)(2,1)S(1)}, bf16[512,512]{1,0:T(8,128)(2,1)S(1)}, u32[]{:S(2)}, u32[]{:S(2)}) collective-permute-start(bf16[512,512]{1,0:T(8,128)(2,1)S(1)} %collective-permute-done.25.refs_4_), channel_id=1, source_target_pairs={{0,1},{1,0},{2,3},{3,2},{4,5},{5,4},{6,7},{7,6},{8,9},{9,8},{10,11... | collective-permute-start | bytes 1572872 | tf_op jit(solution)/shard_map/ppermute | solution.py:33
  273.1 7.8 %collective-permute-start.24 = (bf16[512,512]{1,0:T(8,128)(2,1)S(1)}, bf16[512,512]{1,0:T(8,128)(2,1)S(1)}, u32[]{:S(2)}, u32[]{:S(2)}) collective-permute-start(bf16[512,512]{1,0:T(8,128)(2,1)S(1)} %collective-permute-done.23.refs_2_), channel_id=1, source_target_pairs={{0,1},{1,0},{2,3},{3,2},{4,5},{5,4},{6,7},{7,6},{8,9},{9,8},{10,11... | collective-permute-start | bytes 1572872 | tf_op jit(solution)/shard_map/ppermute | solution.py:33
  273.6 7.4 %collective-permute-start.28 = (bf16[512,512]{1,0:T(8,128)(2,1)S(1)}, bf16[512,512]{1,0:T(8,128)(2,1)S(1)}, u32[]{:S(2)}, u32[]{:S(2)}) collective-permute-start(bf16[512,512]{1,0:T(8,128)(2,1)S(1)} %collective-permute-done.27.refs_6_), channel_id=1, source_target_pairs={{0,1},{1,0},{2,3},{3,2},{4,5},{5,4},{6,7},{7,6},{8,9},{9,8},{10,11... | collective-permute-start | bytes 1572872 | tf_op jit(solution)/shard_map/ppermute | solution.py:33
  (12 other events, 13.2 us)

commit v3 on v2

--- a/solution.py
+++ b/solution.py
@@ -31,10 +31,6 @@
 
 def swap(value, axis):
     return lax.ppermute(value, axis, SWAP)
-
-
-def after(value, *others):
-    return lax.optimization_barrier((value, *others))[0]
 
 
 def quad_gather(block, by_z_first):
@@ -68,6 +64,17 @@
 
 def aligned(value, step):
     return pl.multiple_of(value, step)
+
+
+def layout_kernel(wk_ref, wv_ref, doc_ref, out_ref):
+    for j in range(8):
+        out_ref[j, :128, :128] = wk_ref[:, 128 * j : 128 * j + 128]
+        out_ref[j, :128, 128:] = wv_ref[:, 128 * j : 128 * j + 128]
+    below = doc_ref[...] < lax.broadcasted_iota(jnp.int32, (EXTRA, 128), 0)
+    count = jnp.sum(jnp.where(below, 1.0, 0.0), axis=1, keepdims=True)
+    rows = jnp.broadcast_to(count, (EXTRA, 256)).astype(jnp.bfloat16)
+    for j in range(8):
+        out_ref[j, 128:, :] = rows
 
 
 TOKEN_PIECES = [
@@ -191,12 +198,12 @@
     return jnp.concatenate([q_ref[:, 128 * h : 128 * h + 128] for h in range(4)], axis=0)
 
 
-def near_kernel(where, tile_lo, tile_hi, q_ref, start_ref, kv_own, kv_y, *refs):
+def near_kernel(half, where, tile_lo, tile_hi, q_ref, start_ref, kv_own, kv_y, *refs):
     top, total, acc, ks, vs, sems = refs
     zh, y = where[0], where[2]
-    tile = pl.program_id(0)
-
-    @pl.when(tile == 0)
+    tile = 2 * half + pl.program_id(0)
+
+    @pl.when(pl.program_id(0) == 0)
     def _():
         copy_keys((kv_own, kv_y), y, ks, vs, sems)
 
@@ -310,17 +317,19 @@
     zh, zl, y, x, c = place = [lax.axis_index(axis) for axis in AXES]
     where = jnp.stack(place).astype(jnp.int32)
 
-    below = jnp.sum(
-        doc_ids[:, None] < lax.broadcasted_iota(jnp.int32, (1, 256), 1), axis=0, dtype=jnp.int32
-    ).astype(bf16)
-    wkv = jnp.concatenate([wk.reshape(128, 8, 128), wv.reshape(128, 8, 128)], axis=2)
-    wkv = jnp.concatenate([wkv, jnp.broadcast_to(below, (EXTRA, 8, 256))], axis=0)
-    wkv = lax.all_to_all(jnp.transpose(wkv, (1, 0, 2)), QUAD, 0, 0, tiled=True)
+    wkv = call(
+        layout_kernel,
+        jax.ShapeDtypeStruct((8, 128 + EXTRA, 256), bf16),
+        [VMEM] * 3,
+        [],
+        (128 * EXTRA, 1 << 20),
+    )(wk, wv, doc_ids.reshape(1, 128))
+    wkv = lax.all_to_all(wkv, QUAD, 0, 0, tiled=True)
     wkv_z = swap(wkv, "zh")
     wkvs = [wkv, swap(wkv, "y"), wkv_z, swap(wkv_z, "y")]
 
     wqs = jnp.transpose(wq.reshape(128, 8, 512), (1, 0, 2))
-    wqs = lax.all_to_all(after(wqs, wkv), QUAD, 0, 0, tiled=True).reshape(1024, 512)
+    wqs = lax.all_to_all(wqs, QUAD, 0, 0, tiled=True).reshape(1024, 512)
     wq_z0 = swap(wqs[:512], "zh")
     wq_z1 = swap(wqs[512:], "zh")
     wq_y = swap(wqs, "y")
@@ -330,7 +339,6 @@
     source = tokens.astype(f32)
     mean_sq = jnp.mean(source * source, axis=1, keepdims=True)
     normed = (source * lax.rsqrt(mean_sq + 1e-05) * norm_gain[None, :]).astype(bf16)
-    normed = after(normed, wqs)
     tok_z = [swap(normed[64 * i : 64 * i + 64], "zl") for i in range(2)]
     tok_far = [swap(tok_z[i], "x") for i in range(2)]
     tok = []
@@ -345,7 +353,7 @@
     cosine = jnp.concatenate([cosine, cosine], axis=1)
     sine = jnp.concatenate([-sine, sine], axis=1)
 
-    counts = jnp.concatenate([piece[:, 128, :DOCS] for piece in wkvs], axis=0)
+    counts = jnp.concatenate([piece[:, 128 : 128 + DOCS, 0] for piece in wkvs], axis=0)
     starts = jnp.sum(counts.astype(f32), axis=0).astype(jnp.int32)
     query_start = jnp.max(
         jnp.where(positions[:, None] >= starts[None, :], starts[None, :], 0), axis=1
@@ -384,29 +392,33 @@
     def tile_spec(shape, first):
         return pl.BlockSpec(shape, lambda i: (i + first,) + (0,) * (len(shape) - 1))
 
-    def state_specs(first):
-        return [tile_spec((1, 4 * QT, 128), first)] * 3
-
-    state = call(
-        near_kernel,
-        [jax.ShapeDtypeStruct((4, 4 * QT, 128), f32)] * 3,
-        [SMEM, SMEM, SMEM, tile_spec((QT, 512), 0), tile_spec((QT, 128), 0), ANY, ANY],
-        [
-            pltpu.VMEM((2048, 128), bf16),
-            pltpu.VMEM((2048, 128), bf16),
-            pltpu.SemaphoreType.DMA((8,)),
-        ],
-        (4 * 1024 * 2048 * 512, 8 << 20),
-        grid=(4,),
-        out_specs=state_specs(0),
-    )(where, tile_lo, tile_hi, queries, start_col, keys_values, kv_y)
+    def state_specs():
+        return [tile_spec((1, 4 * QT, 128), 0)] * 3
+
+    def near_half(half):
+        return call(
+            functools.partial(near_kernel, half),
+            [jax.ShapeDtypeStruct((2, 4 * QT, 128), f32)] * 3,
+            [SMEM] * 3
+            + [tile_spec((QT, 512), 2 * half), tile_spec((QT, 128), 2 * half), ANY, ANY],
+            [
+                pltpu.VMEM((2048, 128), bf16),
+                pltpu.VMEM((2048, 128), bf16),
+                pltpu.SemaphoreType.DMA((8,)),
+            ],
+            (4 * 512 * 2048 * 512, 4 << 20),
+            grid=(2,),
+            out_specs=state_specs(),
+        )(where, tile_lo, tile_hi, queries, start_col, keys_values, kv_y)
+
+    state = [near_half(0), near_half(1)]
 
     def far_call(half):
         return call(
             functools.partial(far_kernel, half),
             jax.ShapeDtypeStruct((512, 512), bf16),
             [SMEM, SMEM, SMEM, tile_spec((QT, 512), 2 * half), tile_spec((QT, 128), 2 * half)]
-            + [ANY, ANY] + state_specs(2 * half),
+            + [ANY, ANY] + state_specs(),
             [
                 pltpu.VMEM((2048, 128), bf16),
                 pltpu.VMEM((2048, 128), bf16),
@@ -418,7 +430,7 @@
             (4 * 512 * 2048 * 512, 8 << 20),
             grid=(2,),
             out_specs=pl.BlockSpec((QT, 512), lambda i: (i, 0)),
-        )(where, tile_lo, tile_hi, queries, start_col, kv_z, kv_zy, *state)
+        )(where, tile_lo, tile_hi, queries, start_col, kv_z, kv_zy, *state[half])
 
     attended = [far_call(0), far_call(1)]
 

time: 309 us -> 312 us (level)
  Pallas kernels: 59.1 us -> 63.3 us
    all_to_all x2, waiting for transfers between devices: 8.42 us -> 5.2 us  [the longest x1 5.2 us: split_body(): wkv = lax.all_to_all(wkv, QUAD, 0, 0, tiled=True)]
    pallas_call x1 -> x3, Pallas kernels: 9.94 us -> 12.1 us  [the longest x2 11.2 us: near_half(): call(functools.partial(near_kernel, half), [jax.ShapeDtypeStruct((2, 4 *...]
    unnamed x66 -> x72, local copies, waits for them, and re-layouts: 12.6 us -> 11.5 us
  transfers between devices with their start and end apart: 44 -> 44, of which waited for: 18 -> 17; matrix products, arithmetic and copies ran while one was open for 4% -> 4% of each run, Pallas kernels for 16% -> 17%
where the time goes in v3:
time: 312 us; the launch traced here: 311 us
  waiting for transfers between devices  152 us (49%)
  Pallas kernels  63.3 us (20%)
  starting transfers between devices  52.9 us (17%)
  local copies, waits for them, and re-layouts  19.9 us (6%)
  blocking collectives  18.1 us (6%)
  other arithmetic  4.16 us (1%)
    ppermute x42, waiting for transfers between devices, swap(): return lax.ppermute(value, axis, SWAP)  147 us
    ppermute x42, starting transfers between devices, swap(): return lax.ppermute(value, axis, SWAP)  44.7 us
    all_to_all x1, blocking collectives, split_body(): home = lax.all_to_all(sent.reshape(8, 128, 512), QUAD, 0, 0, tiled=True)  18.1 us
    pallas_call x2, Pallas kernels, far_call(): call(functools.partial(far_kernel, half), jax.ShapeDtypeStruct((512, 512)...  16.9 us
    pallas_call x2, Pallas kernels, output_call(): call(functools.partial(output_kernel, bool(first)), jax.ShapeDtypeStruct(...  12.8 us
    unnamed x72, local copies, waits for them, and re-layouts  11.5 us
    pallas_call x2, Pallas kernels, near_half(): call(functools.partial(near_kernel, half), [jax.ShapeDtypeStruct((2, 4 *...  11.2 us
    pallas_call x1, Pallas kernels, split_body(): call(project_q_kernel, jax.ShapeDtypeStruct((1024, 512), bf16), [SMEM] +...  10.9 us
  transfers between devices with their start and end apart: 44, of which 17 were waited for; matrix products, arithmetic and copies ran while one was open for 4% of the time, Pallas kernels for 17%

profile of v3, /device:TPU:16, one launch (start us, length us, event | category | flops | bytes accessed | tf_op | source)
XLA Modules:
  0.0 310.6 jit_solution(12459463168801133288)
XLA Ops:
  0.0 0.9 copy-done.22
  1.0 0.9 copy-done.23
  2.6 0.9 shard_map.73
  3.5 3.9 %all-to-all-start = ((bf16[8,144,256]{2,1,0:T(8,128)(2,1)}), bf16[8,144,256]{2,1,0:T(8,128)(2,1)S(1)}, u32[]{:S(2)}, u32[]{:S(2)}) async-start(bf16[8,144,256]{2,1,0:T(8,128)(2,1)} %shard_map.73), calls=%async_computation | async-start | bytes 1179648 | tf_op jit(solution)/shard_map/all_to_all | solution.py:327
  7.7 1.3 fusion.2.refs_0_
  9.5 1.6 collective-permute-start.4
  11.2 1.1 copy.26
  12.3 5.2 %all-to-all-done.refs_12_ = bf16[8,144,256]{2,1,0:T(8,128)(2,1)S(1)} async-done(((bf16[8,144,256]{2,1,0:T(8,128)(2,1)}), bf16[8,144,256]{2,1,0:T(8,128)(2,1)S(1)}, u32[]{:S(2)}, u32[]{:S(2)}) %all-to-all-start) | async-done | bytes 589856 | tf_op jit(solution)/shard_map/all_to_all | solution.py:327
  17.5 4.3 %all-to-all-start.1 = ((bf16[8,128,512]{2,1,0:T(8,128)(2,1)}), bf16[8,128,512]{2,1,0:T(8,128)(2,1)}, u32[]{:S(2)}, u32[]{:S(2)}) async-start(bf16[8,128,512]{2,1,0:T(8,128)(2,1)} %bitcast.20), calls=%async_computation.1 | async-start | bytes 2097152 | tf_op jit(solution)/shard_map/all_to_all | solution.py:332
  21.7 1.3 fusion.18
  23.0 2.0 collective-permute-start.6
  25.1 22.8 %collective-permute-done.6.refs_4_ = bf16[64,4096]{1,0:T(8,128)(2,1)S(1)} collective-permute-done((bf16[64,4096]{1,0:T(8,128)(2,1)S(1)}, bf16[64,4096]{1,0:T(8,128)(2,1)S(1)}, u32[]{:S(2)}, u32[]{:S(2)}) %collective-permute-start.6) | collective-permute-done | bytes 524320 | tf_op jit(solution)/shard_map/ppermute | solution.py:33
  47.9 10.7 %collective-permute-done.8.refs_6_ = bf16[64,4096]{1,0:T(8,128)(2,1)S(1)} collective-permute-done((bf16[64,4096]{1,0:T(8,128)(2,1)S(1)}, bf16[64,4096]{1,0:T(8,128)(2,1)S(1)}, u32[]{:S(2)}, u32[]{:S(2)}) %collective-permute-start.8) | collective-permute-done | bytes 524320 | tf_op jit(solution)/shard_map/ppermute | solution.py:33
  58.6 1.5 collective-permute-start.10
  61.0 0.8 copy-done.10
  61.8 0.8 copy-done.13
  62.6 1.5 collective-permute-start
  64.1 9.2 %collective-permute-done.10.refs_8_ = bf16[64,4096]{1,0:T(8,128)(2,1)S(1)} collective-permute-done((bf16[64,4096]{1,0:T(8,128)(2,1)S(1)}, bf16[64,4096]{1,0:T(8,128)(2,1)S(1)}, u32[]{:S(2)}, u32[]{:S(2)}) %collective-permute-start.10) | collective-permute-done | bytes 524320 | tf_op jit(solution)/shard_map/ppermute | solution.py:33
  73.4 10.8 %collective-permute-done.12.refs_10_ = bf16[64,4096]{1,0:T(8,128)(2,1)S(1)} collective-permute-done((bf16[64,4096]{1,0:T(8,128)(2,1)S(1)}, bf16[64,4096]{1,0:T(8,128)(2,1)S(1)}, u32[]{:S(2)}, u32[]{:S(2)}) %collective-permute-start.12) | collective-permute-done | bytes 524320 | tf_op jit(solution)/shard_map/ppermute | solution.py:33
  84.3 2.1 collective-permute-done.1.refs_14_
  86.4 1.5 collective-permute-start.2
  87.9 1.3 fusion.17
  89.8 3.4 %collective-permute-start.15 = (bf16[512,512]{1,0:T(8,128)(2,1)S(1)}, bf16[512,512]{1,0:T(8,128)(2,1)}, u32[]{:S(2)}, u32[]{:S(2)}) collective-permute-start(bf16[512,512]{1,0:T(8,128)(2,1)S(1)} %bitcast.25), channel_id=1, source_target_pairs={{0,16},{16,0},{1,17},{17,1},{2,18},{18,2},{3,19},{19,3},{4,20},{20... | collective-permute-start | bytes 1572872 | tf_op jit(solution)/shard_map/ppermute | solution.py:33
  93.3 1.9 fusion.3
  95.6 7.3 %collective-permute-done.2.refs_15_ = bf16[8,144,256]{2,1,0:T(8,128)(2,1)} collective-permute-done((bf16[8,144,256]{2,1,0:T(8,128)(2,1)}, bf16[8,144,256]{2,1,0:T(8,128)(2,1)}, u32[]{:S(2)}, u32[]{:S(2)}) %collective-permute-start.2) | collective-permute-done | bytes 589856 | tf_op jit(solution)/shard_map/ppermute | solution.py:33
  103.0 9.4 %shard_map.75.kv_own = bf16[1024,256]{1,0:T(8,128)(2,1)} custom-call(s32[5]{0:T(128)S(1)} %stack.23.where, bf16[128,4096]{1,0:T(8,128)(2,1)} %fusion.2.refs_0_, bf16[128,4096]{1,0:T(8,128)(2,1)} %collective-permute-done.3.refs_1_, bf16[128,4096]{1,0:T(8,128)(2,1)} %collective-permute-done.4.refs_2_, bf16[128,4096]{1,0:T(8,128)(2,1)} %collective-permute-done.5.refs_3_, ...), custom_call_target="tpu_custom_call" | custom-call | flops 2147483648 | bytes 11534336 | tf_op jit(solution)/shard_map/pallas_call | solution.py:365
  112.4 3.4 %collective-permute-start.19 = (bf16[1024,256]{1,0:T(8,128)(2,1)}, bf16[1024,256]{1,0:T(8,128)(2,1)}, u32[]{:S(2)}, u32[]{:S(2)}) collective-permute-start(bf16[1024,256]{1,0:T(8,128)(2,1)} %shard_map.75.kv_own), channel_id=1, source_target_pairs={{0,16},{16,0},{1,17},{17,1},{2,18},{18,2},{3,19},{19,3},{4,20},{20... | collective-permute-start | bytes 1572872 | tf_op jit(solution)/shard_map/ppermute | solution.py:33
  115.8 21.0 %collective-permute-done.15.refs_14_ = bf16[512,512]{1,0:T(8,128)(2,1)} collective-permute-done((bf16[512,512]{1,0:T(8,128)(2,1)S(1)}, bf16[512,512]{1,0:T(8,128)(2,1)}, u32[]{:S(2)}, u32[]{:S(2)}) %collective-permute-start.15) | collective-permute-done | bytes 524320 | tf_op jit(solution)/shard_map/ppermute | solution.py:33
  136.8 1.5 collective-permute-start.17
  138.3 9.7 %collective-permute-done.16.refs_15_ = bf16[512,512]{1,0:T(8,128)(2,1)} collective-permute-done((bf16[512,512]{1,0:T(8,128)(2,1)S(1)}, bf16[512,512]{1,0:T(8,128)(2,1)}, u32[]{:S(2)}, u32[]{:S(2)}) %collective-permute-start.16) | collective-permute-done | bytes 524320 | tf_op jit(solution)/shard_map/ppermute | solution.py:33
  148.1 1.5 collective-permute-start.18
  149.6 0.9 fusion.16
  150.4 3.5 %collective-permute-start.30 = (bf16[2048,128]{1,0:T(8,128)(2,1)S(1)}, bf16[2048,128]{1,0:T(8,128)(2,1)S(1)}, u32[]{:S(2)}, u32[]{:S(2)}) collective-permute-start(bf16[2048,128]{1,0:T(8,128)(2,1)S(1)} %get-tuple-element.18.refs_8_), channel_id=1, source_target_pairs={{0,16},{16,0},{1,17},{17,1},{2,18},{18,2},{3,19},{19,3},{4,20},{20... | collective-permute-start | bytes 1572872 | tf_op jit(solution)/shard_map/ppermute | solution.py:33
  153.9 16.7 %collective-permute-done.19.kv_z = bf16[1024,256]{1,0:T(8,128)(2,1)} collective-permute-done((bf16[1024,256]{1,0:T(8,128)(2,1)}, bf16[1024,256]{1,0:T(8,128)(2,1)}, u32[]{:S(2)}, u32[]{:S(2)}) %collective-permute-start.19) | collective-permute-done | bytes 524320 | tf_op jit(solution)/shard_map/ppermute | solution.py:33
  170.6 3.4 %collective-permute-start.33 = (bf16[2048,128]{1,0:T(8,128)(2,1)}, bf16[2048,128]{1,0:T(8,128)(2,1)}, u32[]{:S(2)}, u32[]{:S(2)}) collective-permute-start(bf16[2048,128]{1,0:T(8,128)(2,1)} %get-tuple-element.17.refs_12_), channel_id=1, source_target_pairs={{0,16},{16,0},{1,17},{17,1},{2,18},{18,2},{3,19},{19,3},{4,20},{20... | collective-permute-start | bytes 1572872 | tf_op jit(solution)/shard_map/ppermute | solution.py:33
  174.0 1.5 collective-permute-start.21
  179.5 1.0 collective-permute-start.29
  180.5 1.0 collective-permute-start.20
  181.5 1.0 copy-done.12
  182.6 1.0 copy-done.15
  183.6 1.0 copy-done.18
  184.7 1.0 copy-done.21
  185.7 10.9 %shard_map.74.q_ref = bf16[1024,512]{1,0:T(8,128)(2,1)} custom-call(s32[5]{0:T(128)S(1)} %stack.23.where, bf16[128,4096]{1,0:T(8,128)(2,1)} %fusion.2.refs_0_, bf16[128,4096]{1,0:T(8,128)(2,1)} %collective-permute-done.3.refs_1_, bf16[128,4096]{1,0:T(8,128)(2,1)} %collective-permute-done.4.refs_2_, bf16[128,4096]{1,0:T(8,128)(2,1)} %collective-permute-done.5.refs_3_, ...), custom_call_target="tpu_custom_call" | custom-call | flops 4294967296 | bytes 14680064 | tf_op jit(solution)/shard_map/pallas_call | solution.py:376
  196.6 1.1 collective-permute-start.32
  197.7 6.6 %collective-permute-done.33.refs_14_ = bf16[2048,128]{1,0:T(8,128)(2,1)} collective-permute-done((bf16[2048,128]{1,0:T(8,128)(2,1)}, bf16[2048,128]{1,0:T(8,128)(2,1)}, u32[]{:S(2)}, u32[]{:S(2)}) %collective-permute-start.33) | collective-permute-done | bytes 524320 | tf_op jit(solution)/shard_map/ppermute | solution.py:33
  204.2 1.5 collective-permute-start.31
  206.5 1.2 copy-done.25
  207.7 6.7 %shard_map.76 = (f32[2,1024,128]{2,1,0:T(8,128)S(1)}, f32[2,1024,128]{2,1,0:T(8,128)S(1)}, f32[2,1024,128]{2,1,0:T(8,128)S(1)}) custom-call(s32[5]{0:T(128)S(1)} %stack.23.where, s32[4]{0:T(128)S(1)} %slice.46.tile_lo, s32[4]{0:T(128)S(1)} %slice.47.tile_hi, bf16[1024,512]{1,0:T(8,128)(2,1)S(1)} %copy-done.25, s32[1024,128]{1,0:T(8,128)S(1)} %broadcast_in_dim.9.start_ref, ...), custom_call_target="tpu_custom_call" | custom-call | flops 2147483648 | bytes 4194304 | tf_op jit(solution)/shard_map/pallas_call | solution.py:399
  214.4 4.5 %shard_map.78 = (f32[2,1024,128]{2,1,0:T(8,128)S(1)}, f32[2,1024,128]{2,1,0:T(8,128)S(1)}, f32[2,1024,128]{2,1,0:T(8,128)S(1)}) custom-call(s32[5]{0:T(128)S(1)} %stack.23.where, s32[4]{0:T(128)S(1)} %slice.46.tile_lo, s32[4]{0:T(128)S(1)} %slice.47.tile_hi, bf16[1024,512]{1,0:T(8,128)(2,1)S(1)} %copy-done.25, s32[1024,128]{1,0:T(8,128)S(1)} %broadcast_in_dim.9.start_ref, ...), custom_call_target="tpu_custom_call" | custom-call | flops 2147483648 | bytes 4194304 | tf_op jit(solution)/shard_map/pallas_call | solution.py:399
  218.9 1.0 copy-done.27
  219.9 10.2 %shard_map.79.refs_0_ = bf16[512,512]{1,0:T(8,128)(2,1)S(1)} custom-call(s32[5]{0:T(128)S(1)} %stack.23.where, s32[4]{0:T(128)S(1)} %slice.46.tile_lo, s32[4]{0:T(128)S(1)} %slice.47.tile_hi, bf16[1024,512]{1,0:T(8,128)(2,1)S(1)} %copy-done.25, s32[1024,128]{1,0:T(8,128)S(1)} %broadcast_in_dim.9.start_ref, bf16[1024,256]{1,0:T(8,128)(2,1)} %collective-permute-done.19.kv_z, ...), custom_call_target="tpu_custom_call" | custom-call | flops 2147483648 | bytes 8388608 | tf_op jit(solution)/shard_map/pallas_call | solution.py:417
  230.1 1.7 collective-permute-start.36
  231.8 6.8 %shard_map.77.refs_0_ = bf16[512,512]{1,0:T(8,128)(2,1)S(1)} custom-call(s32[5]{0:T(128)S(1)} %stack.23.where, s32[4]{0:T(128)S(1)} %slice.46.tile_lo, s32[4]{0:T(128)S(1)} %slice.47.tile_hi, bf16[1024,512]{1,0:T(8,128)(2,1)S(1)} %copy-done.25, s32[1024,128]{1,0:T(8,128)S(1)} %broadcast_in_dim.9.start_ref, bf16[1024,256]{1,0:T(8,128)(2,1)} %collective-permute-done.19.kv_z, ...), custom_call_target="tpu_custom_call" | custom-call | flops 2147483648 | bytes 8388608 | tf_op jit(solution)/shard_map/pallas_call | solution.py:417
  238.6 3.2 %collective-permute-start.25 = (bf16[512,512]{1,0:T(8,128)(2,1)S(1)}, bf16[512,512]{1,0:T(8,128)(2,1)S(1)}, u32[]{:S(2)}, u32[]{:S(2)}) collective-permute-start(bf16[512,512]{1,0:T(8,128)(2,1)S(1)} %shard_map.77.refs_0_), channel_id=1, source_target_pairs={{0,8},{8,0},{1,9},{9,1},{2,10},{10,2},{3,11},{11,3},{4,12},{12,4},... | collective-permute-start | bytes 1572872 | tf_op jit(solution)/shard_map/ppermute | solution.py:33
  242.3 1.6 collective-permute-done.36.refs_2_
  244.0 4.1 %collective-permute-start.40 = (bf16[512,512]{1,0:T(8,128)(2,1)S(1)}, bf16[512,512]{1,0:T(8,128)(2,1)S(1)}, u32[]{:S(2)}, u32[]{:S(2)}) collective-permute-start(bf16[512,512]{1,0:T(8,128)(2,1)S(1)} %collective-permute-done.36.refs_2_), channel_id=1, source_target_pairs={{0,8},{8,0},{1,9},{9,1},{2,10},{10,2},{3,11},{11,3},{4,12},{12,4},... | collective-permute-start | bytes 1572872 | tf_op jit(solution)/shard_map/ppermute | solution.py:33
  248.1 6.5 %collective-permute-done.25.refs_4_ = bf16[512,512]{1,0:T(8,128)(2,1)S(1)} collective-permute-done((bf16[512,512]{1,0:T(8,128)(2,1)S(1)}, bf16[512,512]{1,0:T(8,128)(2,1)S(1)}, u32[]{:S(2)}, u32[]{:S(2)}) %collective-permute-start.25) | collective-permute-done | bytes 524320 | tf_op jit(solution)/shard_map/ppermute | solution.py:33
  255.2 10.7 %collective-permute-done.38.refs_4_ = bf16[512,512]{1,0:T(8,128)(2,1)S(1)} collective-permute-done((bf16[512,512]{1,0:T(8,128)(2,1)S(1)}, bf16[512,512]{1,0:T(8,128)(2,1)S(1)}, u32[]{:S(2)}, u32[]{:S(2)}) %collective-permute-start.38) | collective-permute-done | bytes 524320 | tf_op jit(solution)/shard_map/ppermute | solution.py:33
  265.8 9.7 %collective-permute-done.40.refs_6_ = bf16[512,512]{1,0:T(8,128)(2,1)S(1)} collective-permute-done((bf16[512,512]{1,0:T(8,128)(2,1)S(1)}, bf16[512,512]{1,0:T(8,128)(2,1)S(1)}, u32[]{:S(2)}, u32[]{:S(2)}) %collective-permute-start.40) | collective-permute-done | bytes 524320 | tf_op jit(solution)/shard_map/ppermute | solution.py:33
  277.5 5.7 %shard_map.80.refs_16_ = bf16[512,512]{1,0:T(8,128)(2,1)S(1)} custom-call(s32[5]{0:T(128)S(1)} %stack.23.where, bf16[512,512]{1,0:T(8,128)(2,1)S(1)} %shard_map.79.refs_0_, bf16[512,512]{1,0:T(8,128)(2,1)S(1)} %collective-permute-done.35.refs_1_, bf16[512,512]{1,0:T(8,128)(2,1)S(1)} %collective-permute-done.36.refs_2_, ...), custom_call_target="tpu_custom_call" | custom-call | flops 2147483648 | bytes 9437184 | tf_op jit(solution)/shard_map/pallas_call | solution.py:449
  283.2 0.8 copy-done.5
  284.0 7.1 %shard_map.81 = bf16[1024,512]{1,0:T(8,128)(2,1)} custom-call(s32[5]{0:T(128)S(1)} %stack.23.where, bf16[512,512]{1,0:T(8,128)(2,1)S(1)} %shard_map.77.refs_0_, bf16[512,512]{1,0:T(8,128)(2,1)S(1)} %collective-permute-done.22.refs_1_, bf16[512,512]{1,0:T(8,128)(2,1)S(1)} %collective-permute-done.23.refs_2_, ...), custom_call_target="tpu_custom_call" | custom-call | flops 2147483648 | bytes 9437184 | tf_op jit(solution)/shard_map/pallas_call | solution.py:449
  291.1 18.1 %all_to_all.15.sent_ref = bf16[8,128,512]{2,1,0:T(8,128)(2,1)S(1)} all-to-all(bf16[8,128,512]{2,1,0:T(8,128)(2,1)} %bitcast.22), channel_id=1, replica_groups=mesh['zh'=2,'zl'=2,'y'=2,'x'=2,'c'=2] {'zl','x','c'}, dimensions={0} | all-to-all | bytes 2097152 | tf_op jit(solution)/shard_map/all_to_all | solution.py:462
  309.2 1.3 shard_map.82
  (134 shorter events, 11.3 us)
Async XLA Ops:
  2.6 4.8 %copy-start = (bf16[128,4096]{1,0:T(8,128)(2,1)S(1)}, bf16[128,4096]{1,0:T(8,128)(2,1)}, u32[]{:S(2)}) copy-start(bf16[128,4096]{1,0:T(8,128)(2,1)} %tok_ref.1) | copy-start | bytes 3145732
  3.5 14.0 %all-to-all-start = ((bf16[8,144,256]{2,1,0:T(8,128)(2,1)}), bf16[8,144,256]{2,1,0:T(8,128)(2,1)S(1)}, u32[]{:S(2)}, u32[]{:S(2)}) async-start(bf16[8,144,256]{2,1,0:T(8,128)(2,1)} %shard_map.73), calls=%async_computation | async-start | bytes 1179648 | tf_op jit(solution)/shard_map/all_to_all | solution.py:327
  9.0 51.0 %collective-permute-start.3 = (bf16[128,4096]{1,0:T(8,128)(2,1)}, bf16[128,4096]{1,0:T(8,128)(2,1)}, u32[]{:S(2)}, u32[]{:S(2)}) collective-permute-start(bf16[128,4096]{1,0:T(8,128)(2,1)} %fusion.2.refs_0_), channel_id=1, source_target_pairs={{0,1},{1,0},{2,3},{3,2},{4,5},{5,4},{6,7},{7,6},{8,9},{9,8},{10,11... | collective-permute-start | bytes 3145736 | tf_op jit(solution)/shard_map/ppermute | solution.py:33
  9.5 51.1 %collective-permute-start.4 = (bf16[128,4096]{1,0:T(8,128)(2,1)}, bf16[128,4096]{1,0:T(8,128)(2,1)}, u32[]{:S(2)}, u32[]{:S(2)}) collective-permute-start(bf16[128,4096]{1,0:T(8,128)(2,1)} %fusion.2.refs_0_), channel_id=1, source_target_pairs={{0,2},{2,0},{1,3},{3,1},{4,6},{6,4},{5,7},{7,5},{8,10},{10,8},{9,1... | collective-permute-start | bytes 3145736 | tf_op jit(solution)/shard_map/ppermute | solution.py:33
  17.5 5.5 %copy-start.28 = (bf16[8,144,256]{2,1,0:T(8,128)(2,1)}, bf16[8,144,256]{2,1,0:T(8,128)(2,1)S(1)}, u32[]{:S(2)}) copy-start(bf16[8,144,256]{2,1,0:T(8,128)(2,1)S(1)} %all-to-all-done.refs_12_) | copy-start | bytes 1769476
  17.5 70.5 %all-to-all-start.1 = ((bf16[8,128,512]{2,1,0:T(8,128)(2,1)}), bf16[8,128,512]{2,1,0:T(8,128)(2,1)}, u32[]{:S(2)}, u32[]{:S(2)}) async-start(bf16[8,128,512]{2,1,0:T(8,128)(2,1)} %bitcast.20), calls=%async_computation.1 | async-start | bytes 2097152 | tf_op jit(solution)/shard_map/all_to_all | solution.py:332
  23.0 24.9 %collective-permute-start.6 = (bf16[64,4096]{1,0:T(8,128)(2,1)S(1)}, bf16[64,4096]{1,0:T(8,128)(2,1)S(1)}, u32[]{:S(2)}, u32[]{:S(2)}) collective-permute-start(bf16[64,4096]{1,0:T(8,128)(2,1)S(1)} %get-tuple-element.22), channel_id=1, source_target_pairs={{0,8},{8,0},{1,9},{9,1},{2,10},{10,2},{3,11},{11,3},{4,12},{12,4},... | collective-permute-start | bytes 1572872 | tf_op jit(solution)/shard_map/ppermute | solution.py:33
  25.0 33.6 %collective-permute-start.8 = (bf16[64,4096]{1,0:T(8,128)(2,1)S(1)}, bf16[64,4096]{1,0:T(8,128)(2,1)S(1)}, u32[]{:S(2)}, u32[]{:S(2)}) collective-permute-start(bf16[64,4096]{1,0:T(8,128)(2,1)S(1)} %get-tuple-element.21), channel_id=1, source_target_pairs={{0,8},{8,0},{1,9},{9,1},{2,10},{10,2},{3,11},{11,3},{4,12},{12,4},... | collective-permute-start | bytes 1572872 | tf_op jit(solution)/shard_map/ppermute | solution.py:33
  47.9 55.0 %copy-start.6 = (bf16[64,4096]{1,0:T(8,128)(2,1)}, bf16[64,4096]{1,0:T(8,128)(2,1)S(1)}, u32[]{:S(2)}) copy-start(bf16[64,4096]{1,0:T(8,128)(2,1)S(1)} %collective-permute-done.6.refs_4_) | copy-start | bytes 1572868
  47.9 13.0 %collective-permute-start.7 = (bf16[64,4096]{1,0:T(8,128)(2,1)S(1)}, bf16[64,4096]{1,0:T(8,128)(2,1)S(1)}, u32[]{:S(2)}, u32[]{:S(2)}) collective-permute-start(bf16[64,4096]{1,0:T(8,128)(2,1)S(1)} %collective-permute-done.6.refs_4_), channel_id=1, source_target_pairs={{0,1},{1,0},{2,3},{3,2},{4,5},{5,4},{6,7},{7,6},{8,9},{9,8},{10,11... | collective-permute-start | bytes 1572872 | tf_op jit(solution)/shard_map/ppermute | solution.py:33
  58.6 44.4 %copy-start.8 = (bf16[64,4096]{1,0:T(8,128)(2,1)}, bf16[64,4096]{1,0:T(8,128)(2,1)S(1)}, u32[]{:S(2)}) copy-start(bf16[64,4096]{1,0:T(8,128)(2,1)S(1)} %collective-permute-done.8.refs_6_) | copy-start | bytes 1572868
  58.6 3.2 %collective-permute-start.9 = (bf16[64,4096]{1,0:T(8,128)(2,1)S(1)}, bf16[64,4096]{1,0:T(8,128)(2,1)S(1)}, u32[]{:S(2)}, u32[]{:S(2)}) collective-permute-start(bf16[64,4096]{1,0:T(8,128)(2,1)S(1)} %collective-permute-done.8.refs_6_), channel_id=1, source_target_pairs={{0,1},{1,0},{2,3},{3,2},{4,5},{5,4},{6,7},{7,6},{8,9},{9,8},{10,11... | collective-permute-start | bytes 1572872 | tf_op jit(solution)/shard_map/ppermute | solution.py:33
  58.6 14.8 %collective-permute-start.10 = (bf16[64,4096]{1,0:T(8,128)(2,1)S(1)}, bf16[64,4096]{1,0:T(8,128)(2,1)S(1)}, u32[]{:S(2)}, u32[]{:S(2)}) collective-permute-start(bf16[64,4096]{1,0:T(8,128)(2,1)S(1)} %collective-permute-done.6.refs_4_), channel_id=1, source_target_pairs={{0,2},{2,0},{1,3},{3,1},{4,6},{6,4},{5,7},{7,5},{8,10},{10,8},{9,1... | collective-permute-start | bytes 1572872 | tf_op jit(solution)/shard_map/ppermute | solution.py:33
  60.1 24.1 %collective-permute-start.12 = (bf16[64,4096]{1,0:T(8,128)(2,1)S(1)}, bf16[64,4096]{1,0:T(8,128)(2,1)S(1)}, u32[]{:S(2)}, u32[]{:S(2)}) collective-permute-start(bf16[64,4096]{1,0:T(8,128)(2,1)S(1)} %collective-permute-done.8.refs_6_), channel_id=1, source_target_pairs={{0,2},{2,0},{1,3},{3,1},{4,6},{6,4},{5,7},{7,5},{8,10},{10,8},{9,1... | collective-permute-start | bytes 1572872 | tf_op jit(solution)/shard_map/ppermute | solution.py:33
  60.6 25.8 %collective-permute-start.1 = (bf16[8,144,256]{2,1,0:T(8,128)(2,1)}, bf16[8,144,256]{2,1,0:T(8,128)(2,1)}, u32[]{:S(2)}, u32[]{:S(2)}) collective-permute-start(bf16[8,144,256]{2,1,0:T(8,128)(2,1)} %copy-done.28), channel_id=1, source_target_pairs={{0,16},{16,0},{1,17},{17,1},{2,18},{18,2},{3,19},{19,3},{4,20},{20... | collective-permute-start | bytes 1769480 | tf_op jit(solution)/shard_map/ppermute | solution.py:33
  61.8 33.8 %collective-permute-start.5 = (bf16[128,4096]{1,0:T(8,128)(2,1)}, bf16[128,4096]{1,0:T(8,128)(2,1)}, u32[]{:S(2)}, u32[]{:S(2)}) collective-permute-start(bf16[128,4096]{1,0:T(8,128)(2,1)} %collective-permute-done.4.refs_2_), channel_id=1, source_target_pairs={{0,1},{1,0},{2,3},{3,2},{4,5},{5,4},{6,7},{7,6},{8,9},{9,8},{10,11... | collective-permute-start | bytes 3145736 | tf_op jit(solution)/shard_map/ppermute | solution.py:33
  62.6 30.6 %collective-permute-start = (bf16[8,144,256]{2,1,0:T(8,128)(2,1)}, bf16[8,144,256]{2,1,0:T(8,128)(2,1)}, u32[]{:S(2)}, u32[]{:S(2)}) collective-permute-start(bf16[8,144,256]{2,1,0:T(8,128)(2,1)} %copy-done.28), channel_id=1, source_target_pairs={{0,4},{4,0},{1,5},{5,1},{2,6},{6,2},{3,7},{7,3},{8,12},{12,8},{9,1... | collective-permute-start | bytes 1769480 | tf_op jit(solution)/shard_map/ppermute | solution.py:33
  73.4 15.8 %copy-start.16 = (bf16[64,4096]{1,0:T(8,128)(2,1)}, bf16[64,4096]{1,0:T(8,128)(2,1)S(1)}, u32[]{:S(2)}) copy-start(bf16[64,4096]{1,0:T(8,128)(2,1)S(1)} %collective-permute-done.10.refs_8_) | copy-start | bytes 1572868
  73.4 15.8 %collective-permute-start.11 = (bf16[64,4096]{1,0:T(8,128)(2,1)S(1)}, bf16[64,4096]{1,0:T(8,128)(2,1)}, u32[]{:S(2)}, u32[]{:S(2)}) collective-permute-start(bf16[64,4096]{1,0:T(8,128)(2,1)S(1)} %collective-permute-done.10.refs_8_), channel_id=1, source_target_pairs={{0,1},{1,0},{2,3},{3,2},{4,5},{5,4},{6,7},{7,6},{8,9},{9,8},{10,11... | collective-permute-start | bytes 1572872 | tf_op jit(solution)/shard_map/ppermute | solution.py:33
  84.2 5.1 %copy-start.19 = (bf16[64,4096]{1,0:T(8,128)(2,1)}, bf16[64,4096]{1,0:T(8,128)(2,1)S(1)}, u32[]{:S(2)}) copy-start(bf16[64,4096]{1,0:T(8,128)(2,1)S(1)} %collective-permute-done.12.refs_10_) | copy-start | bytes 1572868
  84.2 5.7 %collective-permute-start.13 = (bf16[64,4096]{1,0:T(8,128)(2,1)S(1)}, bf16[64,4096]{1,0:T(8,128)(2,1)}, u32[]{:S(2)}, u32[]{:S(2)}) collective-permute-start(bf16[64,4096]{1,0:T(8,128)(2,1)S(1)} %collective-permute-done.12.refs_10_), channel_id=1, source_target_pairs={{0,1},{1,0},{2,3},{3,2},{4,5},{5,4},{6,7},{7,6},{8,9},{9,8},{10,11... | collective-permute-start | bytes 1572872 | tf_op jit(solution)/shard_map/ppermute | solution.py:33
  86.4 16.5 %collective-permute-start.2 = (bf16[8,144,256]{2,1,0:T(8,128)(2,1)}, bf16[8,144,256]{2,1,0:T(8,128)(2,1)}, u32[]{:S(2)}, u32[]{:S(2)}) collective-permute-start(bf16[8,144,256]{2,1,0:T(8,128)(2,1)} %collective-permute-done.1.refs_14_), channel_id=1, source_target_pairs={{0,4},{4,0},{1,5},{5,1},{2,6},{6,2},{3,7},{7,3},{8,12},{12,8},{9,1... | collective-permute-start | bytes 1769480 | tf_op jit(solution)/shard_map/ppermute | solution.py:33
  89.2 84.8 %collective-permute-start.14 = (bf16[1024,512]{1,0:T(8,128)(2,1)}, bf16[1024,512]{1,0:T(8,128)(2,1)S(1)}, u32[]{:S(2)}, u32[]{:S(2)}) collective-permute-start(bf16[1024,512]{1,0:T(8,128)(2,1)} %bitcast.11.refs_12_), channel_id=1, source_target_pairs={{0,4},{4,0},{1,5},{5,1},{2,6},{6,2},{3,7},{7,3},{8,12},{12,8},{9,1... | collective-permute-start | bytes 3145736 | tf_op jit(solution)/shard_map/ppermute | solution.py:33
  89.8 47.0 %collective-permute-start.15 = (bf16[512,512]{1,0:T(8,128)(2,1)S(1)}, bf16[512,512]{1,0:T(8,128)(2,1)}, u32[]{:S(2)}, u32[]{:S(2)}) collective-permute-start(bf16[512,512]{1,0:T(8,128)(2,1)S(1)} %bitcast.25), channel_id=1, source_target_pairs={{0,16},{16,0},{1,17},{17,1},{2,18},{18,2},{3,19},{19,3},{4,20},{20... | collective-permute-start | bytes 1572872 | tf_op jit(solution)/shard_map/ppermute | solution.py:33
  93.2 54.9 %collective-permute-start.16 = (bf16[512,512]{1,0:T(8,128)(2,1)S(1)}, bf16[512,512]{1,0:T(8,128)(2,1)}, u32[]{:S(2)}, u32[]{:S(2)}) collective-permute-start(bf16[512,512]{1,0:T(8,128)(2,1)S(1)} %bitcast.24), channel_id=1, source_target_pairs={{0,16},{16,0},{1,17},{17,1},{2,18},{18,2},{3,19},{19,3},{4,20},{20... | collective-permute-start | bytes 1572872 | tf_op jit(solution)/shard_map/ppermute | solution.py:33
  95.2 7.8 %copy-start.11 = (bf16[64,4096]{1,0:T(8,128)(2,1)S(1)}, bf16[64,4096]{1,0:T(8,128)(2,1)}, u32[]{:S(2)}) copy-start(bf16[64,4096]{1,0:T(8,128)(2,1)} %copy-done.10) | copy-start | bytes 1572868
  95.2 7.8 %copy-start.14 = (bf16[64,4096]{1,0:T(8,128)(2,1)S(1)}, bf16[64,4096]{1,0:T(8,128)(2,1)}, u32[]{:S(2)}) copy-start(bf16[64,4096]{1,0:T(8,128)(2,1)} %copy-done.13) | copy-start | bytes 1572868
  95.2 7.8 %copy-start.17 = (bf16[64,4096]{1,0:T(8,128)(2,1)S(1)}, bf16[64,4096]{1,0:T(8,128)(2,1)}, u32[]{:S(2)}) copy-start(bf16[64,4096]{1,0:T(8,128)(2,1)} %copy-done.16) | copy-start | bytes 1572868
  95.2 7.8 %copy-start.20 = (bf16[64,4096]{1,0:T(8,128)(2,1)S(1)}, bf16[64,4096]{1,0:T(8,128)(2,1)}, u32[]{:S(2)}) copy-start(bf16[64,4096]{1,0:T(8,128)(2,1)} %copy-done.19) | copy-start | bytes 1572868
  95.6 16.8 %copy-start.3 = (f32[1024,128]{1,0:T(8,128)}, f32[1024,128]{1,0:T(8,128)S(1)}, u32[]{:S(2)}) copy-start(f32[1024,128]{1,0:T(8,128)S(1)} %get-tuple-element.26.refs_18_.refs_16_) | copy-start | bytes 1572868
  95.6 16.8 %copy-start.4 = (f32[1024,128]{1,0:T(8,128)}, f32[1024,128]{1,0:T(8,128)S(1)}, u32[]{:S(2)}) copy-start(f32[1024,128]{1,0:T(8,128)S(1)} %get-tuple-element.27.refs_19_.refs_17_) | copy-start | bytes 1572868
  103.0 46.6 %copy-start.33 = (bf16[4096,128]{1,0:T(8,128)(2,1)S(1)}, bf16[4096,128]{1,0:T(8,128)(2,1)}, u32[]{:S(2)}) copy-start(bf16[4096,128]{1,0:T(8,128)(2,1)} %param.12) | copy-start | bytes 3145732
  112.4 58.3 %collective-permute-start.19 = (bf16[1024,256]{1,0:T(8,128)(2,1)}, bf16[1024,256]{1,0:T(8,128)(2,1)}, u32[]{:S(2)}, u32[]{:S(2)}) collective-permute-start(bf16[1024,256]{1,0:T(8,128)(2,1)} %shard_map.75.kv_own), channel_id=1, source_target_pairs={{0,16},{16,0},{1,17},{17,1},{2,18},{18,2},{3,19},{19,3},{4,20},{20... | collective-permute-start | bytes 1572872 | tf_op jit(solution)/shard_map/ppermute | solution.py:33
  115.8 65.7 %copy-start.7 = (bf16[64,4096]{1,0:T(8,128)(2,1)S(1)}, bf16[64,4096]{1,0:T(8,128)(2,1)}, u32[]{:S(2)}) copy-start(bf16[64,4096]{1,0:T(8,128)(2,1)} %copy-done.6) | copy-start | bytes 1572868
  115.8 65.7 %copy-start.9 = (bf16[64,4096]{1,0:T(8,128)(2,1)S(1)}, bf16[64,4096]{1,0:T(8,128)(2,1)}, u32[]{:S(2)}) copy-start(bf16[64,4096]{1,0:T(8,128)(2,1)} %copy-done.8) | copy-start | bytes 1572868
  136.8 42.7 %collective-permute-start.17 = (bf16[512,512]{1,0:T(8,128)(2,1)}, bf16[512,512]{1,0:T(8,128)(2,1)}, u32[]{:S(2)}, u32[]{:S(2)}) collective-permute-start(bf16[512,512]{1,0:T(8,128)(2,1)} %collective-permute-done.15.refs_14_), channel_id=1, source_target_pairs={{0,4},{4,0},{1,5},{5,1},{2,6},{6,2},{3,7},{7,3},{8,12},{12,8},{9,1... | collective-permute-start | bytes 1572872 | tf_op jit(solution)/shard_map/ppermute | solution.py:33
  148.1 32.5 %collective-permute-start.18 = (bf16[512,512]{1,0:T(8,128)(2,1)}, bf16[512,512]{1,0:T(8,128)(2,1)}, u32[]{:S(2)}, u32[]{:S(2)}) collective-permute-start(bf16[512,512]{1,0:T(8,128)(2,1)} %collective-permute-done.16.refs_15_), channel_id=1, source_target_pairs={{0,4},{4,0},{1,5},{5,1},{2,6},{6,2},{3,7},{7,3},{8,12},{12,8},{9,1... | collective-permute-start | bytes 1572872 | tf_op jit(solution)/shard_map/ppermute | solution.py:33
  150.4 46.2 %collective-permute-start.30 = (bf16[2048,128]{1,0:T(8,128)(2,1)S(1)}, bf16[2048,128]{1,0:T(8,128)(2,1)S(1)}, u32[]{:S(2)}, u32[]{:S(2)}) collective-permute-start(bf16[2048,128]{1,0:T(8,128)(2,1)S(1)} %get-tuple-element.18.refs_8_), channel_id=1, source_target_pairs={{0,16},{16,0},{1,17},{17,1},{2,18},{18,2},{3,19},{19,3},{4,20},{20... | collective-permute-start | bytes 1572872 | tf_op jit(solution)/shard_map/ppermute | solution.py:33
  170.6 33.6 %collective-permute-start.33 = (bf16[2048,128]{1,0:T(8,128)(2,1)}, bf16[2048,128]{1,0:T(8,128)(2,1)}, u32[]{:S(2)}, u32[]{:S(2)}) collective-permute-start(bf16[2048,128]{1,0:T(8,128)(2,1)} %get-tuple-element.17.refs_12_), channel_id=1, source_target_pairs={{0,16},{16,0},{1,17},{17,1},{2,18},{18,2},{3,19},{19,3},{4,20},{20... | collective-permute-start | bytes 1572872 | tf_op jit(solution)/shard_map/ppermute | solution.py:33
  174.0 31.8 %collective-permute-start.21 = (bf16[1024,256]{1,0:T(8,128)(2,1)}, bf16[1024,256]{1,0:T(8,128)(2,1)}, u32[]{:S(2)}, u32[]{:S(2)}) collective-permute-start(bf16[1024,256]{1,0:T(8,128)(2,1)} %shard_map.75.kv_own), channel_id=1, source_target_pairs={{0,4},{4,0},{1,5},{5,1},{2,6},{6,2},{3,7},{7,3},{8,12},{12,8},{9,1... | collective-permute-start | bytes 1572872 | tf_op jit(solution)/shard_map/ppermute | solution.py:33
  179.5 59.1 %collective-permute-start.29 = (bf16[2048,128]{1,0:T(8,128)(2,1)S(1)}, bf16[2048,128]{1,0:T(8,128)(2,1)S(1)}, u32[]{:S(2)}, u32[]{:S(2)}) collective-permute-start(bf16[2048,128]{1,0:T(8,128)(2,1)S(1)} %get-tuple-element.18.refs_8_), channel_id=1, source_target_pairs={{0,4},{4,0},{1,5},{5,1},{2,6},{6,2},{3,7},{7,3},{8,12},{12,8},{9,1... | collective-permute-start | bytes 1572872 | tf_op jit(solution)/shard_map/ppermute | solution.py:33
  180.5 39.4 %collective-permute-start.20 = (bf16[1024,256]{1,0:T(8,128)(2,1)}, bf16[1024,256]{1,0:T(8,128)(2,1)S(1)}, u32[]{:S(2)}, u32[]{:S(2)}) collective-permute-start(bf16[1024,256]{1,0:T(8,128)(2,1)} %collective-permute-done.19.kv_z), channel_id=1, source_target_pairs={{0,4},{4,0},{1,5},{5,1},{2,6},{6,2},{3,7},{7,3},{8,12},{12,8},{9,1... | collective-permute-start | bytes 1572872 | tf_op jit(solution)/shard_map/ppermute | solution.py:33
  196.6 17.8 %copy-start.1 = (bf16[2048,128]{1,0:T(8,128)(2,1)}, bf16[2048,128]{1,0:T(8,128)(2,1)S(1)}, u32[]{:S(2)}) copy-start(bf16[2048,128]{1,0:T(8,128)(2,1)S(1)} %collective-permute-done.30.refs_10_) | copy-start | bytes 1572868
  196.6 45.2 %collective-permute-start.32 = (bf16[2048,128]{1,0:T(8,128)(2,1)}, bf16[2048,128]{1,0:T(8,128)(2,1)S(1)}, u32[]{:S(2)}, u32[]{:S(2)}) collective-permute-start(bf16[2048,128]{1,0:T(8,128)(2,1)} %get-tuple-element.17.refs_12_), channel_id=1, source_target_pairs={{0,4},{4,0},{1,5},{5,1},{2,6},{6,2},{3,7},{7,3},{8,12},{12,8},{9,1... | collective-permute-start | bytes 1572872 | tf_op jit(solution)/shard_map/ppermute | solution.py:33
  204.2 38.0 %collective-permute-start.31 = (bf16[2048,128]{1,0:T(8,128)(2,1)S(1)}, bf16[2048,128]{1,0:T(8,128)(2,1)S(1)}, u32[]{:S(2)}, u32[]{:S(2)}) collective-permute-start(bf16[2048,128]{1,0:T(8,128)(2,1)S(1)} %collective-permute-done.30.refs_10_), channel_id=1, source_target_pairs={{0,4},{4,0},{1,5},{5,1},{2,6},{6,2},{3,7},{7,3},{8,12},{12,8},{9,1... | collective-permute-start | bytes 1572872 | tf_op jit(solution)/shard_map/ppermute | solution.py:33
  205.8 42.3 %collective-permute-start.34 = (bf16[2048,128]{1,0:T(8,128)(2,1)}, bf16[2048,128]{1,0:T(8,128)(2,1)S(1)}, u32[]{:S(2)}, u32[]{:S(2)}) collective-permute-start(bf16[2048,128]{1,0:T(8,128)(2,1)} %collective-permute-done.33.refs_14_), channel_id=1, source_target_pairs={{0,4},{4,0},{1,5},{5,1},{2,6},{6,2},{3,7},{7,3},{8,12},{12,8},{9,1... | collective-permute-start | bytes 1572872 | tf_op jit(solution)/shard_map/ppermute | solution.py:33
  230.1 13.9 %collective-permute-start.36 = (bf16[512,512]{1,0:T(8,128)(2,1)S(1)}, bf16[512,512]{1,0:T(8,128)(2,1)S(1)}, u32[]{:S(2)}, u32[]{:S(2)}) collective-permute-start(bf16[512,512]{1,0:T(8,128)(2,1)S(1)} %shard_map.79.refs_0_), channel_id=1, source_target_pairs={{0,2},{2,0},{1,3},{3,1},{4,6},{6,4},{5,7},{7,5},{8,10},{10,8},{9,1... | collective-permute-start | bytes 1572872 | tf_op jit(solution)/shard_map/ppermute | solution.py:33
  238.6 45.5 %copy-start.2 = (bf16[2048,128]{1,0:T(8,128)(2,1)S(1)}, bf16[2048,128]{1,0:T(8,128)(2,1)}, u32[]{:S(2)}) copy-start(bf16[2048,128]{1,0:T(8,128)(2,1)} %copy-done.1) | copy-start | bytes 1572868
  238.6 16.0 %collective-permute-start.25 = (bf16[512,512]{1,0:T(8,128)(2,1)S(1)}, bf16[512,512]{1,0:T(8,128)(2,1)S(1)}, u32[]{:S(2)}, u32[]{:S(2)}) collective-permute-start(bf16[512,512]{1,0:T(8,128)(2,1)S(1)} %shard_map.77.refs_0_), channel_id=1, source_target_pairs={{0,8},{8,0},{1,9},{9,1},{2,10},{10,2},{3,11},{11,3},{4,12},{12,4},... | collective-permute-start | bytes 1572872 | tf_op jit(solution)/shard_map/ppermute | solution.py:33
  241.8 35.6 %copy-start.29 = (bf16[2048,128]{1,0:T(8,128)(2,1)}, bf16[2048,128]{1,0:T(8,128)(2,1)S(1)}, u32[]{:S(2)}) copy-start(bf16[2048,128]{1,0:T(8,128)(2,1)S(1)} %collective-permute-done.32.refs_13_) | copy-start | bytes 1572868
  241.8 13.3 %collective-permute-start.23 = (bf16[512,512]{1,0:T(8,128)(2,1)S(1)}, bf16[512,512]{1,0:T(8,128)(2,1)S(1)}, u32[]{:S(2)}, u32[]{:S(2)}) collective-permute-start(bf16[512,512]{1,0:T(8,128)(2,1)S(1)} %shard_map.77.refs_0_), channel_id=1, source_target_pairs={{0,2},{2,0},{1,3},{3,1},{4,6},{6,4},{5,7},{7,5},{8,10},{10,8},{9,1... | collective-permute-start | bytes 1572872 | tf_op jit(solution)/shard_map/ppermute | solution.py:33
  242.2 35.3 %copy-start.30 = (bf16[2048,128]{1,0:T(8,128)(2,1)}, bf16[2048,128]{1,0:T(8,128)(2,1)S(1)}, u32[]{:S(2)}) copy-start(bf16[2048,128]{1,0:T(8,128)(2,1)S(1)} %collective-permute-done.31.refs_11_) | copy-start | bytes 1572868
  242.2 23.6 %collective-permute-start.38 = (bf16[512,512]{1,0:T(8,128)(2,1)S(1)}, bf16[512,512]{1,0:T(8,128)(2,1)S(1)}, u32[]{:S(2)}, u32[]{:S(2)}) collective-permute-start(bf16[512,512]{1,0:T(8,128)(2,1)S(1)} %shard_map.79.refs_0_), channel_id=1, source_target_pairs={{0,8},{8,0},{1,9},{9,1},{2,10},{10,2},{3,11},{11,3},{4,12},{12,4},... | collective-permute-start | bytes 1572872 | tf_op jit(solution)/shard_map/ppermute | solution.py:33
  244.0 31.6 %collective-permute-start.40 = (bf16[512,512]{1,0:T(8,128)(2,1)S(1)}, bf16[512,512]{1,0:T(8,128)(2,1)S(1)}, u32[]{:S(2)}, u32[]{:S(2)}) collective-permute-start(bf16[512,512]{1,0:T(8,128)(2,1)S(1)} %collective-permute-done.36.refs_2_), channel_id=1, source_target_pairs={{0,8},{8,0},{1,9},{9,1},{2,10},{10,2},{3,11},{11,3},{4,12},{12,4},... | collective-permute-start | bytes 1572872 | tf_op jit(solution)/shard_map/ppermute | solution.py:33
  248.1 29.4 %copy-start.31 = (bf16[2048,128]{1,0:T(8,128)(2,1)}, bf16[2048,128]{1,0:T(8,128)(2,1)S(1)}, u32[]{:S(2)}) copy-start(bf16[2048,128]{1,0:T(8,128)(2,1)S(1)} %collective-permute-done.34.refs_15_) | copy-start | bytes 1572868
  248.1 27.5 %collective-permute-start.35 = (bf16[512,512]{1,0:T(8,128)(2,1)S(1)}, bf16[512,512]{1,0:T(8,128)(2,1)S(1)}, u32[]{:S(2)}, u32[]{:S(2)}) collective-permute-start(bf16[512,512]{1,0:T(8,128)(2,1)S(1)} %shard_map.79.refs_0_), channel_id=1, source_target_pairs={{0,1},{1,0},{2,3},{3,2},{4,5},{5,4},{6,7},{7,6},{8,9},{9,8},{10,11... | collective-permute-start | bytes 1572872 | tf_op jit(solution)/shard_map/ppermute | solution.py:33
  254.6 21.5 %collective-permute-start.27 = (bf16[512,512]{1,0:T(8,128)(2,1)S(1)}, bf16[512,512]{1,0:T(8,128)(2,1)S(1)}, u32[]{:S(2)}, u32[]{:S(2)}) collective-permute-start(bf16[512,512]{1,0:T(8,128)(2,1)S(1)} %collective-permute-done.25.refs_4_), channel_id=1, source_target_pairs={{0,2},{2,0},{1,3},{3,1},{4,6},{6,4},{5,7},{7,5},{8,10},{10,8},{9,1... | collective-permute-start | bytes 1572872 | tf_op jit(solution)/shard_map/ppermute | solution.py:33
  255.2 21.0 %collective-permute-start.37 = (bf16[512,512]{1,0:T(8,128)(2,1)S(1)}, bf16[512,512]{1,0:T(8,128)(2,1)S(1)}, u32[]{:S(2)}, u32[]{:S(2)}) collective-permute-start(bf16[512,512]{1,0:T(8,128)(2,1)S(1)} %collective-permute-done.36.refs_2_), channel_id=1, source_target_pairs={{0,1},{1,0},{2,3},{3,2},{4,5},{5,4},{6,7},{7,6},{8,9},{9,8},{10,11... | collective-permute-start | bytes 1572872 | tf_op jit(solution)/shard_map/ppermute | solution.py:33
  265.8 10.8 %collective-permute-start.39 = (bf16[512,512]{1,0:T(8,128)(2,1)S(1)}, bf16[512,512]{1,0:T(8,128)(2,1)S(1)}, u32[]{:S(2)}, u32[]{:S(2)}) collective-permute-start(bf16[512,512]{1,0:T(8,128)(2,1)S(1)} %collective-permute-done.38.refs_4_), channel_id=1, source_target_pairs={{0,1},{1,0},{2,3},{3,2},{4,5},{5,4},{6,7},{7,6},{8,9},{9,8},{10,11... | collective-permute-start | bytes 1572872 | tf_op jit(solution)/shard_map/ppermute | solution.py:33
  275.6 1.9 collective-permute-start.41
  275.6 8.4 %collective-permute-start.22 = (bf16[512,512]{1,0:T(8,128)(2,1)S(1)}, bf16[512,512]{1,0:T(8,128)(2,1)S(1)}, u32[]{:S(2)}, u32[]{:S(2)}) collective-permute-start(bf16[512,512]{1,0:T(8,128)(2,1)S(1)} %shard_map.77.refs_0_), channel_id=1, source_target_pairs={{0,1},{1,0},{2,3},{3,2},{4,5},{5,4},{6,7},{7,6},{8,9},{9,8},{10,11... | collective-permute-start | bytes 1572872 | tf_op jit(solution)/shard_map/ppermute | solution.py:33
  276.1 7.9 %collective-permute-start.26 = (bf16[512,512]{1,0:T(8,128)(2,1)S(1)}, bf16[512,512]{1,0:T(8,128)(2,1)S(1)}, u32[]{:S(2)}, u32[]{:S(2)}) collective-permute-start(bf16[512,512]{1,0:T(8,128)(2,1)S(1)} %collective-permute-done.25.refs_4_), channel_id=1, source_target_pairs={{0,1},{1,0},{2,3},{3,2},{4,5},{5,4},{6,7},{7,6},{8,9},{9,8},{10,11... | collective-permute-start | bytes 1572872 | tf_op jit(solution)/shard_map/ppermute | solution.py:33
  276.2 7.9 %collective-permute-start.24 = (bf16[512,512]{1,0:T(8,128)(2,1)S(1)}, bf16[512,512]{1,0:T(8,128)(2,1)S(1)}, u32[]{:S(2)}, u32[]{:S(2)}) collective-permute-start(bf16[512,512]{1,0:T(8,128)(2,1)S(1)} %collective-permute-done.23.refs_2_), channel_id=1, source_target_pairs={{0,1},{1,0},{2,3},{3,2},{4,5},{5,4},{6,7},{7,6},{8,9},{9,8},{10,11... | collective-permute-start | bytes 1572872 | tf_op jit(solution)/shard_map/ppermute | solution.py:33
  276.6 7.4 %collective-permute-start.28 = (bf16[512,512]{1,0:T(8,128)(2,1)S(1)}, bf16[512,512]{1,0:T(8,128)(2,1)S(1)}, u32[]{:S(2)}, u32[]{:S(2)}) collective-permute-start(bf16[512,512]{1,0:T(8,128)(2,1)S(1)} %collective-permute-done.27.refs_6_), channel_id=1, source_target_pairs={{0,1},{1,0},{2,3},{3,2},{4,5},{5,4},{6,7},{7,6},{8,9},{9,8},{10,11... | collective-permute-start | bytes 1572872 | tf_op jit(solution)/shard_map/ppermute | solution.py:33
  (16 other events, 25.1 us)

commit v4 on v3

--- a/solution.py
+++ b/solution.py
@@ -19,7 +19,7 @@
 AXES = ("zh", "zl", "y", "x", "c")
 QUAD = ("zl", "x", "c")
 SWAP = [(0, 1), (1, 0)]
-EXTRA = 16
+EXTRA = 8
 QT = 256
 KT = 512
 NEG = -1e30
@@ -66,14 +66,14 @@
     return pl.multiple_of(value, step)
 
 
-def layout_kernel(wk_ref, wv_ref, doc_ref, out_ref):
-    for j in range(8):
-        out_ref[j, :128, :128] = wk_ref[:, 128 * j : 128 * j + 128]
-        out_ref[j, :128, 128:] = wv_ref[:, 128 * j : 128 * j + 128]
+def layout_kernel(wq_ref, wk_ref, wv_ref, doc_ref, out_ref):
     below = doc_ref[...] < lax.broadcasted_iota(jnp.int32, (EXTRA, 128), 0)
     count = jnp.sum(jnp.where(below, 1.0, 0.0), axis=1, keepdims=True)
-    rows = jnp.broadcast_to(count, (EXTRA, 256)).astype(jnp.bfloat16)
+    rows = jnp.broadcast_to(count, (EXTRA, 768)).astype(jnp.bfloat16)
     for j in range(8):
+        out_ref[j, :128, :512] = wq_ref[:, 512 * j : 512 * j + 512]
+        out_ref[j, :128, 512:640] = wk_ref[:, 128 * j : 128 * j + 128]
+        out_ref[j, :128, 640:] = wv_ref[:, 128 * j : 128 * j + 128]
         out_ref[j, 128:, :] = rows
 
 
@@ -101,56 +101,84 @@
     return copies
 
 
-def weight_row(where, dzh, dy, zlp):
-    return aligned((4 * (where[0] ^ dzh) + 2 * zlp + (where[2] ^ dy)) * 512, 512)
+def weight_copies(where, pieces, dst):
+    copies = []
+    for dzh, dy, ref, source, target in pieces:
+        for zlp in range(2):
+            block = 4 * (where[0] ^ dzh) + 2 * zlp + (where[2] ^ dy)
+            src = ref.at[pl.ds(4 * zlp, 4), pl.ds(0, 128), source]
+            copies.append((src, dst.at[pl.ds(4 * block, 4), :, target]))
+    return copies
 
 
 def turn(part, cos_ref, sin_ref, rows):
     return part * cos_ref[rows, :] + pltpu.roll(part, 64, axis=1) * sin_ref[rows, :]
 
 
-def project_kv_kernel(where, *refs):
-    tok_refs, wkv_refs, (cos_ref, sin_ref) = refs[:12], refs[12:16], refs[16:18]
-    kv_out, xs, wkv, sems = refs[18:]
-    copies = []
-    for (dzh, dy), ref in zip(((0, 0), (0, 1), (1, 0), (1, 1)), wkv_refs):
-        for j in range(8):
-            row = aligned(weight_row(where, dzh, dy, j // 4) + (j % 4) * 128, 128)
-            copies.append((ref.at[j, pl.ds(0, 128), :], wkv.at[pl.ds(row, 128), :]))
+def project_kv_kernel(where, count_ref, *refs):
+    tok_refs, (w_own, w_y, w_z, w_zy, cos_ref, sin_ref) = refs[:12], refs[12:18]
+    kv_out, start_out, bounds_out, xs, wkv, sems = refs[18:]
+    zh, zl, y = where[0], where[1], where[2]
+    columns, whole = pl.ds(512, 256), pl.ds(0, 256)
     near = start_copies(token_copies(0, where, tok_refs, xs), sems)
-    near += start_copies(copies, sems, 4)
-    far = start_copies(token_copies(1, where, tok_refs, xs), sems, 36)
+    pieces = (
+        (0, 0, w_own, columns, whole),
+        (0, 1, w_y, columns, whole),
+        (1, 0, w_z, whole, whole),
+        (1, 1, w_zy, whole, whole),
+    )
+    near += start_copies(weight_copies(where, pieces, wkv), sems, 4)
+    far = start_copies(token_copies(1, where, tok_refs, xs), sems, 12)
+
+    counts = jnp.sum(count_ref[...].astype(jnp.float32), axis=0).astype(jnp.int32)
+    for half in range(2):
+        base = (2 * zh + half) * 1024 + y * 512
+        position = base + lax.broadcasted_iota(jnp.int32, (512, 128), 0)
+        start = jnp.zeros((512, 128), jnp.int32)
+        for d in range(DOCS):
+            row = counts[d : d + 1, :]
+            start = jnp.maximum(start, jnp.where(position >= row, row, 0))
+        start_out[512 * half : 512 * half + 512, :] = start
+    document = [jnp.max(counts[d : d + 1, :]) for d in range(DOCS)]
+    for tile in range(1024 // QT):
+        first = first_position(zh, y, tile)
+        for k, position in enumerate((first, first + QT - 1)):
+            bound = jnp.int32(0)
+            for d in range(DOCS):
+                bound = jnp.maximum(bound, jnp.where(position >= document[d], document[d], 0))
+            bounds_out[4 * k + tile] = bound
+
     for dzl, waits in enumerate((near, far)):
         wait_all(waits)
-        rows = pl.ds(aligned((where[1] ^ dzl) * 512, 512), 512)
-        acc = jnp.dot(xs[rows, :], wkv[...], preferred_element_type=jnp.float32)
+        rows = pl.ds(aligned((zl ^ dzl) * 512, 512), 512)
+        weights = wkv[...].reshape(4096, 256)
+        acc = jnp.dot(xs[rows, :], weights, preferred_element_type=jnp.float32)
         kv_out[rows, :128] = turn(acc[:, :128], cos_ref, sin_ref, rows).astype(jnp.bfloat16)
         kv_out[rows, 128:] = acc[:, 128:].astype(jnp.bfloat16)
 
 
 def project_q_kernel(where, *refs):
     tok_refs = refs[:12]
-    wq_own, wq_y, wq_z0, wq_z1, wq_zy0, wq_zy1, cos_ref, sin_ref = refs[12:20]
+    w_own, w_y, w_z0, w_z1, w_zy0, w_zy1, cos_ref, sin_ref = refs[12:20]
     q_out, xs, wq, sems = refs[20:]
-    copies = []
-    for zlp in range(2):
-        for dzh, dy, src in (
-            (0, 0, wq_own.at[pl.ds(zlp * 512, 512), :]),
-            (0, 1, wq_y.at[pl.ds(zlp * 512, 512), :]),
-            (1, 0, (wq_z0, wq_z1)[zlp]),
-            (1, 1, (wq_zy0, wq_zy1)[zlp]),
-        ):
-            copies.append((src, wq.at[pl.ds(weight_row(where, dzh, dy, zlp), 512), :]))
+    whole, left, right = pl.ds(0, 512), pl.ds(0, 256), pl.ds(256, 256)
     near = start_copies(token_copies(0, where, tok_refs, xs), sems)
-    near += start_copies(copies, sems, 4)
-    far = start_copies(token_copies(1, where, tok_refs, xs), sems, 12)
+    pieces = (
+        (0, 0, w_own, whole, whole),
+        (0, 1, w_y, whole, whole),
+        (1, 0, w_z0, left, left),
+        (1, 1, w_zy0, left, left),
+        (1, 0, w_z1, left, right),
+        (1, 1, w_zy1, left, right),
+    )
+    near += start_copies(weight_copies(where, pieces, wq), sems, 4)
+    far = start_copies(token_copies(1, where, tok_refs, xs), sems, 16)
     for dzl, waits in enumerate((near, far)):
         wait_all(waits)
         rows = pl.ds(aligned((where[1] ^ dzl) * 512, 512), 512)
         for n in range(2):
-            acc = jnp.dot(
-                xs[rows, :], wq[:, 256 * n : 256 * n + 256], preferred_element_type=jnp.float32
-            )
+            weights = wq[:, :, 256 * n : 256 * n + 256].reshape(4096, 256)
+            acc = jnp.dot(xs[rows, :], weights, preferred_element_type=jnp.float32)
             for k in range(2):
                 part = turn(acc[:, 128 * k : 128 * k + 128], cos_ref, sin_ref, rows)
                 columns = slice(256 * n + 128 * k, 256 * n + 128 * k + 128)
@@ -198,7 +226,7 @@
     return jnp.concatenate([q_ref[:, 128 * h : 128 * h + 128] for h in range(4)], axis=0)
 
 
-def near_kernel(half, where, tile_lo, tile_hi, q_ref, start_ref, kv_own, kv_y, *refs):
+def near_kernel(half, where, bounds, q_ref, start_ref, kv_own, kv_y, *refs):
     top, total, acc, ks, vs, sems = refs
     zh, y = where[0], where[2]
     tile = 2 * half + pl.program_id(0)
@@ -214,10 +242,10 @@
     first = first_position(zh, y, tile)
     base = zh * (2048 // KT)
 
-    @pl.loop(jnp.maximum(tile_lo[tile] // KT, base), (first + QT + KT - 1) // KT)
+    @pl.loop(jnp.maximum(bounds[tile] // KT, base), (first + QT + KT - 1) // KT)
     def _(block):
         keys = pl.ds(aligned((block - base) * KT, KT), KT)
-        edge = (block * KT + KT - 1 > first) | (block * KT < tile_hi[tile])
+        edge = (block * KT + KT - 1 > first) | (block * KT < bounds[4 + tile])
 
         @pl.when(edge)
         def _():
@@ -231,7 +259,7 @@
             attend_step(stacked(q_ref), ks[keys, :], vs[keys, :], state, None)
 
 
-def far_kernel(half, where, tile_lo, tile_hi, q_ref, start_ref, kv_z, kv_zy, *refs):
+def far_kernel(half, where, bounds, q_ref, start_ref, kv_z, kv_zy, *refs):
     top_in, total_in, acc_in, out_ref, ks, vs, top, total, acc, sems = refs
     zh, y = where[0], where[2]
     tile = 2 * half + pl.program_id(0)
@@ -244,10 +272,10 @@
     total[...] = total_in[0]
     acc[...] = acc_in[0]
 
-    @pl.loop(tile_lo[tile] // KT, zh * (2048 // KT))
+    @pl.loop(bounds[tile] // KT, zh * (2048 // KT))
     def _(block):
         keys = pl.ds(aligned(block * KT, KT), KT)
-        edge = block * KT < tile_hi[tile]
+        edge = block * KT < bounds[4 + tile]
 
         @pl.when(edge)
         def _():
@@ -264,29 +292,59 @@
         out_ref[:, 128 * h : 128 * h + 128] = result[QT * h : QT * h + QT].astype(jnp.bfloat16)
 
 
-def output_kernel(with_first, where, *refs):
-    att_refs = refs[:8]
-    wo_refs = refs[8:16]
-    rest = refs[16:]
-    out_ref, xs, wo, sems = rest[-4:]
-    zh, zl, y, x, c = (where[i] for i in range(5))
-    copies = []
-    for (dzl, dx, dc), ref in zip(OFFSETS, att_refs):
-        slot = 4 * (zl ^ dzl) + 2 * (x ^ dx) + (c ^ dc)
-        copies.append((ref, xs.at[:, pl.ds(aligned(slot * 512, 512), 512)]))
-    for i, ref in enumerate(wo_refs):
-        column = aligned((2 * (zh ^ (i // 2 % 2)) + (y ^ (i % 2))) * 128, 128)
-        copies.append((ref, wo.at[2048 * (i // 4) : 2048 * (i // 4) + 2048, pl.ds(column, 128)]))
-    started = start_copies(copies, sems)
-    base = 0
-    if with_first:
-        base = 512
-        out_ref[:512, :] = rest[0][...]
-    wait_all(started)
+def head_slot(where, dzl, dx, dc):
+    return 4 * (where[1] ^ dzl) + 2 * (where[3] ^ dx) + (where[4] ^ dc)
+
+
+def output_near_kernel(half, where, *refs):
+    att_refs, wo_refs = refs[:6], refs[6:-4] if half == 0 else refs[6:7]
+    zh, y = where[0], where[2]
+    if half == 0:
+        out_ref, wo, xs, sems = refs[-4:]
+        copies = []
+        for i, ref in enumerate(wo_refs):
+            column = aligned((2 * (zh ^ (i // 2 % 2)) + (y ^ (i % 2))) * 128, 128)
+            rows = slice(2048 * (i // 4), 2048 * (i // 4) + 2048)
+            copies.append((ref, wo.at[rows, pl.ds(column, 128)]))
+    else:
+        out_ref, wo, xs, sems = refs[-4:]
+        copies = [(wo_refs[0], wo)]
+    slots = [head_slot(where, *at) for at in OFFSETS[:6]]
+    for i, ref in enumerate(att_refs):
+        copies.append((ref, xs.at[:, pl.ds(512 * i, 512)]))
+    wait_all(start_copies(copies, sems))
     for n in range(2):
         columns = slice(256 * n, 256 * n + 256)
-        acc = jnp.dot(xs[...], wo[:, columns], preferred_element_type=jnp.float32)
-        out_ref[base : base + 512, columns] = acc.astype(jnp.bfloat16)
+        acc = jnp.zeros((512, 256), jnp.float32)
+        for i, slot in enumerate(slots):
+            acc += jnp.dot(
+                xs[:, 512 * i : 512 * i + 512],
+                wo[pl.ds(aligned(slot * 512, 512), 512), columns],
+                preferred_element_type=jnp.float32,
+            )
+        out_ref[:, columns] = acc
+
+
+def output_far_kernel(where, *refs):
+    far_refs, (wo_ref, part0, part1), (out_ref, xs, wo, sems) = refs[:4], refs[4:7], refs[7:]
+    slots = [head_slot(where, *at) for at in OFFSETS[6:]]
+    copies = []
+    for half in range(2):
+        for i in range(2):
+            src = far_refs[2 * half + i]
+            copies.append((src, xs.at[pl.ds(512 * half, 512), pl.ds(512 * i, 512)]))
+    for i, slot in enumerate(slots):
+        src = wo_ref.at[pl.ds(aligned(slot * 512, 512), 512), :]
+        copies.append((src, wo.at[pl.ds(512 * i, 512), :]))
+    wait_all(start_copies(copies, sems))
+    for half, part in enumerate((part0, part1)):
+        rows = slice(512 * half, 512 * half + 512)
+        for n in range(2):
+            columns = slice(256 * n, 256 * n + 256)
+            acc = part[:, columns] + jnp.dot(
+                xs[rows, :], wo[:, columns], preferred_element_type=jnp.float32
+            )
+            out_ref[rows, columns] = acc.astype(jnp.bfloat16)
 
 
 def finish_kernel(tok_ref, sent_ref, out_ref):
@@ -298,7 +356,7 @@
         out_ref[:, columns] = (tok_ref[:, columns].astype(jnp.float32) + sent).astype(jnp.bfloat16)
 
 
-def call(kernel, out_shape, in_specs, scratch, cost, **more):
+def call(kernel, out_shape, in_specs, scratch, cost, vmem=24, **more):
     flops, moved = cost
     more.setdefault("out_specs", jax.tree.map(lambda _: VMEM, out_shape))
     return pl.pallas_call(
@@ -306,7 +364,7 @@
         out_shape=out_shape,
         in_specs=in_specs,
         scratch_shapes=scratch,
-        compiler_params=pltpu.CompilerParams(vmem_limit_bytes=48 * 1024 * 1024),
+        compiler_params=pltpu.CompilerParams(vmem_limit_bytes=vmem * 1024 * 1024),
         cost_estimate=pl.CostEstimate(flops=flops, bytes_accessed=moved, transcendentals=0),
         **more,
     )
@@ -317,24 +375,19 @@
     zh, zl, y, x, c = place = [lax.axis_index(axis) for axis in AXES]
     where = jnp.stack(place).astype(jnp.int32)
 
-    wkv = call(
+    weights = call(
         layout_kernel,
-        jax.ShapeDtypeStruct((8, 128 + EXTRA, 256), bf16),
-        [VMEM] * 3,
+        jax.ShapeDtypeStruct((8, 128 + EXTRA, 768), bf16),
+        [VMEM] * 4,
         [],
-        (128 * EXTRA, 1 << 20),
-    )(wk, wv, doc_ids.reshape(1, 128))
-    wkv = lax.all_to_all(wkv, QUAD, 0, 0, tiled=True)
-    wkv_z = swap(wkv, "zh")
-    wkvs = [wkv, swap(wkv, "y"), wkv_z, swap(wkv_z, "y")]
-
-    wqs = jnp.transpose(wq.reshape(128, 8, 512), (1, 0, 2))
-    wqs = lax.all_to_all(wqs, QUAD, 0, 0, tiled=True).reshape(1024, 512)
-    wq_z0 = swap(wqs[:512], "zh")
-    wq_z1 = swap(wqs[512:], "zh")
-    wq_y = swap(wqs, "y")
-    wq_zy0 = swap(wq_z0, "y")
-    wq_zy1 = swap(wq_z1, "y")
+        (128 * EXTRA, 3 << 20),
+    )(wq, wk, wv, doc_ids.reshape(1, 128))
+    weights = lax.all_to_all(weights, QUAD, 0, 0, tiled=True)
+    w_y = swap(weights, "y")
+    wkv_z = swap(weights[:, :, 512:], "zh")
+    wkv_zy = swap(wkv_z, "y")
+    wq_z = [swap(weights[:, :128, 256 * n : 256 * n + 256], "zh") for n in range(2)]
+    wq_zy = [swap(wq_z[n], "y") for n in range(2)]
 
     source = tokens.astype(f32)
     mean_sq = jnp.mean(source * source, axis=1, keepdims=True)
@@ -353,37 +406,37 @@
     cosine = jnp.concatenate([cosine, cosine], axis=1)
     sine = jnp.concatenate([-sine, sine], axis=1)
 
-    counts = jnp.concatenate([piece[:, 128 : 128 + DOCS, 0] for piece in wkvs], axis=0)
-    starts = jnp.sum(counts.astype(f32), axis=0).astype(jnp.int32)
-    query_start = jnp.max(
-        jnp.where(positions[:, None] >= starts[None, :], starts[None, :], 0), axis=1
-    )
-    tile_lo = query_start[::QT]
-    tile_hi = query_start[QT - 1 :: QT]
-    start_col = jnp.broadcast_to(query_start[:, None], (1024, 128))
-
-    keys_values = call(
+    counts = jnp.concatenate(
+        [piece[:, 128:, -128:] for piece in (weights, w_y, wkv_z, wkv_zy)], axis=0
+    )
+
+    keys_values, start_col, bounds = call(
         project_kv_kernel,
-        jax.ShapeDtypeStruct((1024, 256), bf16),
-        [SMEM] + [ANY] * 16 + [VMEM, VMEM],
+        (
+            jax.ShapeDtypeStruct((1024, 256), bf16),
+            jax.ShapeDtypeStruct((1024, 128), jnp.int32),
+            jax.ShapeDtypeStruct((8,), jnp.int32),
+        ),
+        [SMEM, VMEM] + [ANY] * 16 + [VMEM, VMEM],
         [
             pltpu.VMEM((1024, 4096), bf16),
-            pltpu.VMEM((4096, 256), bf16),
-            pltpu.SemaphoreType.DMA((44,)),
+            pltpu.VMEM((32, 128, 256), bf16),
+            pltpu.SemaphoreType.DMA((20,)),
         ],
         (2 * 1024 * 4096 * 256, 11 << 20),
-    )(where, *tok, *wkvs, cosine, sine)
+        out_specs=(VMEM, VMEM, SMEM),
+    )(where, counts, *tok, weights, w_y, wkv_z, wkv_zy, cosine, sine)
     queries = call(
         project_q_kernel,
         jax.ShapeDtypeStruct((1024, 512), bf16),
         [SMEM] + [ANY] * 18 + [VMEM, VMEM],
         [
             pltpu.VMEM((1024, 4096), bf16),
-            pltpu.VMEM((4096, 512), bf16),
-            pltpu.SemaphoreType.DMA((20,)),
+            pltpu.VMEM((32, 128, 512), bf16),
+            pltpu.SemaphoreType.DMA((24,)),
         ],
         (2 * 1024 * 4096 * 512, 14 << 20),
-    )(where, *tok, wqs, wq_y, wq_z0, wq_z1, wq_zy0, wq_zy1, cosine, sine)
+    )(where, *tok, weights, w_y, *wq_z, *wq_zy, cosine, sine)
 
     kv_y = swap(keys_values, "y")
     kv_z = swap(keys_values, "zh")
@@ -399,7 +452,7 @@
         return call(
             functools.partial(near_kernel, half),
             [jax.ShapeDtypeStruct((2, 4 * QT, 128), f32)] * 3,
-            [SMEM] * 3
+            [SMEM] * 2
             + [tile_spec((QT, 512), 2 * half), tile_spec((QT, 128), 2 * half), ANY, ANY],
             [
                 pltpu.VMEM((2048, 128), bf16),
@@ -409,7 +462,7 @@
             (4 * 512 * 2048 * 512, 4 << 20),
             grid=(2,),
             out_specs=state_specs(),
-        )(where, tile_lo, tile_hi, queries, start_col, keys_values, kv_y)
+        )(where, bounds, queries, start_col, keys_values, kv_y)
 
     state = [near_half(0), near_half(1)]
 
@@ -417,7 +470,7 @@
         return call(
             functools.partial(far_kernel, half),
             jax.ShapeDtypeStruct((512, 512), bf16),
-            [SMEM, SMEM, SMEM, tile_spec((QT, 512), 2 * half), tile_spec((QT, 128), 2 * half)]
+            [SMEM, SMEM, tile_spec((QT, 512), 2 * half), tile_spec((QT, 128), 2 * half)]
             + [ANY, ANY] + state_specs(),
             [
                 pltpu.VMEM((2048, 128), bf16),
@@ -430,7 +483,7 @@
             (4 * 512 * 2048 * 512, 8 << 20),
             grid=(2,),
             out_specs=pl.BlockSpec((QT, 512), lambda i: (i, 0)),
-        )(where, tile_lo, tile_hi, queries, start_col, kv_z, kv_zy, *state[half])
+        )(where, bounds, queries, start_col, kv_z, kv_zy, *state[half])
 
     attended = [far_call(0), far_call(1)]
 
@@ -440,25 +493,33 @@
         by_z = swap(piece, "zh")
         wos += [piece, swap(piece, "y"), by_z, swap(by_z, "y")]
 
-    def output(half, first):
-        att = quad_gather(attended[half], half == 1)
-        rows = 1024 if first else 512
-        return output_call(att, first, rows)
-
-    def output_call(att, first, rows):
+    att = [quad_gather(attended[half], half == 1) for half in range(2)]
+
+    def output_near(half, weights):
+        rows = jax.ShapeDtypeStruct((512, 512), f32)
+        laid = jax.ShapeDtypeStruct((4096, 512), bf16)
         return call(
-            functools.partial(output_kernel, bool(first)),
-            jax.ShapeDtypeStruct((rows, 512), bf16),
-            [SMEM] + [ANY] * 16 + [VMEM] * len(first),
-            [
-                pltpu.VMEM((512, 4096), bf16),
-                pltpu.VMEM((4096, 512), bf16),
-                pltpu.SemaphoreType.DMA((16,)),
-            ],
-            (2 * 512 * 4096 * 512, 9 << 20),
-        )(where, *[att[at] for at in OFFSETS], *wos, *first)
-
-    sent = output(1, [output(0, [])])
+            functools.partial(output_near_kernel, half),
+            [rows, laid] if half == 0 else [rows],
+            [SMEM] + [ANY] * (6 + len(weights)),
+            ([] if half == 0 else [pltpu.VMEM((4096, 512), bf16)])
+            + [pltpu.VMEM((512, 3072), bf16), pltpu.SemaphoreType.DMA((14,))],
+            (2 * 512 * 3072 * 512, 9 << 20),
+        )(where, *[att[half][at] for at in OFFSETS[:6]], *weights)
+
+    part0, laid = output_near(0, wos)
+    (part1,) = output_near(1, [laid])
+    sent = call(
+        output_far_kernel,
+        jax.ShapeDtypeStruct((1024, 512), bf16),
+        [SMEM] + [ANY] * 5 + [VMEM] * 2,
+        [
+            pltpu.VMEM((1024, 1024), bf16),
+            pltpu.VMEM((1024, 512), bf16),
+            pltpu.SemaphoreType.DMA((6,)),
+        ],
+        (2 * 1024 * 1024 * 512, 5 << 20),
+    )(where, *[att[half][at] for half in range(2) for at in OFFSETS[6:]], laid, part0, part1)
     home = lax.all_to_all(sent.reshape(8, 128, 512), QUAD, 0, 0, tiled=True)
     return call(
         finish_kernel,

time: 312 us -> 308 us (0.987)
  the two profiles are of different devices: /device:TPU:16 before, /device:TPU:0 now
where the time goes in v4:
time: 308 us; the launch traced here: 304 us
  waiting for transfers between devices  194 us (63%)
  Pallas kernels  40.4 us (13%)
  starting transfers between devices  37.6 us (12%)
  blocking collectives  17.2 us (6%)
  local copies, waits for them, and re-layouts  10.3 us (3%)
  other arithmetic  4.11 us (1%)
    ppermute x41, waiting for transfers between devices, swap(): return lax.ppermute(value, axis, SWAP)  177 us
    ppermute x41, starting transfers between devices, swap(): return lax.ppermute(value, axis, SWAP)  32.2 us
    all_to_all x1, blocking collectives, split_body(): home = lax.all_to_all(sent.reshape(8, 128, 512), QUAD, 0, 0, tiled=True)  17.2 us
    all_to_all x1, waiting for transfers between devices, split_body(): weights = lax.all_to_all(weights, QUAD, 0, 0, tiled=True)  16.7 us
    pallas_call x2, Pallas kernels, near_half(): call(functools.partial(near_kernel, half), [jax.ShapeDtypeStruct((2, 4 *...  10.4 us
    pallas_call x1, Pallas kernels, split_body(): call(project_q_kernel, jax.ShapeDtypeStruct((1024, 512), bf16), [SMEM] +...  8.41 us
    pallas_call x1, Pallas kernels, split_body(): call(project_kv_kernel, (jax.ShapeDtypeStruct((1024, 256), bf16), jax.Sha...  8.41 us
    pallas_call x2, Pallas kernels, output_near(): call(functools.partial(output_near_kernel, half), [rows, laid] if half ==...  6.9 us
  transfers between devices with their start and end apart: 42, of which 19 were waited for; matrix products, arithmetic and copies ran while one was open for 3% of the time, Pallas kernels for 12%

profile of v4, /device:TPU:0, one launch (start us, length us, event | category | flops | bytes accessed | tf_op | source)
XLA Modules:
  0.0 304.1 jit_solution(4171715356567210958)
XLA Ops:
  0.0 1.2 copy-done.5
  1.2 0.9 copy-done.6
  2.2 0.9 copy-done.7
  3.1 0.7 copy-done.8
  4.0 1.2 copy-done.2
  5.2 5.4 %all-to-all-start = ((bf16[8,136,768]{2,1,0:T(8,128)(2,1)}), bf16[8,136,768]{2,1,0:T(8,128)(2,1)S(1)}, u32[]{:S(2)}, u32[]{:S(2)}) async-start(bf16[8,136,768]{2,1,0:T(8,128)(2,1)} %copy-done.2), calls=%async_computation | async-start | bytes 3342336 | tf_op jit(solution)/shard_map/all_to_all | solution.py:385
  10.9 1.5 fusion.2.refs_0_
  12.4 1.1 fusion.18
  13.5 2.0 collective-permute-start.6
  15.5 16.7 %all-to-all-done.refs_12_ = bf16[8,136,768]{2,1,0:T(8,128)(2,1)S(1)} async-done(((bf16[8,136,768]{2,1,0:T(8,128)(2,1)}), bf16[8,136,768]{2,1,0:T(8,128)(2,1)S(1)}, u32[]{:S(2)}, u32[]{:S(2)}) %all-to-all-start) | async-done | bytes 1671200 | tf_op jit(solution)/shard_map/all_to_all | solution.py:385
  32.3 1.5 collective-permute-start
  33.8 9.7 %collective-permute-done.6.refs_4_ = bf16[64,4096]{1,0:T(8,128)(2,1)S(1)} collective-permute-done((bf16[64,4096]{1,0:T(8,128)(2,1)}, bf16[64,4096]{1,0:T(8,128)(2,1)S(1)}, u32[]{:S(2)}, u32[]{:S(2)}) %collective-permute-start.6) | collective-permute-done | bytes 524320 | tf_op jit(solution)/shard_map/ppermute | solution.py:33
  43.5 1.5 collective-permute-start.10
  45.0 9.3 %collective-permute-done.8.refs_6_ = bf16[64,4096]{1,0:T(8,128)(2,1)} collective-permute-done((bf16[64,4096]{1,0:T(8,128)(2,1)}, bf16[64,4096]{1,0:T(8,128)(2,1)}, u32[]{:S(2)}, u32[]{:S(2)}) %collective-permute-start.8) | collective-permute-done | bytes 524320 | tf_op jit(solution)/shard_map/ppermute | solution.py:33
  54.3 1.5 collective-permute-start.12
  55.7 0.6 collective-permute-start.4
  56.3 2.7 collective-permute-start.1
  59.0 10.4 %collective-permute-done.12.refs_10_ = bf16[64,4096]{1,0:T(8,128)(2,1)} collective-permute-done((bf16[64,4096]{1,0:T(8,128)(2,1)}, bf16[64,4096]{1,0:T(8,128)(2,1)}, u32[]{:S(2)}, u32[]{:S(2)}) %collective-permute-start.12) | collective-permute-done | bytes 524320 | tf_op jit(solution)/shard_map/ppermute | solution.py:33
  69.4 13.5 %collective-permute-done.1.refs_14_ = bf16[8,136,256]{2,1,0:T(8,128)(2,1)} collective-permute-done((bf16[8,136,256]{2,1,0:T(8,128)(2,1)S(1)}, bf16[8,136,256]{2,1,0:T(8,128)(2,1)}, u32[]{:S(2)}, u32[]{:S(2)}) %collective-permute-start.1) | collective-permute-done | bytes 557088 | tf_op jit(solution)/shard_map/ppermute | solution.py:33
  82.9 1.5 collective-permute-start.2
  84.4 0.8 copy-done.3
  85.2 5.2 %collective-permute-done.4.refs_2_ = bf16[128,4096]{1,0:T(8,128)(2,1)} collective-permute-done((bf16[128,4096]{1,0:T(8,128)(2,1)S(1)}, bf16[128,4096]{1,0:T(8,128)(2,1)}, u32[]{:S(2)}, u32[]{:S(2)}) %collective-permute-start.4) | collective-permute-done | bytes 1048608 | tf_op jit(solution)/shard_map/ppermute | solution.py:33
  90.4 1.1 fusion.16
  91.5 0.5 collective-permute-start.11
  92.1 5.4 %collective-permute-done.2.refs_15_ = bf16[8,136,256]{2,1,0:T(8,128)(2,1)} collective-permute-done((bf16[8,136,256]{2,1,0:T(8,128)(2,1)}, bf16[8,136,256]{2,1,0:T(8,128)(2,1)}, u32[]{:S(2)}, u32[]{:S(2)}) %collective-permute-start.2) | collective-permute-done | bytes 557088 | tf_op jit(solution)/shard_map/ppermute | solution.py:33
  97.5 2.9 collective-permute-start.15
  100.5 1.9 fusion.3
  102.8 0.7 slice.47
  103.5 0.7 slice.48
  104.2 0.7 slice.45
  105.0 28.3 %collective-permute-done.14.refs_14_ = bf16[8,128,256]{2,1,0:T(8,128)(2,1)} collective-permute-done((bf16[8,128,256]{2,1,0:T(8,128)(2,1)}, bf16[8,128,256]{2,1,0:T(8,128)(2,1)}, u32[]{:S(2)}, u32[]{:S(2)}) %collective-permute-start.14) | collective-permute-done | bytes 524320 | tf_op jit(solution)/shard_map/ppermute | solution.py:33
  133.3 1.5 collective-permute-start.16
  134.8 9.6 %collective-permute-done.15.refs_15_ = bf16[8,128,256]{2,1,0:T(8,128)(2,1)} collective-permute-done((bf16[8,128,256]{2,1,0:T(8,128)(2,1)}, bf16[8,128,256]{2,1,0:T(8,128)(2,1)}, u32[]{:S(2)}, u32[]{:S(2)}) %collective-permute-start.15) | collective-permute-done | bytes 524320 | tf_op jit(solution)/shard_map/ppermute | solution.py:33
  144.4 1.5 collective-permute-start.17
  146.0 8.4 %shard_map.74 = (bf16[1024,256]{1,0:T(8,128)(2,1)S(1)}, s32[1024,128]{1,0:T(8,128)S(1)}, s32[8]{0:T(128)S(1)}) custom-call(s32[5]{0:T(128)S(1)} %stack.23.where, bf16[32,8,128]{2,1,0:T(8,128)(2,1)S(1)} %pad_maximum_fusion.2.count_ref, bf16[128,4096]{1,0:T(8,128)(2,1)S(1)} %fusion.2.refs_0_, bf16[128,4096]{1,0:T(8,128)(2,1)} %collective-permute-done.3.refs_1_, ...), custom_call_target="tpu_custom_call" | custom-call | flops 2147483648 | bytes 11534336 | tf_op jit(solution)/shard_map/pallas_call | solution.py:413
  154.6 3.0 collective-permute-start.32
  157.6 0.5 collective-permute-start.20
  158.5 1.6 collective-permute-start.31
  160.1 41.9 %collective-permute-done.18.kv_z = bf16[1024,256]{1,0:T(8,128)(2,1)S(1)} collective-permute-done((bf16[1024,256]{1,0:T(8,128)(2,1)S(1)}, bf16[1024,256]{1,0:T(8,128)(2,1)S(1)}, u32[]{:S(2)}, u32[]{:S(2)}) %collective-permute-start.18) | collective-permute-done | bytes 524320 | tf_op jit(solution)/shard_map/ppermute | solution.py:33
  202.0 0.5 collective-permute-start.19
  202.5 8.4 %shard_map.75.q_ref = bf16[1024,512]{1,0:T(8,128)(2,1)S(1)} custom-call(s32[5]{0:T(128)S(1)} %stack.23.where, bf16[128,4096]{1,0:T(8,128)(2,1)S(1)} %fusion.2.refs_0_, bf16[128,4096]{1,0:T(8,128)(2,1)} %collective-permute-done.3.refs_1_, bf16[128,4096]{1,0:T(8,128)(2,1)} %collective-permute-done.4.refs_2_, bf16[128,4096]{1,0:T(8,128)(2,1)} %collective-permute-done.5.refs_3_, ...), custom_call_target="tpu_custom_call" | custom-call | flops 4294967296 | bytes 14680064 | tf_op jit(solution)/shard_map/pallas_call | solution.py:429
  211.0 2.3 collective-permute-done.32.refs_8_
  213.8 10.6 %collective-permute-done.35.refs_12_ = bf16[2048,128]{1,0:T(8,128)(2,1)S(1)} collective-permute-done((bf16[2048,128]{1,0:T(8,128)(2,1)S(1)}, bf16[2048,128]{1,0:T(8,128)(2,1)S(1)}, u32[]{:S(2)}, u32[]{:S(2)}) %collective-permute-start.35) | collective-permute-done | bytes 524320 | tf_op jit(solution)/shard_map/ppermute | solution.py:33
  224.4 0.5 collective-permute-start.33
  224.9 1.5 collective-permute-start.36
  226.4 3.2 %shard_map.76 = (f32[2,1024,128]{2,1,0:T(8,128)S(1)}, f32[2,1024,128]{2,1,0:T(8,128)S(1)}, f32[2,1024,128]{2,1,0:T(8,128)S(1)}) custom-call(s32[5]{0:T(128)S(1)} %stack.23.where, s32[8]{0:T(128)S(1)} %get-tuple-element.16.bounds, bf16[1024,512]{1,0:T(8,128)(2,1)S(1)} %shard_map.75.q_ref, s32[1024,128]{1,0:T(8,128)S(1)} %get-tuple-element.17.start_ref, ...), custom_call_target="tpu_custom_call" | custom-call | flops 2147483648 | bytes 4194304 | tf_op jit(solution)/shard_map/pallas_call | solution.py:452
  229.6 7.2 %shard_map.78 = (f32[2,1024,128]{2,1,0:T(8,128)S(1)}, f32[2,1024,128]{2,1,0:T(8,128)S(1)}, f32[2,1024,128]{2,1,0:T(8,128)S(1)}) custom-call(s32[5]{0:T(128)S(1)} %stack.23.where, s32[8]{0:T(128)S(1)} %get-tuple-element.16.bounds, bf16[1024,512]{1,0:T(8,128)(2,1)S(1)} %shard_map.75.q_ref, s32[1024,128]{1,0:T(8,128)S(1)} %get-tuple-element.17.start_ref, ...), custom_call_target="tpu_custom_call" | custom-call | flops 2147483648 | bytes 4194304 | tf_op jit(solution)/shard_map/pallas_call | solution.py:452
  236.9 1.3 shard_map.77.refs_0_
  238.2 1.2 collective-permute-start.21
  239.4 1.3 shard_map.79.refs_0_
  240.7 2.1 collective-permute-start.24
  242.8 6.7 %collective-permute-done.36.refs_13_ = bf16[2048,128]{1,0:T(8,128)(2,1)S(1)} collective-permute-done((bf16[2048,128]{1,0:T(8,128)(2,1)S(1)}, bf16[2048,128]{1,0:T(8,128)(2,1)S(1)}, u32[]{:S(2)}, u32[]{:S(2)}) %collective-permute-start.36) | collective-permute-done | bytes 524320 | tf_op jit(solution)/shard_map/ppermute | solution.py:33
  249.5 1.1 collective-permute-start.38
  250.6 1.3 collective-permute-done.21.refs_2_
  251.9 2.3 collective-permute-done.29.refs_4_
  254.2 9.4 %collective-permute-done.24.refs_4_ = bf16[512,512]{1,0:T(8,128)(2,1)S(1)} collective-permute-done((bf16[512,512]{1,0:T(8,128)(2,1)S(1)}, bf16[512,512]{1,0:T(8,128)(2,1)S(1)}, u32[]{:S(2)}, u32[]{:S(2)}) %collective-permute-start.24) | collective-permute-done | bytes 524320 | tf_op jit(solution)/shard_map/ppermute | solution.py:33
  263.6 0.9 collective-permute-start.25
  265.4 10.3 %collective-permute-done.25.refs_2_ = bf16[512,512]{1,0:T(8,128)(2,1)S(1)} collective-permute-done((bf16[512,512]{1,0:T(8,128)(2,1)S(1)}, bf16[512,512]{1,0:T(8,128)(2,1)S(1)}, u32[]{:S(2)}, u32[]{:S(2)}) %collective-permute-start.25) | collective-permute-done | bytes 524320 | tf_op jit(solution)/shard_map/ppermute | solution.py:33
  275.8 0.7 collective-permute-done.22.refs_0_
  276.4 3.7 %shard_map.80 = (f32[512,512]{1,0:T(8,128)S(1)}, bf16[4096,512]{1,0:T(8,128)(2,1)S(1)}) custom-call(s32[5]{0:T(128)S(1)} %stack.23.where, bf16[512,512]{1,0:T(8,128)(2,1)S(1)} %shard_map.77.refs_0_, bf16[512,512]{1,0:T(8,128)(2,1)S(1)} %collective-permute-done.27.refs_1_, bf16[512,512]{1,0:T(8,128)(2,1)S(1)} %collective-permute-done.21.refs_2_, ...), custom_call_target="tpu_custom_call" | custom-call | flops 1610612736 | bytes 9437184 | tf_op jit(solution)/shard_map/pallas_call | solution.py:501
  280.1 3.2 %shard_map.81.refs_6_ = f32[512,512]{1,0:T(8,128)S(1)} custom-call(s32[5]{0:T(128)S(1)} %stack.23.where, bf16[512,512]{1,0:T(8,128)(2,1)S(1)} %shard_map.79.refs_0_, bf16[512,512]{1,0:T(8,128)(2,1)S(1)} %collective-permute-done.37.refs_1_, bf16[512,512]{1,0:T(8,128)(2,1)S(1)} %collective-permute-done.38.refs_2_, ...), custom_call_target="tpu_custom_call" | custom-call | flops 1610612736 | bytes 9437184 | tf_op jit(solution)/shard_map/pallas_call | solution.py:501
  283.4 2.2 shard_map.82
  285.7 17.2 %all_to_all.10.sent_ref = bf16[8,128,512]{2,1,0:T(8,128)(2,1)S(1)} all-to-all(bf16[8,128,512]{2,1,0:T(8,128)(2,1)S(1)} %bitcast.7), channel_id=1, replica_groups=mesh['zh'=2,'zl'=2,'y'=2,'x'=2,'c'=2] {'zl','x','c'}, dimensions={0} | all-to-all | bytes 2097152 | tf_op jit(solution)/shard_map/all_to_all | solution.py:523
  302.8 1.3 shard_map.83
  (71 shorter events, 3.1 us)
Async XLA Ops:
  0.0 1.2 copy-start.5
  1.2 0.9 copy-start.6
  2.2 0.9 copy-start.7
  3.1 0.7 copy-start.8
  3.9 1.2 copy-start.2
  5.2 5.4 %copy-start = (bf16[128,4096]{1,0:T(8,128)(2,1)S(1)}, bf16[128,4096]{1,0:T(8,128)(2,1)}, u32[]{:S(2)}) copy-start(bf16[128,4096]{1,0:T(8,128)(2,1)} %tok_ref.1) | copy-start | bytes 3145732
  5.2 5.7 %copy-start.10 = (f32[4096]{0:T(1024)S(1)}, f32[4096]{0:T(1024)}, u32[]{:S(2)}) copy-start(f32[4096]{0:T(1024)} %param.8) | copy-start | bytes 49156
  5.2 27.1 %all-to-all-start = ((bf16[8,136,768]{2,1,0:T(8,128)(2,1)}), bf16[8,136,768]{2,1,0:T(8,128)(2,1)S(1)}, u32[]{:S(2)}, u32[]{:S(2)}) async-start(bf16[8,136,768]{2,1,0:T(8,128)(2,1)} %copy-done.2), calls=%async_computation | async-start | bytes 3342336 | tf_op jit(solution)/shard_map/all_to_all | solution.py:385
  13.5 30.0 %collective-permute-start.6 = (bf16[64,4096]{1,0:T(8,128)(2,1)}, bf16[64,4096]{1,0:T(8,128)(2,1)S(1)}, u32[]{:S(2)}, u32[]{:S(2)}) collective-permute-start(bf16[64,4096]{1,0:T(8,128)(2,1)} %get-tuple-element.32), channel_id=1, source_target_pairs={{0,8},{8,0},{1,9},{9,1},{2,10},{10,2},{3,11},{11,3},{4,12},{12,4},... | collective-permute-start | bytes 1572872 | tf_op jit(solution)/shard_map/ppermute | solution.py:33
  15.5 38.8 %collective-permute-start.8 = (bf16[64,4096]{1,0:T(8,128)(2,1)}, bf16[64,4096]{1,0:T(8,128)(2,1)}, u32[]{:S(2)}, u32[]{:S(2)}) collective-permute-start(bf16[64,4096]{1,0:T(8,128)(2,1)} %get-tuple-element.31), channel_id=1, source_target_pairs={{0,8},{8,0},{1,9},{9,1},{2,10},{10,2},{3,11},{11,3},{4,12},{12,4},... | collective-permute-start | bytes 1572872 | tf_op jit(solution)/shard_map/ppermute | solution.py:33
  32.3 65.2 %collective-permute-start = (bf16[8,136,768]{2,1,0:T(8,128)(2,1)S(1)}, bf16[8,136,768]{2,1,0:T(8,128)(2,1)}, u32[]{:S(2)}, u32[]{:S(2)}) collective-permute-start(bf16[8,136,768]{2,1,0:T(8,128)(2,1)S(1)} %all-to-all-done.refs_12_), channel_id=1, source_target_pairs={{0,4},{4,0},{1,5},{5,1},{2,6},{6,2},{3,7},{7,3},{8,12},{12,8},{9,1... | collective-permute-start | bytes 5013512 | tf_op jit(solution)/shard_map/ppermute | solution.py:33
  43.5 15.5 %collective-permute-start.10 = (bf16[64,4096]{1,0:T(8,128)(2,1)S(1)}, bf16[64,4096]{1,0:T(8,128)(2,1)}, u32[]{:S(2)}, u32[]{:S(2)}) collective-permute-start(bf16[64,4096]{1,0:T(8,128)(2,1)S(1)} %collective-permute-done.6.refs_4_), channel_id=1, source_target_pairs={{0,2},{2,0},{1,3},{3,1},{4,6},{6,4},{5,7},{7,5},{8,10},{10,8},{9,1... | collective-permute-start | bytes 1572872 | tf_op jit(solution)/shard_map/ppermute | solution.py:33
  54.3 15.1 %collective-permute-start.12 = (bf16[64,4096]{1,0:T(8,128)(2,1)}, bf16[64,4096]{1,0:T(8,128)(2,1)}, u32[]{:S(2)}, u32[]{:S(2)}) collective-permute-start(bf16[64,4096]{1,0:T(8,128)(2,1)} %collective-permute-done.8.refs_6_), channel_id=1, source_target_pairs={{0,2},{2,0},{1,3},{3,1},{4,6},{6,4},{5,7},{7,5},{8,10},{10,8},{9,1... | collective-permute-start | bytes 1572872 | tf_op jit(solution)/shard_map/ppermute | solution.py:33
  55.7 34.7 %collective-permute-start.4 = (bf16[128,4096]{1,0:T(8,128)(2,1)S(1)}, bf16[128,4096]{1,0:T(8,128)(2,1)}, u32[]{:S(2)}, u32[]{:S(2)}) collective-permute-start(bf16[128,4096]{1,0:T(8,128)(2,1)S(1)} %fusion.2.refs_0_), channel_id=1, source_target_pairs={{0,2},{2,0},{1,3},{3,1},{4,6},{6,4},{5,7},{7,5},{8,10},{10,8},{9,1... | collective-permute-start | bytes 3145736 | tf_op jit(solution)/shard_map/ppermute | solution.py:33
  56.3 26.5 %collective-permute-start.1 = (bf16[8,136,256]{2,1,0:T(8,128)(2,1)S(1)}, bf16[8,136,256]{2,1,0:T(8,128)(2,1)}, u32[]{:S(2)}, u32[]{:S(2)}) collective-permute-start(bf16[8,136,256]{2,1,0:T(8,128)(2,1)S(1)} %slice.46), channel_id=1, source_target_pairs={{0,16},{16,0},{1,17},{17,1},{2,18},{18,2},{3,19},{19,3},{4,20},{20... | collective-permute-start | bytes 1671176 | tf_op jit(solution)/shard_map/ppermute | solution.py:33
  59.0 25.4 %collective-permute-start.7 = (bf16[64,4096]{1,0:T(8,128)(2,1)S(1)}, bf16[64,4096]{1,0:T(8,128)(2,1)S(1)}, u32[]{:S(2)}, u32[]{:S(2)}) collective-permute-start(bf16[64,4096]{1,0:T(8,128)(2,1)S(1)} %collective-permute-done.6.refs_4_), channel_id=1, source_target_pairs={{0,1},{1,0},{2,3},{3,2},{4,5},{5,4},{6,7},{7,6},{8,9},{9,8},{10,11... | collective-permute-start | bytes 1572872 | tf_op jit(solution)/shard_map/ppermute | solution.py:33
  69.4 22.7 %collective-permute-start.3 = (bf16[128,4096]{1,0:T(8,128)(2,1)S(1)}, bf16[128,4096]{1,0:T(8,128)(2,1)}, u32[]{:S(2)}, u32[]{:S(2)}) collective-permute-start(bf16[128,4096]{1,0:T(8,128)(2,1)S(1)} %fusion.2.refs_0_), channel_id=1, source_target_pairs={{0,1},{1,0},{2,3},{3,2},{4,5},{5,4},{6,7},{7,6},{8,9},{9,8},{10,11... | collective-permute-start | bytes 3145736 | tf_op jit(solution)/shard_map/ppermute | solution.py:33
  82.9 14.6 %collective-permute-start.2 = (bf16[8,136,256]{2,1,0:T(8,128)(2,1)}, bf16[8,136,256]{2,1,0:T(8,128)(2,1)}, u32[]{:S(2)}, u32[]{:S(2)}) collective-permute-start(bf16[8,136,256]{2,1,0:T(8,128)(2,1)} %collective-permute-done.1.refs_14_), channel_id=1, source_target_pairs={{0,4},{4,0},{1,5},{5,1},{2,6},{6,2},{3,7},{7,3},{8,12},{12,8},{9,1... | collective-permute-start | bytes 1671176 | tf_op jit(solution)/shard_map/ppermute | solution.py:33
  84.4 0.8 copy-start.3
  85.2 6.4 %collective-permute-start.9 = (bf16[64,4096]{1,0:T(8,128)(2,1)}, bf16[64,4096]{1,0:T(8,128)(2,1)}, u32[]{:S(2)}, u32[]{:S(2)}) collective-permute-start(bf16[64,4096]{1,0:T(8,128)(2,1)} %collective-permute-done.8.refs_6_), channel_id=1, source_target_pairs={{0,1},{1,0},{2,3},{3,2},{4,5},{5,4},{6,7},{7,6},{8,9},{9,8},{10,11... | collective-permute-start | bytes 1572872 | tf_op jit(solution)/shard_map/ppermute | solution.py:33
  90.4 55.5 %collective-permute-start.5 = (bf16[128,4096]{1,0:T(8,128)(2,1)}, bf16[128,4096]{1,0:T(8,128)(2,1)}, u32[]{:S(2)}, u32[]{:S(2)}) collective-permute-start(bf16[128,4096]{1,0:T(8,128)(2,1)} %collective-permute-done.4.refs_2_), channel_id=1, source_target_pairs={{0,1},{1,0},{2,3},{3,2},{4,5},{5,4},{6,7},{7,6},{8,9},{9,8},{10,11... | collective-permute-start | bytes 3145736 | tf_op jit(solution)/shard_map/ppermute | solution.py:33
  91.5 54.4 %collective-permute-start.11 = (bf16[64,4096]{1,0:T(8,128)(2,1)}, bf16[64,4096]{1,0:T(8,128)(2,1)}, u32[]{:S(2)}, u32[]{:S(2)}) collective-permute-start(bf16[64,4096]{1,0:T(8,128)(2,1)} %collective-permute-done.10.refs_8_), channel_id=1, source_target_pairs={{0,1},{1,0},{2,3},{3,2},{4,5},{5,4},{6,7},{7,6},{8,9},{9,8},{10,11... | collective-permute-start | bytes 1572872 | tf_op jit(solution)/shard_map/ppermute | solution.py:33
  92.0 53.9 %collective-permute-start.13 = (bf16[64,4096]{1,0:T(8,128)(2,1)}, bf16[64,4096]{1,0:T(8,128)(2,1)}, u32[]{:S(2)}, u32[]{:S(2)}) collective-permute-start(bf16[64,4096]{1,0:T(8,128)(2,1)} %collective-permute-done.12.refs_10_), channel_id=1, source_target_pairs={{0,1},{1,0},{2,3},{3,2},{4,5},{5,4},{6,7},{7,6},{8,9},{9,8},{10,11... | collective-permute-start | bytes 1572872 | tf_op jit(solution)/shard_map/ppermute | solution.py:33
  97.5 35.8 %collective-permute-start.14 = (bf16[8,128,256]{2,1,0:T(8,128)(2,1)}, bf16[8,128,256]{2,1,0:T(8,128)(2,1)}, u32[]{:S(2)}, u32[]{:S(2)}) collective-permute-start(bf16[8,128,256]{2,1,0:T(8,128)(2,1)} %get-tuple-element.28), channel_id=1, source_target_pairs={{0,16},{16,0},{1,17},{17,1},{2,18},{18,2},{3,19},{19,3},{4,20},{20... | collective-permute-start | bytes 1572872 | tf_op jit(solution)/shard_map/ppermute | solution.py:33
  97.5 46.9 %collective-permute-start.15 = (bf16[8,128,256]{2,1,0:T(8,128)(2,1)}, bf16[8,128,256]{2,1,0:T(8,128)(2,1)}, u32[]{:S(2)}, u32[]{:S(2)}) collective-permute-start(bf16[8,128,256]{2,1,0:T(8,128)(2,1)} %get-tuple-element.27), channel_id=1, source_target_pairs={{0,16},{16,0},{1,17},{17,1},{2,18},{18,2},{3,19},{19,3},{4,20},{20... | collective-permute-start | bytes 1572872 | tf_op jit(solution)/shard_map/ppermute | solution.py:33
  100.5 45.4 %copy-start.4 = (bf16[64,4096]{1,0:T(8,128)(2,1)S(1)}, bf16[64,4096]{1,0:T(8,128)(2,1)}, u32[]{:S(2)}) copy-start(bf16[64,4096]{1,0:T(8,128)(2,1)} %copy-done.3) | copy-start | bytes 1572868
  133.3 24.3 %collective-permute-start.16 = (bf16[8,128,256]{2,1,0:T(8,128)(2,1)}, bf16[8,128,256]{2,1,0:T(8,128)(2,1)S(1)}, u32[]{:S(2)}, u32[]{:S(2)}) collective-permute-start(bf16[8,128,256]{2,1,0:T(8,128)(2,1)} %collective-permute-done.14.refs_14_), channel_id=1, source_target_pairs={{0,4},{4,0},{1,5},{5,1},{2,6},{6,2},{3,7},{7,3},{8,12},{12,8},{9,1... | collective-permute-start | bytes 1572872 | tf_op jit(solution)/shard_map/ppermute | solution.py:33
  144.4 14.1 %collective-permute-start.17 = (bf16[8,128,256]{2,1,0:T(8,128)(2,1)}, bf16[8,128,256]{2,1,0:T(8,128)(2,1)S(1)}, u32[]{:S(2)}, u32[]{:S(2)}) collective-permute-start(bf16[8,128,256]{2,1,0:T(8,128)(2,1)} %collective-permute-done.15.refs_15_), channel_id=1, source_target_pairs={{0,4},{4,0},{1,5},{5,1},{2,6},{6,2},{3,7},{7,3},{8,12},{12,8},{9,1... | collective-permute-start | bytes 1572872 | tf_op jit(solution)/shard_map/ppermute | solution.py:33
  146.0 8.5 %copy-start.9 = (bf16[4096,128]{1,0:T(8,128)(2,1)S(1)}, bf16[4096,128]{1,0:T(8,128)(2,1)}, u32[]{:S(2)}) copy-start(bf16[4096,128]{1,0:T(8,128)(2,1)} %param.12) | copy-start | bytes 3145732
  154.4 47.6 %collective-permute-start.18 = (bf16[1024,256]{1,0:T(8,128)(2,1)S(1)}, bf16[1024,256]{1,0:T(8,128)(2,1)S(1)}, u32[]{:S(2)}, u32[]{:S(2)}) collective-permute-start(bf16[1024,256]{1,0:T(8,128)(2,1)S(1)} %get-tuple-element.18.kv_own), channel_id=1, source_target_pairs={{0,16},{16,0},{1,17},{17,1},{2,18},{18,2},{3,19},{19,3},{4,20},{20... | collective-permute-start | bytes 1572872 | tf_op jit(solution)/shard_map/ppermute | solution.py:33
  154.6 58.7 %collective-permute-start.32 = (bf16[2048,128]{1,0:T(8,128)(2,1)S(1)}, bf16[2048,128]{1,0:T(8,128)(2,1)S(1)}, u32[]{:S(2)}, u32[]{:S(2)}) collective-permute-start(bf16[2048,128]{1,0:T(8,128)(2,1)S(1)} %get-tuple-element.30.refs_6_), channel_id=1, source_target_pairs={{0,16},{16,0},{1,17},{17,1},{2,18},{18,2},{3,19},{19,3},{4,20},{20... | collective-permute-start | bytes 1572872 | tf_op jit(solution)/shard_map/ppermute | solution.py:33
  157.5 66.9 %collective-permute-start.35 = (bf16[2048,128]{1,0:T(8,128)(2,1)S(1)}, bf16[2048,128]{1,0:T(8,128)(2,1)S(1)}, u32[]{:S(2)}, u32[]{:S(2)}) collective-permute-start(bf16[2048,128]{1,0:T(8,128)(2,1)S(1)} %get-tuple-element.29.refs_10_), channel_id=1, source_target_pairs={{0,16},{16,0},{1,17},{17,1},{2,18},{18,2},{3,19},{19,3},{4,20},{20... | collective-permute-start | bytes 1572872 | tf_op jit(solution)/shard_map/ppermute | solution.py:33
  157.6 67.3 %collective-permute-start.20 = (bf16[1024,256]{1,0:T(8,128)(2,1)S(1)}, bf16[1024,256]{1,0:T(8,128)(2,1)S(1)}, u32[]{:S(2)}, u32[]{:S(2)}) collective-permute-start(bf16[1024,256]{1,0:T(8,128)(2,1)S(1)} %get-tuple-element.18.kv_own), channel_id=1, source_target_pairs={{0,4},{4,0},{1,5},{5,1},{2,6},{6,2},{3,7},{7,3},{8,12},{12,8},{9,1... | collective-permute-start | bytes 1572872 | tf_op jit(solution)/shard_map/ppermute | solution.py:33
  158.5 80.9 %collective-permute-start.31 = (bf16[2048,128]{1,0:T(8,128)(2,1)S(1)}, bf16[2048,128]{1,0:T(8,128)(2,1)S(1)}, u32[]{:S(2)}, u32[]{:S(2)}) collective-permute-start(bf16[2048,128]{1,0:T(8,128)(2,1)S(1)} %get-tuple-element.30.refs_6_), channel_id=1, source_target_pairs={{0,4},{4,0},{1,5},{5,1},{2,6},{6,2},{3,7},{7,3},{8,12},{12,8},{9,1... | collective-permute-start | bytes 1572872 | tf_op jit(solution)/shard_map/ppermute | solution.py:33
  202.0 34.8 %collective-permute-start.19 = (bf16[1024,256]{1,0:T(8,128)(2,1)S(1)}, bf16[1024,256]{1,0:T(8,128)(2,1)S(1)}, u32[]{:S(2)}, u32[]{:S(2)}) collective-permute-start(bf16[1024,256]{1,0:T(8,128)(2,1)S(1)} %collective-permute-done.18.kv_z), channel_id=1, source_target_pairs={{0,4},{4,0},{1,5},{5,1},{2,6},{6,2},{3,7},{7,3},{8,12},{12,8},{9,1... | collective-permute-start | bytes 1572872 | tf_op jit(solution)/shard_map/ppermute | solution.py:33
  213.3 27.4 %collective-permute-start.34 = (bf16[2048,128]{1,0:T(8,128)(2,1)S(1)}, bf16[2048,128]{1,0:T(8,128)(2,1)S(1)}, u32[]{:S(2)}, u32[]{:S(2)}) collective-permute-start(bf16[2048,128]{1,0:T(8,128)(2,1)S(1)} %get-tuple-element.29.refs_10_), channel_id=1, source_target_pairs={{0,4},{4,0},{1,5},{5,1},{2,6},{6,2},{3,7},{7,3},{8,12},{12,8},{9,1... | collective-permute-start | bytes 1572872 | tf_op jit(solution)/shard_map/ppermute | solution.py:33
  224.4 18.4 %collective-permute-start.33 = (bf16[2048,128]{1,0:T(8,128)(2,1)S(1)}, bf16[2048,128]{1,0:T(8,128)(2,1)S(1)}, u32[]{:S(2)}, u32[]{:S(2)}) collective-permute-start(bf16[2048,128]{1,0:T(8,128)(2,1)S(1)} %collective-permute-done.32.refs_8_), channel_id=1, source_target_pairs={{0,4},{4,0},{1,5},{5,1},{2,6},{6,2},{3,7},{7,3},{8,12},{12,8},{9,1... | collective-permute-start | bytes 1572872 | tf_op jit(solution)/shard_map/ppermute | solution.py:33
  224.9 24.6 %collective-permute-start.36 = (bf16[2048,128]{1,0:T(8,128)(2,1)S(1)}, bf16[2048,128]{1,0:T(8,128)(2,1)S(1)}, u32[]{:S(2)}, u32[]{:S(2)}) collective-permute-start(bf16[2048,128]{1,0:T(8,128)(2,1)S(1)} %collective-permute-done.35.refs_12_), channel_id=1, source_target_pairs={{0,4},{4,0},{1,5},{5,1},{2,6},{6,2},{3,7},{7,3},{8,12},{12,8},{9,1... | collective-permute-start | bytes 1572872 | tf_op jit(solution)/shard_map/ppermute | solution.py:33
  238.2 13.7 %collective-permute-start.21 = (bf16[512,512]{1,0:T(8,128)(2,1)S(1)}, bf16[512,512]{1,0:T(8,128)(2,1)S(1)}, u32[]{:S(2)}, u32[]{:S(2)}) collective-permute-start(bf16[512,512]{1,0:T(8,128)(2,1)S(1)} %shard_map.77.refs_0_), channel_id=1, source_target_pairs={{0,2},{2,0},{1,3},{3,1},{4,6},{6,4},{5,7},{7,5},{8,10},{10,8},{9,1... | collective-permute-start | bytes 1572872 | tf_op jit(solution)/shard_map/ppermute | solution.py:33
  239.4 14.8 %collective-permute-start.29 = (bf16[512,512]{1,0:T(8,128)(2,1)S(1)}, bf16[512,512]{1,0:T(8,128)(2,1)S(1)}, u32[]{:S(2)}, u32[]{:S(2)}) collective-permute-start(bf16[512,512]{1,0:T(8,128)(2,1)S(1)} %shard_map.77.refs_0_), channel_id=1, source_target_pairs={{0,8},{8,0},{1,9},{9,1},{2,10},{10,2},{3,11},{11,3},{4,12},{12,4},... | collective-permute-start | bytes 1572872 | tf_op jit(solution)/shard_map/ppermute | solution.py:33
  240.7 22.9 %collective-permute-start.24 = (bf16[512,512]{1,0:T(8,128)(2,1)S(1)}, bf16[512,512]{1,0:T(8,128)(2,1)S(1)}, u32[]{:S(2)}, u32[]{:S(2)}) collective-permute-start(bf16[512,512]{1,0:T(8,128)(2,1)S(1)} %shard_map.79.refs_0_), channel_id=1, source_target_pairs={{0,8},{8,0},{1,9},{9,1},{2,10},{10,2},{3,11},{11,3},{4,12},{12,4},... | collective-permute-start | bytes 1572872 | tf_op jit(solution)/shard_map/ppermute | solution.py:33
  242.8 21.8 %collective-permute-start.27 = (bf16[512,512]{1,0:T(8,128)(2,1)S(1)}, bf16[512,512]{1,0:T(8,128)(2,1)S(1)}, u32[]{:S(2)}, u32[]{:S(2)}) collective-permute-start(bf16[512,512]{1,0:T(8,128)(2,1)S(1)} %shard_map.77.refs_0_), channel_id=1, source_target_pairs={{0,1},{1,0},{2,3},{3,2},{4,5},{5,4},{6,7},{7,6},{8,9},{9,8},{10,11... | collective-permute-start | bytes 1572872 | tf_op jit(solution)/shard_map/ppermute | solution.py:33
  249.5 15.3 %collective-permute-start.38 = (bf16[512,512]{1,0:T(8,128)(2,1)S(1)}, bf16[512,512]{1,0:T(8,128)(2,1)S(1)}, u32[]{:S(2)}, u32[]{:S(2)}) collective-permute-start(bf16[512,512]{1,0:T(8,128)(2,1)S(1)} %shard_map.79.refs_0_), channel_id=1, source_target_pairs={{0,2},{2,0},{1,3},{3,1},{4,6},{6,4},{5,7},{7,5},{8,10},{10,8},{9,1... | collective-permute-start | bytes 1572872 | tf_op jit(solution)/shard_map/ppermute | solution.py:33
  251.9 13.0 %collective-permute-start.28 = (bf16[512,512]{1,0:T(8,128)(2,1)S(1)}, bf16[512,512]{1,0:T(8,128)(2,1)S(1)}, u32[]{:S(2)}, u32[]{:S(2)}) collective-permute-start(bf16[512,512]{1,0:T(8,128)(2,1)S(1)} %collective-permute-done.21.refs_2_), channel_id=1, source_target_pairs={{0,1},{1,0},{2,3},{3,2},{4,5},{5,4},{6,7},{7,6},{8,9},{9,8},{10,11... | collective-permute-start | bytes 1572872 | tf_op jit(solution)/shard_map/ppermute | solution.py:33
  254.2 11.2 %collective-permute-start.30 = (bf16[512,512]{1,0:T(8,128)(2,1)S(1)}, bf16[512,512]{1,0:T(8,128)(2,1)S(1)}, u32[]{:S(2)}, u32[]{:S(2)}) collective-permute-start(bf16[512,512]{1,0:T(8,128)(2,1)S(1)} %collective-permute-done.29.refs_4_), channel_id=1, source_target_pairs={{0,1},{1,0},{2,3},{3,2},{4,5},{5,4},{6,7},{7,6},{8,9},{9,8},{10,11... | collective-permute-start | bytes 1572872 | tf_op jit(solution)/shard_map/ppermute | solution.py:33
  263.6 12.2 %collective-permute-start.25 = (bf16[512,512]{1,0:T(8,128)(2,1)S(1)}, bf16[512,512]{1,0:T(8,128)(2,1)S(1)}, u32[]{:S(2)}, u32[]{:S(2)}) collective-permute-start(bf16[512,512]{1,0:T(8,128)(2,1)S(1)} %collective-permute-done.24.refs_4_), channel_id=1, source_target_pairs={{0,2},{2,0},{1,3},{3,1},{4,6},{6,4},{5,7},{7,5},{8,10},{10,8},{9,1... | collective-permute-start | bytes 1572872 | tf_op jit(solution)/shard_map/ppermute | solution.py:33
  264.6 11.9 %collective-permute-start.22 = (bf16[512,512]{1,0:T(8,128)(2,1)S(1)}, bf16[512,512]{1,0:T(8,128)(2,1)S(1)}, u32[]{:S(2)}, u32[]{:S(2)}) collective-permute-start(bf16[512,512]{1,0:T(8,128)(2,1)S(1)} %collective-permute-done.21.refs_2_), channel_id=1, source_target_pairs={{0,8},{8,0},{1,9},{9,1},{2,10},{10,2},{3,11},{11,3},{4,12},{12,4},... | collective-permute-start | bytes 1572872 | tf_op jit(solution)/shard_map/ppermute | solution.py:33
  264.8 15.3 %collective-permute-start.37 = (bf16[512,512]{1,0:T(8,128)(2,1)S(1)}, bf16[512,512]{1,0:T(8,128)(2,1)S(1)}, u32[]{:S(2)}, u32[]{:S(2)}) collective-permute-start(bf16[512,512]{1,0:T(8,128)(2,1)S(1)} %shard_map.79.refs_0_), channel_id=1, source_target_pairs={{0,1},{1,0},{2,3},{3,2},{4,5},{5,4},{6,7},{7,6},{8,9},{9,8},{10,11... | collective-permute-start | bytes 1572872 | tf_op jit(solution)/shard_map/ppermute | solution.py:33
  264.9 15.3 %collective-permute-start.39 = (bf16[512,512]{1,0:T(8,128)(2,1)S(1)}, bf16[512,512]{1,0:T(8,128)(2,1)S(1)}, u32[]{:S(2)}, u32[]{:S(2)}) collective-permute-start(bf16[512,512]{1,0:T(8,128)(2,1)S(1)} %collective-permute-done.38.refs_2_), channel_id=1, source_target_pairs={{0,1},{1,0},{2,3},{3,2},{4,5},{5,4},{6,7},{7,6},{8,9},{9,8},{10,11... | collective-permute-start | bytes 1572872 | tf_op jit(solution)/shard_map/ppermute | solution.py:33
  265.4 14.8 %collective-permute-start.40 = (bf16[512,512]{1,0:T(8,128)(2,1)S(1)}, bf16[512,512]{1,0:T(8,128)(2,1)S(1)}, u32[]{:S(2)}, u32[]{:S(2)}) collective-permute-start(bf16[512,512]{1,0:T(8,128)(2,1)S(1)} %collective-permute-done.24.refs_4_), channel_id=1, source_target_pairs={{0,1},{1,0},{2,3},{3,2},{4,5},{5,4},{6,7},{7,6},{8,9},{9,8},{10,11... | collective-permute-start | bytes 1572872 | tf_op jit(solution)/shard_map/ppermute | solution.py:33
  275.8 7.6 %collective-permute-start.26 = (bf16[512,512]{1,0:T(8,128)(2,1)S(1)}, bf16[512,512]{1,0:T(8,128)(2,1)S(1)}, u32[]{:S(2)}, u32[]{:S(2)}) collective-permute-start(bf16[512,512]{1,0:T(8,128)(2,1)S(1)} %collective-permute-done.25.refs_2_), channel_id=1, source_target_pairs={{0,1},{1,0},{2,3},{3,2},{4,5},{5,4},{6,7},{7,6},{8,9},{9,8},{10,11... | collective-permute-start | bytes 1572872 | tf_op jit(solution)/shard_map/ppermute | solution.py:33
  276.4 7.0 %collective-permute-start.23 = (bf16[512,512]{1,0:T(8,128)(2,1)S(1)}, bf16[512,512]{1,0:T(8,128)(2,1)S(1)}, u32[]{:S(2)}, u32[]{:S(2)}) collective-permute-start(bf16[512,512]{1,0:T(8,128)(2,1)S(1)} %collective-permute-done.22.refs_0_), channel_id=1, source_target_pairs={{0,1},{1,0},{2,3},{3,2},{4,5},{5,4},{6,7},{7,6},{8,9},{9,8},{10,11... | collective-permute-start | bytes 1572872 | tf_op jit(solution)/shard_map/ppermute | solution.py:33
  285.7 17.2 %copy-start.1 = (bf16[128,4096]{1,0:T(8,128)(2,1)S(1)}, bf16[128,4096]{1,0:T(8,128)(2,1)}, u32[]{:S(2)}) copy-start(bf16[128,4096]{1,0:T(8,128)(2,1)} %tok_ref.1) | copy-start | bytes 3145732

commit v5 on v4

--- a/solution.py
+++ b/solution.py
@@ -27,6 +27,7 @@
 ANY = pl.BlockSpec(memory_space=pl.ANY)
 VMEM = pl.BlockSpec(memory_space=pltpu.VMEM)
 SMEM = pl.BlockSpec(memory_space=pltpu.SMEM)
+HBM = pl.BlockSpec(memory_space=pltpu.HBM)
 
 
 def swap(value, axis):
@@ -66,15 +67,19 @@
     return pl.multiple_of(value, step)
 
 
-def layout_kernel(wq_ref, wk_ref, wv_ref, doc_ref, out_ref):
+def layout_kernel(wq_ref, wk_ref, wv_ref, doc_ref, out_ref, sems):
+    copies = []
+    for j in range(8):
+        for ref, first, size in ((wq_ref, 0, 512), (wk_ref, 512, 128), (wv_ref, 640, 128)):
+            target = out_ref.at[j, pl.ds(0, 128), pl.ds(first, size)]
+            copies.append((ref.at[:, pl.ds(size * j, size)], target))
+    started = start_copies(copies, sems)
     below = doc_ref[...] < lax.broadcasted_iota(jnp.int32, (EXTRA, 128), 0)
     count = jnp.sum(jnp.where(below, 1.0, 0.0), axis=1, keepdims=True)
     rows = jnp.broadcast_to(count, (EXTRA, 768)).astype(jnp.bfloat16)
     for j in range(8):
-        out_ref[j, :128, :512] = wq_ref[:, 512 * j : 512 * j + 512]
-        out_ref[j, :128, 512:640] = wk_ref[:, 128 * j : 128 * j + 128]
-        out_ref[j, :128, 640:] = wv_ref[:, 128 * j : 128 * j + 128]
         out_ref[j, 128:, :] = rows
+    wait_all(started)
 
 
 TOKEN_PIECES = [
@@ -159,30 +164,58 @@
 
 def project_q_kernel(where, *refs):
     tok_refs = refs[:12]
-    w_own, w_y, w_z0, w_z1, w_zy0, w_zy1, cos_ref, sin_ref = refs[12:20]
-    q_out, xs, wq, sems = refs[20:]
-    whole, left, right = pl.ds(0, 512), pl.ds(0, 256), pl.ds(256, 256)
+    w_own, w_y, w_z0, w_z1, w_z2, w_zy0, cos_ref, sin_ref = refs[12:20]
+    q_out, part_out, xs, wq, sems = refs[20:]
+    whole, left = pl.ds(0, 512), pl.ds(0, 256)
+    slim = pl.ds(0, 128)
     near = start_copies(token_copies(0, where, tok_refs, xs), sems)
     pieces = (
         (0, 0, w_own, whole, whole),
         (0, 1, w_y, whole, whole),
         (1, 0, w_z0, left, left),
+        (1, 0, w_z1, slim, pl.ds(256, 128)),
+        (1, 0, w_z2, slim, pl.ds(384, 128)),
         (1, 1, w_zy0, left, left),
-        (1, 0, w_z1, left, right),
-        (1, 1, w_zy1, left, right),
     )
     near += start_copies(weight_copies(where, pieces, wq), sems, 4)
     far = start_copies(token_copies(1, where, tok_refs, xs), sems, 16)
+    for zlp in range(2):
+        block = 4 * (where[0] ^ 1) + 2 * zlp + (where[2] ^ 1)
+        wq[pl.ds(4 * block, 4), :, 256:] = jnp.zeros((4, 128, 256), jnp.bfloat16)
     for dzl, waits in enumerate((near, far)):
         wait_all(waits)
         rows = pl.ds(aligned((where[1] ^ dzl) * 512, 512), 512)
-        for n in range(2):
-            weights = wq[:, :, 256 * n : 256 * n + 256].reshape(4096, 256)
-            acc = jnp.dot(xs[rows, :], weights, preferred_element_type=jnp.float32)
-            for k in range(2):
-                part = turn(acc[:, 128 * k : 128 * k + 128], cos_ref, sin_ref, rows)
-                columns = slice(256 * n + 128 * k, 256 * n + 128 * k + 128)
-                q_out[rows, columns] = part.astype(jnp.bfloat16)
+        weights = wq[:, :, :256].reshape(4096, 256)
+        acc = jnp.dot(xs[rows, :], weights, preferred_element_type=jnp.float32)
+        for k in range(2):
+            columns = slice(128 * k, 128 * k + 128)
+            part = turn(acc[:, columns], cos_ref, sin_ref, rows)
+            q_out[rows, columns] = part.astype(jnp.bfloat16)
+        weights = wq[:, :, 256:].reshape(4096, 256)
+        part_out[rows, :] = jnp.dot(xs[rows, :], weights, preferred_element_type=jnp.float32)
+
+
+def project_rest_kernel(where, *refs):
+    tok_refs, (w_zy1, w_zy2, part_ref, cos_ref, sin_ref) = refs[:12], refs[12:17]
+    q_out, xs, wq, sems = refs[17:]
+    copies = [(w_zy1, wq.at[:, :, pl.ds(0, 128)]), (w_zy2, wq.at[:, :, pl.ds(128, 128)])]
+    for dzl in range(2):
+        for ref, target in token_copies(dzl, where, tok_refs, xs):
+            copies.append((ref, target))
+    split = copies[:2]
+    for ref, target in copies[2:]:
+        for zlp in range(2):
+            block = 4 * (where[0] ^ 1) + 2 * zlp + (where[2] ^ 1)
+            source = ref.at[:, pl.ds(aligned(block * 512, 512), 512)]
+            split.append((source, target.at[:, pl.ds(512 * zlp, 512)]))
+    wait_all(start_copies(split, sems))
+    acc = part_ref[...] + jnp.dot(
+        xs[...], wq[...].reshape(1024, 256), preferred_element_type=jnp.float32
+    )
+    for k in range(2):
+        columns = slice(128 * k, 128 * k + 128)
+        part = turn(acc[:, columns], cos_ref, sin_ref, slice(None))
+        q_out[:, columns] = part.astype(jnp.bfloat16)
 
 
 FACTOR = math.log2(math.e) / math.sqrt(HEAD_WIDTH)
@@ -222,11 +255,11 @@
     acc[...] = acc[...] * shrink + jnp.dot(weights, values, preferred_element_type=jnp.float32)
 
 
-def stacked(q_ref):
-    return jnp.concatenate([q_ref[:, 128 * h : 128 * h + 128] for h in range(4)], axis=0)
-
-
-def near_kernel(half, where, bounds, q_ref, start_ref, kv_own, kv_y, *refs):
+def stacked(*q_refs):
+    return jnp.concatenate([ref[:, 128 * h : 128 * h + 128] for ref in q_refs for h in range(2)])
+
+
+def near_kernel(half, where, bounds, q_ref, q2_ref, start_ref, kv_own, kv_y, *refs):
     top, total, acc, ks, vs, sems = refs
     zh, y = where[0], where[2]
     tile = 2 * half + pl.program_id(0)
@@ -252,14 +285,14 @@
             key_pos = block * KT + lax.broadcasted_iota(jnp.int32, (QT, KT), 1)
             query_pos = first + lax.broadcasted_iota(jnp.int32, (QT, KT), 0)
             mask = (key_pos <= query_pos) & (key_pos >= start_ref[:, :1])
-            attend_step(stacked(q_ref), ks[keys, :], vs[keys, :], state, mask)
+            attend_step(stacked(q_ref, q2_ref), ks[keys, :], vs[keys, :], state, mask)
 
         @pl.when(jnp.logical_not(edge))
         def _():
-            attend_step(stacked(q_ref), ks[keys, :], vs[keys, :], state, None)
-
-
-def far_kernel(half, where, bounds, q_ref, start_ref, kv_z, kv_zy, *refs):
+            attend_step(stacked(q_ref, q2_ref), ks[keys, :], vs[keys, :], state, None)
+
+
+def far_kernel(half, where, bounds, q_ref, q2_ref, start_ref, kv_z, kv_zy, *refs):
     top_in, total_in, acc_in, out_ref, ks, vs, top, total, acc, sems = refs
     zh, y = where[0], where[2]
     tile = 2 * half + pl.program_id(0)
@@ -281,11 +314,11 @@
         def _():
             key_pos = block * KT + lax.broadcasted_iota(jnp.int32, (QT, KT), 1)
             mask = key_pos >= start_ref[:, :1]
-            attend_step(stacked(q_ref), ks[keys, :], vs[keys, :], (top, total, acc), mask)
+            attend_step(stacked(q_ref, q2_ref), ks[keys, :], vs[keys, :], (top, total, acc), mask)
 
         @pl.when(jnp.logical_not(edge))
         def _():
-            attend_step(stacked(q_ref), ks[keys, :], vs[keys, :], (top, total, acc), None)
+            attend_step(stacked(q_ref, q2_ref), ks[keys, :], vs[keys, :], (top, total, acc), None)
 
     result = acc[...] / jnp.sum(total[...], axis=1, keepdims=True)
     for h in range(4):
@@ -378,16 +411,17 @@
     weights = call(
         layout_kernel,
         jax.ShapeDtypeStruct((8, 128 + EXTRA, 768), bf16),
-        [VMEM] * 4,
-        [],
+        [HBM] * 3 + [VMEM],
+        [pltpu.SemaphoreType.DMA((24,))],
         (128 * EXTRA, 3 << 20),
     )(wq, wk, wv, doc_ids.reshape(1, 128))
     weights = lax.all_to_all(weights, QUAD, 0, 0, tiled=True)
     w_y = swap(weights, "y")
     wkv_z = swap(weights[:, :, 512:], "zh")
     wkv_zy = swap(wkv_z, "y")
-    wq_z = [swap(weights[:, :128, 256 * n : 256 * n + 256], "zh") for n in range(2)]
-    wq_zy = [swap(wq_z[n], "y") for n in range(2)]
+    cuts = [slice(0, 256), slice(256, 384), slice(384, 512)]
+    wq_z = [swap(weights[:, :128, cut], "zh") for cut in cuts]
+    wq_zy = [swap(piece, "y") for piece in wq_z]
 
     source = tokens.astype(f32)
     mean_sq = jnp.mean(source * source, axis=1, keepdims=True)
@@ -426,9 +460,9 @@
         (2 * 1024 * 4096 * 256, 11 << 20),
         out_specs=(VMEM, VMEM, SMEM),
     )(where, counts, *tok, weights, w_y, wkv_z, wkv_zy, cosine, sine)
-    queries = call(
+    first_queries, part = call(
         project_q_kernel,
-        jax.ShapeDtypeStruct((1024, 512), bf16),
+        (jax.ShapeDtypeStruct((1024, 256), bf16), jax.ShapeDtypeStruct((1024, 256), f32)),
         [SMEM] + [ANY] * 18 + [VMEM, VMEM],
         [
             pltpu.VMEM((1024, 4096), bf16),
@@ -436,7 +470,19 @@
             pltpu.SemaphoreType.DMA((24,)),
         ],
         (2 * 1024 * 4096 * 512, 14 << 20),
-    )(where, *tok, weights, w_y, *wq_z, *wq_zy, cosine, sine)
+    )(where, *tok, weights, w_y, *wq_z, wq_zy[0], cosine, sine)
+    rest_queries = call(
+        project_rest_kernel,
+        jax.ShapeDtypeStruct((1024, 256), bf16),
+        [SMEM] + [ANY] * 14 + [VMEM] * 3,
+        [
+            pltpu.VMEM((1024, 1024), bf16),
+            pltpu.VMEM((8, 128, 256), bf16),
+            pltpu.SemaphoreType.DMA((26,)),
+        ],
+        (2 * 1024 * 1024 * 256, 5 << 20),
+    )(where, *tok, *wq_zy[1:], part, cosine, sine)
+    queries = (first_queries, rest_queries)
 
     kv_y = swap(keys_values, "y")
     kv_z = swap(keys_values, "zh")
@@ -453,7 +499,8 @@
             functools.partial(near_kernel, half),
             [jax.ShapeDtypeStruct((2, 4 * QT, 128), f32)] * 3,
             [SMEM] * 2
-            + [tile_spec((QT, 512), 2 * half), tile_spec((QT, 128), 2 * half), ANY, ANY],
+            + [tile_spec((QT, 256), 2 * half), tile_spec((QT, 256), 2 * half),
+            tile_spec((QT, 128), 2 * half), ANY, ANY],
             [
                 pltpu.VMEM((2048, 128), bf16),
                 pltpu.VMEM((2048, 128), bf16),
@@ -462,7 +509,7 @@
             (4 * 512 * 2048 * 512, 4 << 20),
             grid=(2,),
             out_specs=state_specs(),
-        )(where, bounds, queries, start_col, keys_values, kv_y)
+        )(where, bounds, *queries, start_col, keys_values, kv_y)
 
     state = [near_half(0), near_half(1)]
 
@@ -470,7 +517,8 @@
         return call(
             functools.partial(far_kernel, half),
             jax.ShapeDtypeStruct((512, 512), bf16),
-            [SMEM, SMEM, tile_spec((QT, 512), 2 * half), tile_spec((QT, 128), 2 * half)]
+            [SMEM, SMEM, tile_spec((QT, 256), 2 * half), tile_spec((QT, 256), 2 * half),
+                tile_spec((QT, 128), 2 * half)]
             + [ANY, ANY] + state_specs(),
             [
                 pltpu.VMEM((2048, 128), bf16),
@@ -483,7 +531,7 @@
             (4 * 512 * 2048 * 512, 8 << 20),
             grid=(2,),
             out_specs=pl.BlockSpec((QT, 512), lambda i: (i, 0)),
-        )(where, bounds, queries, start_col, kv_z, kv_zy, *state[half])
+        )(where, bounds, *queries, start_col, kv_z, kv_zy, *state[half])
 
     attended = [far_call(0), far_call(1)]
 

time: 308 us -> 316 us (1.026); the launches traced: 304 us -> 316 us
  starting transfers between devices: 37.6 us -> 42.4 us
  Pallas kernels: 40.4 us -> 44 us
    ppermute x41 -> x43, waiting for transfers between devices: 177 us -> 195 us  [swap(): return lax.ppermute(value, axis, SWAP)]
    all_to_all x1, waiting for transfers between devices: 16.7 us -> 0.01 us  [split_body(): weights = lax.all_to_all(weights, QUAD, 0, 0, tiled=True)]
    ppermute x41 -> x43, starting transfers between devices: 32.2 us -> 37 us  [swap(): return lax.ppermute(value, axis, SWAP)]
    pallas_call x2 -> x3, Pallas kernels: 8.57 us -> 11.8 us  [the longest x1 8.04 us: split_body(): call(project_q_kernel, (jax.ShapeDtypeStruct((1024, 256), bf16), jax.Shap...]
  transfers between devices with their start and end apart: 42 -> 44, of which waited for: 19 -> 15; matrix products, arithmetic and copies ran while one was open for 3% -> 4% of each run, Pallas kernels for 12% -> 13%
where the time goes in v5:
time: 316 us
  waiting for transfers between devices  195 us (62%)
  Pallas kernels  44 us (14%)
  starting transfers between devices  42.4 us (13%)
  blocking collectives  17.2 us (5%)
  local copies, waits for them, and re-layouts  10 us (3%)
  other arithmetic  6.96 us (2%)
    ppermute x43, waiting for transfers between devices, swap(): return lax.ppermute(value, axis, SWAP)  195 us
    ppermute x43, starting transfers between devices, swap(): return lax.ppermute(value, axis, SWAP)  37 us
    all_to_all x1, blocking collectives, split_body(): home = lax.all_to_all(sent.reshape(8, 128, 512), QUAD, 0, 0, tiled=True)  17.2 us
    pallas_call x2, Pallas kernels, near_half(): call(functools.partial(near_kernel, half), [jax.ShapeDtypeStruct((2, 4 *...  10.8 us
    pallas_call x1, Pallas kernels, split_body(): call(project_kv_kernel, (jax.ShapeDtypeStruct((1024, 256), bf16), jax.Sha...  8.42 us
    pallas_call x1, Pallas kernels, split_body(): call(project_q_kernel, (jax.ShapeDtypeStruct((1024, 256), bf16), jax.Shap...  8.04 us
    pallas_call x2, Pallas kernels, output_near(): call(functools.partial(output_near_kernel, half), [rows, laid] if half ==...  6.78 us
  transfers between devices with their start and end apart: 44, of which 15 were waited for; matrix products, arithmetic and copies ran while one was open for 4% of the time, Pallas kernels for 13%

profile of v5, /device:TPU:0, one launch (start us, length us, event | category | flops | bytes accessed | tf_op | source)
XLA Modules:
  0.0 315.8 jit_solution(15168878966540049872)
XLA Ops:
  0.0 1.2 copy-done.5
  1.2 0.9 copy-done.6
  2.2 0.9 copy-done.7
  3.1 0.7 copy-done.8
  3.8 0.6 shard_map.73
  4.4 1.2 copy-done.2
  5.7 5.4 %all-to-all-start = ((bf16[8,136,768]{2,1,0:T(8,128)(2,1)}), bf16[8,136,768]{2,1,0:T(8,128)(2,1)S(1)}, u32[]{:S(2)}, u32[]{:S(2)}) async-start(bf16[8,136,768]{2,1,0:T(8,128)(2,1)} %copy-done.2), calls=%async_computation | async-start | bytes 3342336 | tf_op jit(solution)/shard_map/all_to_all | solution.py:418
  11.4 1.5 fusion.2.refs_0_
  13.0 2.1 collective-permute-start.6
  15.2 28.8 %collective-permute-done.6.refs_4_ = bf16[64,4096]{1,0:T(8,128)(2,1)S(1)} collective-permute-done((bf16[64,4096]{1,0:T(8,128)(2,1)S(1)}, bf16[64,4096]{1,0:T(8,128)(2,1)S(1)}, u32[]{:S(2)}, u32[]{:S(2)}) %collective-permute-start.6) | collective-permute-done | bytes 524320 | tf_op jit(solution)/shard_map/ppermute | solution.py:34
  44.0 1.5 collective-permute-start.10
  45.5 9.3 %collective-permute-done.8.refs_6_ = bf16[64,4096]{1,0:T(8,128)(2,1)} collective-permute-done((bf16[64,4096]{1,0:T(8,128)(2,1)S(1)}, bf16[64,4096]{1,0:T(8,128)(2,1)}, u32[]{:S(2)}, u32[]{:S(2)}) %collective-permute-start.8) | collective-permute-done | bytes 524320 | tf_op jit(solution)/shard_map/ppermute | solution.py:34
  54.8 1.5 collective-permute-start.12
  56.2 1.5 collective-permute-start
  57.8 0.6 collective-permute-start.4
  58.4 2.7 collective-permute-start.1
  61.0 8.9 %collective-permute-done.12.refs_10_ = bf16[64,4096]{1,0:T(8,128)(2,1)} collective-permute-done((bf16[64,4096]{1,0:T(8,128)(2,1)}, bf16[64,4096]{1,0:T(8,128)(2,1)}, u32[]{:S(2)}, u32[]{:S(2)}) %collective-permute-start.12) | collective-permute-done | bytes 524320 | tf_op jit(solution)/shard_map/ppermute | solution.py:34
  69.9 14.7 %collective-permute-done.1.refs_14_ = bf16[8,136,256]{2,1,0:T(8,128)(2,1)} collective-permute-done((bf16[8,136,256]{2,1,0:T(8,128)(2,1)S(1)}, bf16[8,136,256]{2,1,0:T(8,128)(2,1)}, u32[]{:S(2)}, u32[]{:S(2)}) %collective-permute-start.1) | collective-permute-done | bytes 557088 | tf_op jit(solution)/shard_map/ppermute | solution.py:34
  85.1 0.8 copy-done.3
  85.9 5.0 %collective-permute-done.4.refs_2_ = bf16[128,4096]{1,0:T(8,128)(2,1)} collective-permute-done((bf16[128,4096]{1,0:T(8,128)(2,1)S(1)}, bf16[128,4096]{1,0:T(8,128)(2,1)}, u32[]{:S(2)}, u32[]{:S(2)}) %collective-permute-start.4) | collective-permute-done | bytes 1048608 | tf_op jit(solution)/shard_map/ppermute | solution.py:34
  91.0 0.8 slice.55
  92.4 13.6 %collective-permute-done.2.refs_15_ = bf16[8,136,256]{2,1,0:T(8,128)(2,1)} collective-permute-done((bf16[8,136,256]{2,1,0:T(8,128)(2,1)}, bf16[8,136,256]{2,1,0:T(8,128)(2,1)}, u32[]{:S(2)}, u32[]{:S(2)}) %collective-permute-start.2) | collective-permute-done | bytes 557088 | tf_op jit(solution)/shard_map/ppermute | solution.py:34
  105.9 2.6 collective-permute-start.14
  108.5 0.9 fusion.16
  109.8 3.2 fusion.3
  113.1 1.9 pad_maximum_fusion
  115.0 0.7 slice.51
  115.7 0.7 slice.52
  116.5 0.7 slice.49
  117.2 2.7 collective-permute-start.16
  119.9 27.6 %collective-permute-done.15.refs_15_ = bf16[8,128,128]{2,1,0:T(8,128)(2,1)S(1)} collective-permute-done((bf16[8,128,128]{2,1,0:T(8,128)(2,1)}, bf16[8,128,128]{2,1,0:T(8,128)(2,1)S(1)}, u32[]{:S(2)}, u32[]{:S(2)}) %collective-permute-start.15) | collective-permute-done | bytes 262176 | tf_op jit(solution)/shard_map/ppermute | solution.py:34
  147.5 1.5 collective-permute-start.18
  149.5 8.4 %shard_map.74 = (bf16[1024,256]{1,0:T(8,128)(2,1)S(1)}, s32[1024,128]{1,0:T(8,128)S(1)}, s32[8]{0:T(128)S(1)}) custom-call(s32[5]{0:T(128)S(1)} %stack.23.where, bf16[32,8,128]{2,1,0:T(8,128)(2,1)S(1)} %pad_maximum_fusion.2.count_ref, bf16[128,4096]{1,0:T(8,128)(2,1)S(1)} %fusion.2.refs_0_, bf16[128,4096]{1,0:T(8,128)(2,1)} %collective-permute-done.3.refs_1_, ...), custom_call_target="tpu_custom_call" | custom-call | flops 2147483648 | bytes 11534336 | tf_op jit(solution)/shard_map/pallas_call | solution.py:447
  158.1 3.0 collective-permute-start.34
  161.2 1.5 collective-permute-start.22
  162.7 5.2 %collective-permute-done.17.refs_17_ = bf16[8,128,256]{2,1,0:T(8,128)(2,1)S(1)} collective-permute-done((bf16[8,128,256]{2,1,0:T(8,128)(2,1)}, bf16[8,128,256]{2,1,0:T(8,128)(2,1)S(1)}, u32[]{:S(2)}, u32[]{:S(2)}) %collective-permute-start.17) | collective-permute-done | bytes 524320 | tf_op jit(solution)/shard_map/ppermute | solution.py:34
  167.9 1.5 collective-permute-start.19
  169.4 35.5 %collective-permute-done.20.kv_z = bf16[1024,256]{1,0:T(8,128)(2,1)S(1)} collective-permute-done((bf16[1024,256]{1,0:T(8,128)(2,1)S(1)}, bf16[1024,256]{1,0:T(8,128)(2,1)S(1)}, u32[]{:S(2)}, u32[]{:S(2)}) %collective-permute-start.20) | collective-permute-done | bytes 524320 | tf_op jit(solution)/shard_map/ppermute | solution.py:34
  204.9 1.5 collective-permute-start.21
  206.5 8.0 %shard_map.75 = (bf16[1024,256]{1,0:T(8,128)(2,1)S(1)}, f32[1024,256]{1,0:T(8,128)S(1)}) custom-call(s32[5]{0:T(128)S(1)} %stack.23.where, bf16[128,4096]{1,0:T(8,128)(2,1)S(1)} %fusion.2.refs_0_, bf16[128,4096]{1,0:T(8,128)(2,1)} %collective-permute-done.3.refs_1_, bf16[128,4096]{1,0:T(8,128)(2,1)} %collective-permute-done.4.refs_2_, ...), custom_call_target="tpu_custom_call" | custom-call | flops 4294967296 | bytes 14680064 | tf_op jit(solution)/shard_map/pallas_call | solution.py:463
  214.5 0.6 collective-permute-start.33
  215.1 3.1 shard_map.76.q2_ref
  218.2 1.6 collective-permute-start.36
  219.8 7.5 %collective-permute-done.37.refs_12_ = bf16[2048,128]{1,0:T(8,128)(2,1)S(1)} collective-permute-done((bf16[2048,128]{1,0:T(8,128)(2,1)S(1)}, bf16[2048,128]{1,0:T(8,128)(2,1)S(1)}, u32[]{:S(2)}, u32[]{:S(2)}) %collective-permute-start.37) | collective-permute-done | bytes 524320 | tf_op jit(solution)/shard_map/ppermute | solution.py:34
  227.3 1.5 collective-permute-start.35
  229.4 3.3 %shard_map.77 = (f32[2,1024,128]{2,1,0:T(8,128)S(1)}, f32[2,1024,128]{2,1,0:T(8,128)S(1)}, f32[2,1024,128]{2,1,0:T(8,128)S(1)}) custom-call(s32[5]{0:T(128)S(1)} %stack.23.where, s32[8]{0:T(128)S(1)} %get-tuple-element.18.bounds, bf16[1024,256]{1,0:T(8,128)(2,1)S(1)} %get-tuple-element.19.q_ref, bf16[1024,256]{1,0:T(8,128)(2,1)S(1)} %shard_map.76.q2_ref, ...), custom_call_target="tpu_custom_call" | custom-call | flops 2147483648 | bytes 4194304 | tf_op jit(solution)/shard_map/pallas_call | solution.py:498
  232.7 7.5 %shard_map.79 = (f32[2,1024,128]{2,1,0:T(8,128)S(1)}, f32[2,1024,128]{2,1,0:T(8,128)S(1)}, f32[2,1024,128]{2,1,0:T(8,128)S(1)}) custom-call(s32[5]{0:T(128)S(1)} %stack.23.where, s32[8]{0:T(128)S(1)} %get-tuple-element.18.bounds, bf16[1024,256]{1,0:T(8,128)(2,1)S(1)} %get-tuple-element.19.q_ref, bf16[1024,256]{1,0:T(8,128)(2,1)S(1)} %shard_map.76.q2_ref, ...), custom_call_target="tpu_custom_call" | custom-call | flops 2147483648 | bytes 4194304 | tf_op jit(solution)/shard_map/pallas_call | solution.py:498
  240.2 1.3 shard_map.78.refs_0_
  241.6 1.0 collective-permute-start.23
  242.5 1.3 shard_map.80.refs_0_
  243.9 2.1 collective-permute-start.26
  245.9 7.5 %collective-permute-done.35.refs_9_ = bf16[2048,128]{1,0:T(8,128)(2,1)S(1)} collective-permute-done((bf16[2048,128]{1,0:T(8,128)(2,1)S(1)}, bf16[2048,128]{1,0:T(8,128)(2,1)S(1)}, u32[]{:S(2)}, u32[]{:S(2)}) %collective-permute-start.35) | collective-permute-done | bytes 524320 | tf_op jit(solution)/shard_map/ppermute | solution.py:34
  253.4 10.2 %collective-permute-done.38.refs_13_ = bf16[2048,128]{1,0:T(8,128)(2,1)S(1)} collective-permute-done((bf16[2048,128]{1,0:T(8,128)(2,1)S(1)}, bf16[2048,128]{1,0:T(8,128)(2,1)S(1)}, u32[]{:S(2)}, u32[]{:S(2)}) %collective-permute-start.38) | collective-permute-done | bytes 524320 | tf_op jit(solution)/shard_map/ppermute | solution.py:34
  264.2 2.1 collective-permute-done.26.refs_4_
  266.2 1.7 collective-permute-start.27
  268.2 10.2 %collective-permute-done.40.refs_2_ = bf16[512,512]{1,0:T(8,128)(2,1)S(1)} collective-permute-done((bf16[512,512]{1,0:T(8,128)(2,1)S(1)}, bf16[512,512]{1,0:T(8,128)(2,1)S(1)}, u32[]{:S(2)}, u32[]{:S(2)}) %collective-permute-start.40) | collective-permute-done | bytes 524320 | tf_op jit(solution)/shard_map/ppermute | solution.py:34
  278.4 0.5 collective-permute-start.41
  279.0 8.7 %collective-permute-done.27.refs_2_ = bf16[512,512]{1,0:T(8,128)(2,1)S(1)} collective-permute-done((bf16[512,512]{1,0:T(8,128)(2,1)S(1)}, bf16[512,512]{1,0:T(8,128)(2,1)S(1)}, u32[]{:S(2)}, u32[]{:S(2)}) %collective-permute-start.27) | collective-permute-done | bytes 524320 | tf_op jit(solution)/shard_map/ppermute | solution.py:34
  287.8 0.5 collective-permute-start.25
  288.3 3.6 %shard_map.81 = (f32[512,512]{1,0:T(8,128)S(1)}, bf16[4096,512]{1,0:T(8,128)(2,1)S(1)}) custom-call(s32[5]{0:T(128)S(1)} %stack.23.where, bf16[512,512]{1,0:T(8,128)(2,1)S(1)} %shard_map.78.refs_0_, bf16[512,512]{1,0:T(8,128)(2,1)S(1)} %collective-permute-done.29.refs_1_, bf16[512,512]{1,0:T(8,128)(2,1)S(1)} %collective-permute-done.23.refs_2_, ...), custom_call_target="tpu_custom_call" | custom-call | flops 1610612736 | bytes 9437184 | tf_op jit(solution)/shard_map/pallas_call | solution.py:549
  291.9 3.2 %shard_map.82.refs_6_ = f32[512,512]{1,0:T(8,128)S(1)} custom-call(s32[5]{0:T(128)S(1)} %stack.23.where, bf16[512,512]{1,0:T(8,128)(2,1)S(1)} %shard_map.80.refs_0_, bf16[512,512]{1,0:T(8,128)(2,1)S(1)} %collective-permute-done.39.refs_1_, bf16[512,512]{1,0:T(8,128)(2,1)S(1)} %collective-permute-done.40.refs_2_, ...), custom_call_target="tpu_custom_call" | custom-call | flops 1610612736 | bytes 9437184 | tf_op jit(solution)/shard_map/pallas_call | solution.py:549
  295.1 2.2 shard_map.83
  297.4 17.2 %all_to_all.10.sent_ref = bf16[8,128,512]{2,1,0:T(8,128)(2,1)S(1)} all-to-all(bf16[8,128,512]{2,1,0:T(8,128)(2,1)S(1)} %bitcast.7), channel_id=1, replica_groups=mesh['zh'=2,'zl'=2,'y'=2,'x'=2,'c'=2] {'zl','x','c'}, dimensions={0} | all-to-all | bytes 2097152 | tf_op jit(solution)/shard_map/all_to_all | solution.py:571
  314.5 1.3 shard_map.84
  (79 shorter events, 4.3 us)
Async XLA Ops:
  0.0 1.2 copy-start.5
  1.2 0.9 copy-start.6
  2.2 0.9 copy-start.7
  3.1 0.7 copy-start.8
  4.4 1.2 copy-start.2
  5.7 5.4 %copy-start = (bf16[128,4096]{1,0:T(8,128)(2,1)S(1)}, bf16[128,4096]{1,0:T(8,128)(2,1)}, u32[]{:S(2)}) copy-start(bf16[128,4096]{1,0:T(8,128)(2,1)} %tok_ref.1) | copy-start | bytes 3145732
  5.7 5.7 %copy-start.11 = (f32[4096]{0:T(1024)S(1)}, f32[4096]{0:T(1024)}, u32[]{:S(2)}) copy-start(f32[4096]{0:T(1024)} %param.8) | copy-start | bytes 49156
  5.7 50.6 %all-to-all-start = ((bf16[8,136,768]{2,1,0:T(8,128)(2,1)}), bf16[8,136,768]{2,1,0:T(8,128)(2,1)S(1)}, u32[]{:S(2)}, u32[]{:S(2)}) async-start(bf16[8,136,768]{2,1,0:T(8,128)(2,1)} %copy-done.2), calls=%async_computation | async-start | bytes 3342336 | tf_op jit(solution)/shard_map/all_to_all | solution.py:418
  13.0 31.0 %collective-permute-start.6 = (bf16[64,4096]{1,0:T(8,128)(2,1)S(1)}, bf16[64,4096]{1,0:T(8,128)(2,1)S(1)}, u32[]{:S(2)}, u32[]{:S(2)}) collective-permute-start(bf16[64,4096]{1,0:T(8,128)(2,1)S(1)} %get-tuple-element.36), channel_id=1, source_target_pairs={{0,8},{8,0},{1,9},{9,1},{2,10},{10,2},{3,11},{11,3},{4,12},{12,4},... | collective-permute-start | bytes 1572872 | tf_op jit(solution)/shard_map/ppermute | solution.py:34
  15.1 39.7 %collective-permute-start.8 = (bf16[64,4096]{1,0:T(8,128)(2,1)S(1)}, bf16[64,4096]{1,0:T(8,128)(2,1)}, u32[]{:S(2)}, u32[]{:S(2)}) collective-permute-start(bf16[64,4096]{1,0:T(8,128)(2,1)S(1)} %get-tuple-element.35), channel_id=1, source_target_pairs={{0,8},{8,0},{1,9},{9,1},{2,10},{10,2},{3,11},{11,3},{4,12},{12,4},... | collective-permute-start | bytes 1572872 | tf_op jit(solution)/shard_map/ppermute | solution.py:34
  44.0 17.0 %collective-permute-start.10 = (bf16[64,4096]{1,0:T(8,128)(2,1)S(1)}, bf16[64,4096]{1,0:T(8,128)(2,1)}, u32[]{:S(2)}, u32[]{:S(2)}) collective-permute-start(bf16[64,4096]{1,0:T(8,128)(2,1)S(1)} %collective-permute-done.6.refs_4_), channel_id=1, source_target_pairs={{0,2},{2,0},{1,3},{3,1},{4,6},{6,4},{5,7},{7,5},{8,10},{10,8},{9,1... | collective-permute-start | bytes 1572872 | tf_op jit(solution)/shard_map/ppermute | solution.py:34
  54.8 15.1 %collective-permute-start.12 = (bf16[64,4096]{1,0:T(8,128)(2,1)}, bf16[64,4096]{1,0:T(8,128)(2,1)}, u32[]{:S(2)}, u32[]{:S(2)}) collective-permute-start(bf16[64,4096]{1,0:T(8,128)(2,1)} %collective-permute-done.8.refs_6_), channel_id=1, source_target_pairs={{0,2},{2,0},{1,3},{3,1},{4,6},{6,4},{5,7},{7,5},{8,10},{10,8},{9,1... | collective-permute-start | bytes 1572872 | tf_op jit(solution)/shard_map/ppermute | solution.py:34
  56.2 53.2 %collective-permute-start = (bf16[8,136,768]{2,1,0:T(8,128)(2,1)S(1)}, bf16[8,136,768]{2,1,0:T(8,128)(2,1)}, u32[]{:S(2)}, u32[]{:S(2)}) collective-permute-start(bf16[8,136,768]{2,1,0:T(8,128)(2,1)S(1)} %all-to-all-done.refs_12_), channel_id=1, source_target_pairs={{0,4},{4,0},{1,5},{5,1},{2,6},{6,2},{3,7},{7,3},{8,12},{12,8},{9,1... | collective-permute-start | bytes 5013512 | tf_op jit(solution)/shard_map/ppermute | solution.py:34
  57.8 33.2 %collective-permute-start.4 = (bf16[128,4096]{1,0:T(8,128)(2,1)S(1)}, bf16[128,4096]{1,0:T(8,128)(2,1)}, u32[]{:S(2)}, u32[]{:S(2)}) collective-permute-start(bf16[128,4096]{1,0:T(8,128)(2,1)S(1)} %fusion.2.refs_0_), channel_id=1, source_target_pairs={{0,2},{2,0},{1,3},{3,1},{4,6},{6,4},{5,7},{7,5},{8,10},{10,8},{9,1... | collective-permute-start | bytes 3145736 | tf_op jit(solution)/shard_map/ppermute | solution.py:34
  58.4 26.2 %collective-permute-start.1 = (bf16[8,136,256]{2,1,0:T(8,128)(2,1)S(1)}, bf16[8,136,256]{2,1,0:T(8,128)(2,1)}, u32[]{:S(2)}, u32[]{:S(2)}) collective-permute-start(bf16[8,136,256]{2,1,0:T(8,128)(2,1)S(1)} %slice.50), channel_id=1, source_target_pairs={{0,16},{16,0},{1,17},{17,1},{2,18},{18,2},{3,19},{19,3},{4,20},{20... | collective-permute-start | bytes 1671176 | tf_op jit(solution)/shard_map/ppermute | solution.py:34
  61.0 24.1 %collective-permute-start.7 = (bf16[64,4096]{1,0:T(8,128)(2,1)S(1)}, bf16[64,4096]{1,0:T(8,128)(2,1)S(1)}, u32[]{:S(2)}, u32[]{:S(2)}) collective-permute-start(bf16[64,4096]{1,0:T(8,128)(2,1)S(1)} %collective-permute-done.6.refs_4_), channel_id=1, source_target_pairs={{0,1},{1,0},{2,3},{3,2},{4,5},{5,4},{6,7},{7,6},{8,9},{9,8},{10,11... | collective-permute-start | bytes 1572872 | tf_op jit(solution)/shard_map/ppermute | solution.py:34
  69.9 22.4 %collective-permute-start.3 = (bf16[128,4096]{1,0:T(8,128)(2,1)S(1)}, bf16[128,4096]{1,0:T(8,128)(2,1)}, u32[]{:S(2)}, u32[]{:S(2)}) collective-permute-start(bf16[128,4096]{1,0:T(8,128)(2,1)S(1)} %fusion.2.refs_0_), channel_id=1, source_target_pairs={{0,1},{1,0},{2,3},{3,2},{4,5},{5,4},{6,7},{7,6},{8,9},{9,8},{10,11... | collective-permute-start | bytes 3145736 | tf_op jit(solution)/shard_map/ppermute | solution.py:34
  84.6 21.4 %collective-permute-start.2 = (bf16[8,136,256]{2,1,0:T(8,128)(2,1)}, bf16[8,136,256]{2,1,0:T(8,128)(2,1)}, u32[]{:S(2)}, u32[]{:S(2)}) collective-permute-start(bf16[8,136,256]{2,1,0:T(8,128)(2,1)} %collective-permute-done.1.refs_14_), channel_id=1, source_target_pairs={{0,4},{4,0},{1,5},{5,1},{2,6},{6,2},{3,7},{7,3},{8,12},{12,8},{9,1... | collective-permute-start | bytes 1671176 | tf_op jit(solution)/shard_map/ppermute | solution.py:34
  85.1 0.8 copy-start.3
  85.9 5.9 %collective-permute-start.9 = (bf16[64,4096]{1,0:T(8,128)(2,1)}, bf16[64,4096]{1,0:T(8,128)(2,1)}, u32[]{:S(2)}, u32[]{:S(2)}) collective-permute-start(bf16[64,4096]{1,0:T(8,128)(2,1)} %collective-permute-done.8.refs_6_), channel_id=1, source_target_pairs={{0,1},{1,0},{2,3},{3,2},{4,5},{5,4},{6,7},{7,6},{8,9},{9,8},{10,11... | collective-permute-start | bytes 1572872 | tf_op jit(solution)/shard_map/ppermute | solution.py:34
  90.9 58.6 %collective-permute-start.5 = (bf16[128,4096]{1,0:T(8,128)(2,1)}, bf16[128,4096]{1,0:T(8,128)(2,1)}, u32[]{:S(2)}, u32[]{:S(2)}) collective-permute-start(bf16[128,4096]{1,0:T(8,128)(2,1)} %collective-permute-done.4.refs_2_), channel_id=1, source_target_pairs={{0,1},{1,0},{2,3},{3,2},{4,5},{5,4},{6,7},{7,6},{8,9},{9,8},{10,11... | collective-permute-start | bytes 3145736 | tf_op jit(solution)/shard_map/ppermute | solution.py:34
  91.8 25.4 %collective-permute-start.11 = (bf16[64,4096]{1,0:T(8,128)(2,1)}, bf16[64,4096]{1,0:T(8,128)(2,1)}, u32[]{:S(2)}, u32[]{:S(2)}) collective-permute-start(bf16[64,4096]{1,0:T(8,128)(2,1)} %collective-permute-done.10.refs_8_), channel_id=1, source_target_pairs={{0,1},{1,0},{2,3},{3,2},{4,5},{5,4},{6,7},{7,6},{8,9},{9,8},{10,11... | collective-permute-start | bytes 1572872 | tf_op jit(solution)/shard_map/ppermute | solution.py:34
  92.3 57.2 %collective-permute-start.13 = (bf16[64,4096]{1,0:T(8,128)(2,1)}, bf16[64,4096]{1,0:T(8,128)(2,1)}, u32[]{:S(2)}, u32[]{:S(2)}) collective-permute-start(bf16[64,4096]{1,0:T(8,128)(2,1)} %collective-permute-done.12.refs_10_), channel_id=1, source_target_pairs={{0,1},{1,0},{2,3},{3,2},{4,5},{5,4},{6,7},{7,6},{8,9},{9,8},{10,11... | collective-permute-start | bytes 1572872 | tf_op jit(solution)/shard_map/ppermute | solution.py:34
  105.9 43.0 %collective-permute-start.14 = (bf16[8,128,256]{2,1,0:T(8,128)(2,1)}, bf16[8,128,256]{2,1,0:T(8,128)(2,1)}, u32[]{:S(2)}, u32[]{:S(2)}) collective-permute-start(bf16[8,128,256]{2,1,0:T(8,128)(2,1)} %slice.55), channel_id=1, source_target_pairs={{0,16},{16,0},{1,17},{17,1},{2,18},{18,2},{3,19},{19,3},{4,20},{20... | collective-permute-start | bytes 1572872 | tf_op jit(solution)/shard_map/ppermute | solution.py:34
  109.5 38.0 %collective-permute-start.15 = (bf16[8,128,128]{2,1,0:T(8,128)(2,1)}, bf16[8,128,128]{2,1,0:T(8,128)(2,1)S(1)}, u32[]{:S(2)}, u32[]{:S(2)}) collective-permute-start(bf16[8,128,128]{2,1,0:T(8,128)(2,1)} %get-tuple-element.32), channel_id=1, source_target_pairs={{0,16},{16,0},{1,17},{17,1},{2,18},{18,2},{3,19},{19,3},{4,20},{20... | collective-permute-start | bytes 786440 | tf_op jit(solution)/shard_map/ppermute | solution.py:34
  113.1 4.1 %copy-start.10 = (bf16[8,128,128]{2,1,0:T(8,128)(2,1)S(1)}, bf16[8,128,128]{2,1,0:T(8,128)(2,1)}, u32[]{:S(2)}) copy-start(bf16[8,128,128]{2,1,0:T(8,128)(2,1)} %get-tuple-element.31) | copy-start | bytes 786436
  113.1 36.4 %copy-start.4 = (bf16[64,4096]{1,0:T(8,128)(2,1)S(1)}, bf16[64,4096]{1,0:T(8,128)(2,1)}, u32[]{:S(2)}) copy-start(bf16[64,4096]{1,0:T(8,128)(2,1)} %copy-done.3) | copy-start | bytes 1572868
  117.2 43.9 %collective-permute-start.16 = (bf16[8,128,128]{2,1,0:T(8,128)(2,1)S(1)}, bf16[8,128,128]{2,1,0:T(8,128)(2,1)S(1)}, u32[]{:S(2)}, u32[]{:S(2)}) collective-permute-start(bf16[8,128,128]{2,1,0:T(8,128)(2,1)S(1)} %copy-done.10), channel_id=1, source_target_pairs={{0,16},{16,0},{1,17},{17,1},{2,18},{18,2},{3,19},{19,3},{4,20},{20... | collective-permute-start | bytes 786440 | tf_op jit(solution)/shard_map/ppermute | solution.py:34
  147.5 13.7 %collective-permute-start.18 = (bf16[8,128,128]{2,1,0:T(8,128)(2,1)S(1)}, bf16[8,128,128]{2,1,0:T(8,128)(2,1)S(1)}, u32[]{:S(2)}, u32[]{:S(2)}) collective-permute-start(bf16[8,128,128]{2,1,0:T(8,128)(2,1)S(1)} %collective-permute-done.15.refs_15_), channel_id=1, source_target_pairs={{0,4},{4,0},{1,5},{5,1},{2,6},{6,2},{3,7},{7,3},{8,12},{12,8},{9,1... | collective-permute-start | bytes 786440 | tf_op jit(solution)/shard_map/ppermute | solution.py:34
  149.0 18.9 %collective-permute-start.17 = (bf16[8,128,256]{2,1,0:T(8,128)(2,1)}, bf16[8,128,256]{2,1,0:T(8,128)(2,1)S(1)}, u32[]{:S(2)}, u32[]{:S(2)}) collective-permute-start(bf16[8,128,256]{2,1,0:T(8,128)(2,1)} %collective-permute-done.14.refs_14_), channel_id=1, source_target_pairs={{0,4},{4,0},{1,5},{5,1},{2,6},{6,2},{3,7},{7,3},{8,12},{12,8},{9,1... | collective-permute-start | bytes 1572872 | tf_op jit(solution)/shard_map/ppermute | solution.py:34
  149.5 8.5 %copy-start.9 = (bf16[4096,128]{1,0:T(8,128)(2,1)S(1)}, bf16[4096,128]{1,0:T(8,128)(2,1)}, u32[]{:S(2)}) copy-start(bf16[4096,128]{1,0:T(8,128)(2,1)} %param.12) | copy-start | bytes 3145732
  157.9 47.0 %collective-permute-start.20 = (bf16[1024,256]{1,0:T(8,128)(2,1)S(1)}, bf16[1024,256]{1,0:T(8,128)(2,1)S(1)}, u32[]{:S(2)}, u32[]{:S(2)}) collective-permute-start(bf16[1024,256]{1,0:T(8,128)(2,1)S(1)} %get-tuple-element.22.kv_own), channel_id=1, source_target_pairs={{0,16},{16,0},{1,17},{17,1},{2,18},{18,2},{3,19},{19,3},{4,20},{20... | collective-permute-start | bytes 1572872 | tf_op jit(solution)/shard_map/ppermute | solution.py:34
  158.1 60.1 %collective-permute-start.34 = (bf16[2048,128]{1,0:T(8,128)(2,1)S(1)}, bf16[2048,128]{1,0:T(8,128)(2,1)S(1)}, u32[]{:S(2)}, u32[]{:S(2)}) collective-permute-start(bf16[2048,128]{1,0:T(8,128)(2,1)S(1)} %get-tuple-element.34.refs_6_), channel_id=1, source_target_pairs={{0,16},{16,0},{1,17},{17,1},{2,18},{18,2},{3,19},{19,3},{4,20},{20... | collective-permute-start | bytes 1572872 | tf_op jit(solution)/shard_map/ppermute | solution.py:34
  161.1 66.2 %collective-permute-start.37 = (bf16[2048,128]{1,0:T(8,128)(2,1)S(1)}, bf16[2048,128]{1,0:T(8,128)(2,1)S(1)}, u32[]{:S(2)}, u32[]{:S(2)}) collective-permute-start(bf16[2048,128]{1,0:T(8,128)(2,1)S(1)} %get-tuple-element.33.refs_10_), channel_id=1, source_target_pairs={{0,16},{16,0},{1,17},{17,1},{2,18},{18,2},{3,19},{19,3},{4,20},{20... | collective-permute-start | bytes 1572872 | tf_op jit(solution)/shard_map/ppermute | solution.py:34
  161.2 67.7 %collective-permute-start.22 = (bf16[1024,256]{1,0:T(8,128)(2,1)S(1)}, bf16[1024,256]{1,0:T(8,128)(2,1)S(1)}, u32[]{:S(2)}, u32[]{:S(2)}) collective-permute-start(bf16[1024,256]{1,0:T(8,128)(2,1)S(1)} %get-tuple-element.22.kv_own), channel_id=1, source_target_pairs={{0,4},{4,0},{1,5},{5,1},{2,6},{6,2},{3,7},{7,3},{8,12},{12,8},{9,1... | collective-permute-start | bytes 1572872 | tf_op jit(solution)/shard_map/ppermute | solution.py:34
  167.9 46.6 %collective-permute-start.19 = (bf16[8,128,128]{2,1,0:T(8,128)(2,1)S(1)}, bf16[8,128,128]{2,1,0:T(8,128)(2,1)S(1)}, u32[]{:S(2)}, u32[]{:S(2)}) collective-permute-start(bf16[8,128,128]{2,1,0:T(8,128)(2,1)S(1)} %collective-permute-done.16.refs_16_), channel_id=1, source_target_pairs={{0,4},{4,0},{1,5},{5,1},{2,6},{6,2},{3,7},{7,3},{8,12},{12,8},{9,1... | collective-permute-start | bytes 786440 | tf_op jit(solution)/shard_map/ppermute | solution.py:34
  204.9 35.3 %collective-permute-start.21 = (bf16[1024,256]{1,0:T(8,128)(2,1)S(1)}, bf16[1024,256]{1,0:T(8,128)(2,1)S(1)}, u32[]{:S(2)}, u32[]{:S(2)}) collective-permute-start(bf16[1024,256]{1,0:T(8,128)(2,1)S(1)} %collective-permute-done.20.kv_z), channel_id=1, source_target_pairs={{0,4},{4,0},{1,5},{5,1},{2,6},{6,2},{3,7},{7,3},{8,12},{12,8},{9,1... | collective-permute-start | bytes 1572872 | tf_op jit(solution)/shard_map/ppermute | solution.py:34
  214.5 28.0 %collective-permute-start.33 = (bf16[2048,128]{1,0:T(8,128)(2,1)S(1)}, bf16[2048,128]{1,0:T(8,128)(2,1)S(1)}, u32[]{:S(2)}, u32[]{:S(2)}) collective-permute-start(bf16[2048,128]{1,0:T(8,128)(2,1)S(1)} %get-tuple-element.34.refs_6_), channel_id=1, source_target_pairs={{0,4},{4,0},{1,5},{5,1},{2,6},{6,2},{3,7},{7,3},{8,12},{12,8},{9,1... | collective-permute-start | bytes 1572872 | tf_op jit(solution)/shard_map/ppermute | solution.py:34
  218.2 25.6 %collective-permute-start.36 = (bf16[2048,128]{1,0:T(8,128)(2,1)S(1)}, bf16[2048,128]{1,0:T(8,128)(2,1)S(1)}, u32[]{:S(2)}, u32[]{:S(2)}) collective-permute-start(bf16[2048,128]{1,0:T(8,128)(2,1)S(1)} %get-tuple-element.33.refs_10_), channel_id=1, source_target_pairs={{0,4},{4,0},{1,5},{5,1},{2,6},{6,2},{3,7},{7,3},{8,12},{12,8},{9,1... | collective-permute-start | bytes 1572872 | tf_op jit(solution)/shard_map/ppermute | solution.py:34
  227.3 26.1 %collective-permute-start.35 = (bf16[2048,128]{1,0:T(8,128)(2,1)S(1)}, bf16[2048,128]{1,0:T(8,128)(2,1)S(1)}, u32[]{:S(2)}, u32[]{:S(2)}) collective-permute-start(bf16[2048,128]{1,0:T(8,128)(2,1)S(1)} %collective-permute-done.34.refs_8_), channel_id=1, source_target_pairs={{0,4},{4,0},{1,5},{5,1},{2,6},{6,2},{3,7},{7,3},{8,12},{12,8},{9,1... | collective-permute-start | bytes 1572872 | tf_op jit(solution)/shard_map/ppermute | solution.py:34
  228.8 34.8 %collective-permute-start.38 = (bf16[2048,128]{1,0:T(8,128)(2,1)S(1)}, bf16[2048,128]{1,0:T(8,128)(2,1)S(1)}, u32[]{:S(2)}, u32[]{:S(2)}) collective-permute-start(bf16[2048,128]{1,0:T(8,128)(2,1)S(1)} %collective-permute-done.37.refs_12_), channel_id=1, source_target_pairs={{0,4},{4,0},{1,5},{5,1},{2,6},{6,2},{3,7},{7,3},{8,12},{12,8},{9,1... | collective-permute-start | bytes 1572872 | tf_op jit(solution)/shard_map/ppermute | solution.py:34
  241.6 22.1 %collective-permute-start.23 = (bf16[512,512]{1,0:T(8,128)(2,1)S(1)}, bf16[512,512]{1,0:T(8,128)(2,1)S(1)}, u32[]{:S(2)}, u32[]{:S(2)}) collective-permute-start(bf16[512,512]{1,0:T(8,128)(2,1)S(1)} %shard_map.78.refs_0_), channel_id=1, source_target_pairs={{0,2},{2,0},{1,3},{3,1},{4,6},{6,4},{5,7},{7,5},{8,10},{10,8},{9,1... | collective-permute-start | bytes 1572872 | tf_op jit(solution)/shard_map/ppermute | solution.py:34
  242.5 21.1 %collective-permute-start.31 = (bf16[512,512]{1,0:T(8,128)(2,1)S(1)}, bf16[512,512]{1,0:T(8,128)(2,1)S(1)}, u32[]{:S(2)}, u32[]{:S(2)}) collective-permute-start(bf16[512,512]{1,0:T(8,128)(2,1)S(1)} %shard_map.78.refs_0_), channel_id=1, source_target_pairs={{0,8},{8,0},{1,9},{9,1},{2,10},{10,2},{3,11},{11,3},{4,12},{12,4},... | collective-permute-start | bytes 1572872 | tf_op jit(solution)/shard_map/ppermute | solution.py:34
  243.9 22.4 %collective-permute-start.26 = (bf16[512,512]{1,0:T(8,128)(2,1)S(1)}, bf16[512,512]{1,0:T(8,128)(2,1)S(1)}, u32[]{:S(2)}, u32[]{:S(2)}) collective-permute-start(bf16[512,512]{1,0:T(8,128)(2,1)S(1)} %shard_map.80.refs_0_), channel_id=1, source_target_pairs={{0,8},{8,0},{1,9},{9,1},{2,10},{10,2},{3,11},{11,3},{4,12},{12,4},... | collective-permute-start | bytes 1572872 | tf_op jit(solution)/shard_map/ppermute | solution.py:34
  253.4 14.5 %collective-permute-start.29 = (bf16[512,512]{1,0:T(8,128)(2,1)S(1)}, bf16[512,512]{1,0:T(8,128)(2,1)S(1)}, u32[]{:S(2)}, u32[]{:S(2)}) collective-permute-start(bf16[512,512]{1,0:T(8,128)(2,1)S(1)} %shard_map.78.refs_0_), channel_id=1, source_target_pairs={{0,1},{1,0},{2,3},{3,2},{4,5},{5,4},{6,7},{7,6},{8,9},{9,8},{10,11... | collective-permute-start | bytes 1572872 | tf_op jit(solution)/shard_map/ppermute | solution.py:34
  263.6 14.8 %collective-permute-start.40 = (bf16[512,512]{1,0:T(8,128)(2,1)S(1)}, bf16[512,512]{1,0:T(8,128)(2,1)S(1)}, u32[]{:S(2)}, u32[]{:S(2)}) collective-permute-start(bf16[512,512]{1,0:T(8,128)(2,1)S(1)} %shard_map.80.refs_0_), channel_id=1, source_target_pairs={{0,2},{2,0},{1,3},{3,1},{4,6},{6,4},{5,7},{7,5},{8,10},{10,8},{9,1... | collective-permute-start | bytes 1572872 | tf_op jit(solution)/shard_map/ppermute | solution.py:34
  263.7 14.8 %collective-permute-start.30 = (bf16[512,512]{1,0:T(8,128)(2,1)S(1)}, bf16[512,512]{1,0:T(8,128)(2,1)S(1)}, u32[]{:S(2)}, u32[]{:S(2)}) collective-permute-start(bf16[512,512]{1,0:T(8,128)(2,1)S(1)} %collective-permute-done.23.refs_2_), channel_id=1, source_target_pairs={{0,1},{1,0},{2,3},{3,2},{4,5},{5,4},{6,7},{7,6},{8,9},{9,8},{10,11... | collective-permute-start | bytes 1572872 | tf_op jit(solution)/shard_map/ppermute | solution.py:34
  263.7 15.3 %collective-permute-start.32 = (bf16[512,512]{1,0:T(8,128)(2,1)S(1)}, bf16[512,512]{1,0:T(8,128)(2,1)S(1)}, u32[]{:S(2)}, u32[]{:S(2)}) collective-permute-start(bf16[512,512]{1,0:T(8,128)(2,1)S(1)} %collective-permute-done.31.refs_4_), channel_id=1, source_target_pairs={{0,1},{1,0},{2,3},{3,2},{4,5},{5,4},{6,7},{7,6},{8,9},{9,8},{10,11... | collective-permute-start | bytes 1572872 | tf_op jit(solution)/shard_map/ppermute | solution.py:34
  266.2 21.5 %collective-permute-start.27 = (bf16[512,512]{1,0:T(8,128)(2,1)S(1)}, bf16[512,512]{1,0:T(8,128)(2,1)S(1)}, u32[]{:S(2)}, u32[]{:S(2)}) collective-permute-start(bf16[512,512]{1,0:T(8,128)(2,1)S(1)} %collective-permute-done.26.refs_4_), channel_id=1, source_target_pairs={{0,2},{2,0},{1,3},{3,1},{4,6},{6,4},{5,7},{7,5},{8,10},{10,8},{9,1... | collective-permute-start | bytes 1572872 | tf_op jit(solution)/shard_map/ppermute | solution.py:34
  267.9 19.9 %collective-permute-start.24 = (bf16[512,512]{1,0:T(8,128)(2,1)S(1)}, bf16[512,512]{1,0:T(8,128)(2,1)S(1)}, u32[]{:S(2)}, u32[]{:S(2)}) collective-permute-start(bf16[512,512]{1,0:T(8,128)(2,1)S(1)} %collective-permute-done.23.refs_2_), channel_id=1, source_target_pairs={{0,8},{8,0},{1,9},{9,1},{2,10},{10,2},{3,11},{11,3},{4,12},{12,4},... | collective-permute-start | bytes 1572872 | tf_op jit(solution)/shard_map/ppermute | solution.py:34
  278.4 13.5 %collective-permute-start.39 = (bf16[512,512]{1,0:T(8,128)(2,1)S(1)}, bf16[512,512]{1,0:T(8,128)(2,1)S(1)}, u32[]{:S(2)}, u32[]{:S(2)}) collective-permute-start(bf16[512,512]{1,0:T(8,128)(2,1)S(1)} %shard_map.80.refs_0_), channel_id=1, source_target_pairs={{0,1},{1,0},{2,3},{3,2},{4,5},{5,4},{6,7},{7,6},{8,9},{9,8},{10,11... | collective-permute-start | bytes 1572872 | tf_op jit(solution)/shard_map/ppermute | solution.py:34
  278.4 13.5 %collective-permute-start.41 = (bf16[512,512]{1,0:T(8,128)(2,1)S(1)}, bf16[512,512]{1,0:T(8,128)(2,1)S(1)}, u32[]{:S(2)}, u32[]{:S(2)}) collective-permute-start(bf16[512,512]{1,0:T(8,128)(2,1)S(1)} %collective-permute-done.40.refs_2_), channel_id=1, source_target_pairs={{0,1},{1,0},{2,3},{3,2},{4,5},{5,4},{6,7},{7,6},{8,9},{9,8},{10,11... | collective-permute-start | bytes 1572872 | tf_op jit(solution)/shard_map/ppermute | solution.py:34
  279.0 13.0 %collective-permute-start.42 = (bf16[512,512]{1,0:T(8,128)(2,1)S(1)}, bf16[512,512]{1,0:T(8,128)(2,1)S(1)}, u32[]{:S(2)}, u32[]{:S(2)}) collective-permute-start(bf16[512,512]{1,0:T(8,128)(2,1)S(1)} %collective-permute-done.26.refs_4_), channel_id=1, source_target_pairs={{0,1},{1,0},{2,3},{3,2},{4,5},{5,4},{6,7},{7,6},{8,9},{9,8},{10,11... | collective-permute-start | bytes 1572872 | tf_op jit(solution)/shard_map/ppermute | solution.py:34
  287.8 7.3 %collective-permute-start.28 = (bf16[512,512]{1,0:T(8,128)(2,1)S(1)}, bf16[512,512]{1,0:T(8,128)(2,1)S(1)}, u32[]{:S(2)}, u32[]{:S(2)}) collective-permute-start(bf16[512,512]{1,0:T(8,128)(2,1)S(1)} %collective-permute-done.27.refs_2_), channel_id=1, source_target_pairs={{0,1},{1,0},{2,3},{3,2},{4,5},{5,4},{6,7},{7,6},{8,9},{9,8},{10,11... | collective-permute-start | bytes 1572872 | tf_op jit(solution)/shard_map/ppermute | solution.py:34
  287.8 7.3 %collective-permute-start.25 = (bf16[512,512]{1,0:T(8,128)(2,1)S(1)}, bf16[512,512]{1,0:T(8,128)(2,1)S(1)}, u32[]{:S(2)}, u32[]{:S(2)}) collective-permute-start(bf16[512,512]{1,0:T(8,128)(2,1)S(1)} %collective-permute-done.24.refs_0_), channel_id=1, source_target_pairs={{0,1},{1,0},{2,3},{3,2},{4,5},{5,4},{6,7},{7,6},{8,9},{9,8},{10,11... | collective-permute-start | bytes 1572872 | tf_op jit(solution)/shard_map/ppermute | solution.py:34
  297.3 17.2 %copy-start.1 = (bf16[128,4096]{1,0:T(8,128)(2,1)S(1)}, bf16[128,4096]{1,0:T(8,128)(2,1)}, u32[]{:S(2)}) copy-start(bf16[128,4096]{1,0:T(8,128)(2,1)} %tok_ref.1) | copy-start | bytes 3145732
